TPU v7x, 32 devices: a whole 2x2x4 slice. The times are simulated.
32 devices in a mesh: dp: 4 (over y, core), blk: 8 (over z, x).
Axes of the slice: x: 2, y: 2, z: 4, core: 2. Of those that a mesh axis runs over, the one named last changes fastest.
Arguments:
- tokens: bfloat16 [4, 3072, 1152], P('dp', 'blk'), may hold values from -6 to 6
- condition: bfloat16 [4, 12, 1152], P('dp'), may hold values from -6 to 6
- cotangent: bfloat16 [4, 3072, 1152], P('dp', 'blk'), may hold values from -6 to 6
- segments: int32 [4, 3072], P('dp', 'blk'), may hold values from 0 to 11, as said below
- kept_patch: int32 [4, 3072], P('dp', 'blk'), may hold values from 0 to 1023, as said below
- res_class: int32 [4, 12], P('dp'), may hold values from 0 to 1, as said below
- pack_order: int32 [4, 12], P('dp'), may hold values from 0 to 11, as said below
- ada_weight: bfloat16 [1152, 6912], P(('dp', 'blk')), may hold values from -0.1875 to 0.1875
- ada_bias: bfloat16 [6912], P(('dp', 'blk')), may hold values from -3 to 3
- qkv_weight: bfloat16 [1152, 3456], P(('dp', 'blk')), may hold values from -0.1875 to 0.1875
- query_bias: bfloat16 [1152], P(('dp', 'blk')), may hold values from -3 to 3
- value_bias: bfloat16 [1152], P(('dp', 'blk')), may hold values from -3 to 3
- proj_weight: bfloat16 [1152, 1152], P(('dp', 'blk')), may hold values from -0.875 to 0.875
- proj_bias: bfloat16 [1152], P(('dp', 'blk')), may hold values from -3 to 3
- hidden_weight: bfloat16 [1152, 4608], P(('dp', 'blk')), may hold values from -0.1875 to 0.1875
- hidden_bias: bfloat16 [4608], P(('dp', 'blk')), may hold values from -3 to 3
- output_weight: bfloat16 [4608, 1152], P(('dp', 'blk')), may hold values from -0.09375 to 0.09375
- output_bias: bfloat16 [1152], P(('dp', 'blk')), may hold values from -3 to 3
Outputs:
- block_out: bfloat16 [4, 3072, 1152], P('dp', 'blk')
- grad_tokens: float32 [4, 3072, 1152], P('dp', 'blk')
- grad_condition: float32 [4, 12, 1152], P('dp')
- grad_ada_weight: float32 [1152, 6912], P(('dp', 'blk'))
- grad_ada_bias: float32 [6912], P(('dp', 'blk'))
- grad_qkv_weight: float32 [1152, 3456], P(('dp', 'blk'))
- grad_query_bias: float32 [1152], P(('dp', 'blk'))
- grad_value_bias: float32 [1152], P(('dp', 'blk'))
- grad_proj_weight: float32 [1152, 1152], P(('dp', 'blk'))
- grad_proj_bias: float32 [1152], P(('dp', 'blk'))
- grad_hidden_weight: float32 [1152, 4608], P(('dp', 'blk'))
- grad_hidden_bias: float32 [4608], P(('dp', 'blk'))
- grad_output_weight: float32 [4608, 1152], P(('dp', 'blk'))
- grad_output_bias: float32 [1152], P(('dp', 'blk'))
Inputs may be any that keep to these rules, and one draw needn't show every extreme that they name: `segments`: in each row segment numbers never fall, run through 0 to 11, and segment s holds 512 consecutive tokens if res_class of image pack_order[row, s] is 1, else 128. `res_class`: each row has 4 images of class 1 and 8 of class 0. `pack_order`: each row is a permutation of the row's image numbers. `kept_patch`: within an image the indices are distinct and increasing and lie in its grid of side 32 or 16 by its class; an image keeps half its grid.
All inputs are finite; a program needn't handle non-finite values.
Results may differ from a plain program's by a relative error of at most 0.02.
Values may be sent and summed in bfloat16 or wider, within the bound.
No kernel may reach another device: no remote copies, remote signals or barrier semaphores. Data moves between devices by JAX's collectives and lax.ppermute only.
A program may use at most 256 MiB of HBM per device.

v0:
```python
from functools import partial

import jax
import jax.numpy as jnp
from jax import lax
from jax.sharding import PartitionSpec as P

HEADS = 16
BIG_SIDE = 32
SMALL_SIDE = 16


highest_mode = lax.Precision.HIGHEST


def shifted(shard, axis, by):
    count = lax.axis_size(axis)
    return lax.ppermute(shard, axis, [(i, (i + by) % count) for i in range(count)])


def over_rows(left, right):
    return lax.dot_general(
        left, right, (((0,), (0,)), ((), ())), preferred_element_type=jnp.float32
    )


def over_cols(left, right):
    return lax.dot_general(
        left, right, (((1,), (1,)), ((), ())), preferred_element_type=jnp.float32
    )


def halves(data):
    upper_part = data.astype(jnp.bfloat16)
    return (upper_part, (data - upper_part.astype(jnp.float32)).astype(jnp.bfloat16))


def place_code(retained_index, big_token, model_width):
    grid_side = jnp.where(big_token, BIG_SIDE, SMALL_SIDE).astype(jnp.int32)
    row_pos = retained_index // grid_side
    col_pos = retained_index - row_pos * grid_side
    quarter = model_width // 4
    frequency = 1.0 / 10000.0 ** (jnp.arange(quarter, dtype=jnp.float32) / quarter)
    across = col_pos.astype(jnp.float32)[:, None] * frequency[None, :]
    downward = row_pos.astype(jnp.float32)[:, None] * frequency[None, :]
    return jnp.concatenate(
        [jnp.sin(across), jnp.cos(across), jnp.sin(downward), jnp.cos(downward)], axis=1
    )


def layer_norm(values_in):
    centered = values_in - jnp.mean(values_in, axis=1, keepdims=True)
    spread = jnp.mean(centered * centered, axis=1, keepdims=True)
    inverse = lax.rsqrt(spread + 1e-06)
    return (centered * inverse, inverse)


def norm_back(grad_in, normed, inverse):
    mean_grad = jnp.mean(grad_in, axis=1, keepdims=True)
    mean_proj = jnp.mean(grad_in * normed, axis=1, keepdims=True)
    return inverse * (grad_in - mean_grad - normed * mean_proj)


def key_segments(row_seg, source, rows_per_device, size_blk):
    inside = (source >= 0) & (source < size_blk)
    start_row = jnp.clip(source, 0, size_blk - 1) * rows_per_device
    seg_piece = lax.dynamic_slice_in_dim(row_seg, start_row, rows_per_device)
    return jnp.where(inside, seg_piece, -1)


def attend(queries, query_seg, key_rows, value_rows, key_seg, state, score_scale):
    running_peak, running_total, accumulated = state
    raw_scores = (
        jnp.einsum("qhd,khd->hqk", queries, key_rows, preferred_element_type=jnp.float32)
        * score_scale
    )
    allowed = (query_seg[:, None] == key_seg[None, :])[None]
    masked = jnp.where(allowed, raw_scores, -1e30)
    new_peak = jnp.maximum(running_peak, jnp.max(masked, axis=2))
    weights = jnp.where(allowed, jnp.exp(masked - new_peak[:, :, None]), 0.0)
    factor = jnp.exp(running_peak - new_peak)
    running_total = running_total * factor + jnp.sum(weights, axis=2)
    contribution = jnp.einsum(
        "hqk,khd->qhd", weights.astype(jnp.bfloat16), value_rows, preferred_element_type=jnp.float32
    )
    accumulated = accumulated * factor.T[:, :, None] + contribution
    return (new_peak, running_total, accumulated)


def attend_back(
    queries, query_seg, grad_out, log_total, row_delta, key_rows, value_rows, key_seg, score_scale
):
    raw_scores = (
        jnp.einsum("qhd,khd->hqk", queries, key_rows, preferred_element_type=jnp.float32)
        * score_scale
    )
    allowed = (query_seg[:, None] == key_seg[None, :])[None]
    weights = jnp.where(allowed, jnp.exp(raw_scores - log_total[:, :, None]), 0.0)
    grad_values = jnp.einsum(
        "hqk,qhd->khd", weights.astype(jnp.bfloat16), grad_out, preferred_element_type=jnp.float32
    )
    grad_weights = jnp.einsum(
        "qhd,khd->hqk", grad_out, value_rows, preferred_element_type=jnp.float32
    )
    grad_scores = (weights * (grad_weights - row_delta[:, :, None])).astype(jnp.bfloat16)
    grad_queries = (
        jnp.einsum("hqk,khd->qhd", grad_scores, key_rows, preferred_element_type=jnp.float32)
        * score_scale
    )
    grad_keys = (
        jnp.einsum("hqk,qhd->khd", grad_scores, queries, preferred_element_type=jnp.float32)
        * score_scale
    )
    return (grad_queries, grad_keys, grad_values)


def pass_grads(grad_keys, grad_values):
    return (
        shifted(grad_keys.astype(jnp.bfloat16), "blk", 1).astype(grad_keys.dtype),
        shifted(grad_values.astype(jnp.bfloat16), "blk", 1).astype(grad_values.dtype),
    )


def per_device(
    tokens,
    condition,
    cotangent,
    segments,
    kept_patch,
    res_class,
    pack_order,
    ada_weight,
    ada_bias,
    qkv_weight,
    query_bias,
    value_bias,
    proj_weight,
    proj_bias,
    hidden_weight,
    hidden_bias,
    output_weight,
    output_bias,
):
    gathered = (
        lax.all_gather(ada_weight, ("dp", "blk"), axis=0, tiled=True),
        lax.all_gather(ada_bias, ("dp", "blk"), axis=0, tiled=True),
        lax.all_gather(qkv_weight, ("dp", "blk"), axis=0, tiled=True),
        lax.all_gather(query_bias, ("dp", "blk"), axis=0, tiled=True),
        lax.all_gather(value_bias, ("dp", "blk"), axis=0, tiled=True),
        lax.all_gather(proj_weight, ("dp", "blk"), axis=0, tiled=True),
        lax.all_gather(proj_bias, ("dp", "blk"), axis=0, tiled=True),
        lax.all_gather(hidden_weight, ("dp", "blk"), axis=0, tiled=True),
        lax.all_gather(hidden_bias, ("dp", "blk"), axis=0, tiled=True),
        lax.all_gather(output_weight, ("dp", "blk"), axis=0, tiled=True),
        lax.all_gather(output_bias, ("dp", "blk"), axis=0, tiled=True),
    )
    (
        full_ada,
        full_ada_bias,
        full_qkv,
        full_query_bias,
        full_value_bias,
        whole_projection,
        full_proj_bias,
        full_hidden,
        full_hidden_bias,
        full_output,
        full_output_bias,
    ) = gathered
    rows_per_device = tokens.shape[1]
    model_width = tokens.shape[2]
    head_size = model_width // HEADS
    score_scale = head_size ** (-0.5)
    count_segs = condition.shape[1]
    own_index = lax.axis_index("blk")
    size_blk = lax.axis_size("blk")
    token_seg = segments[0]
    row_seg = lax.all_gather(token_seg, "blk", axis=0, tiled=True)
    image_ids = jnp.arange(count_segs, dtype=jnp.int32)
    pick_image = pack_order[0][:, None] == image_ids[None, :]
    seg_cond = jnp.dot(
        pick_image.astype(jnp.bfloat16), condition[0], preferred_element_type=jnp.float32
    )
    seg_big = jnp.sum(jnp.where(pick_image, res_class[0][None, :], 0), axis=1)
    silu_cond, silu_pull = jax.vjp(jax.nn.silu, seg_cond)
    silu_low = silu_cond.astype(jnp.bfloat16)
    modulation = jnp.dot(
        silu_low, full_ada, preferred_element_type=jnp.float32
    ) + full_ada_bias.astype(jnp.float32)
    pick_token = token_seg[:, None] == image_ids[None, :]
    pick_float = pick_token.astype(jnp.float32)
    per_token = jnp.dot(pick_float, modulation, precision=highest_mode)
    token_big = jnp.sum(jnp.where(pick_token, seg_big[None, :], 0), axis=1)
    shift_attn, scale_attn, gate_attn, shift_mlp, scale_mlp, gate_mlp = jnp.split(
        per_token, 6, axis=1
    )
    hidden = tokens[0].astype(jnp.float32) + place_code(kept_patch[0], token_big == 1, model_width)
    first_norm, first_inverse = layer_norm(hidden)
    attn_in = (first_norm * (1.0 + scale_attn) + shift_attn).astype(jnp.bfloat16)
    projected = jnp.dot(attn_in, full_qkv, preferred_element_type=jnp.float32)
    shape_heads = (rows_per_device, HEADS, head_size)
    queries = (
        (projected[:, :model_width] + full_query_bias.astype(jnp.float32))
        .astype(jnp.bfloat16)
        .reshape(shape_heads)
    )
    key_rows = projected[:, model_width : 2 * model_width].astype(jnp.bfloat16).reshape(shape_heads)
    value_rows = (
        (projected[:, 2 * model_width :] + full_value_bias.astype(jnp.float32))
        .astype(jnp.bfloat16)
        .reshape(shape_heads)
    )
    start_state = (
        jnp.full((HEADS, rows_per_device), -1e30, jnp.float32),
        jnp.zeros((HEADS, rows_per_device), jnp.float32),
        jnp.zeros(shape_heads, jnp.float32),
    )
    state = attend(queries, token_seg, key_rows, value_rows, token_seg, start_state, score_scale)

    def forward_hop(hop_index, carry):
        key_now, value_now, inner_state = carry
        key_now, value_now = shifted((key_now, value_now), "blk", 1)
        source = (own_index - hop_index) % size_blk
        inner_state = attend(
            queries,
            token_seg,
            key_now,
            value_now,
            key_segments(row_seg, source, rows_per_device, size_blk),
            inner_state,
            score_scale,
        )
        return (key_now, value_now, inner_state)

    last_keys, last_values, state = lax.fori_loop(
        1, size_blk, forward_hop, (key_rows, value_rows, state)
    )
    final_peak, final_total, accumulated = state
    attn_heads = accumulated / final_total.T[:, :, None]
    log_total = final_peak + jnp.log(final_total)
    attn_low = attn_heads.reshape(rows_per_device, model_width).astype(jnp.bfloat16)
    branch = jnp.dot(
        attn_low, whole_projection, preferred_element_type=jnp.float32
    ) + full_proj_bias.astype(jnp.float32)
    after_attn = hidden + gate_attn * branch
    second_norm, second_inverse = layer_norm(after_attn)
    mlp_in = (second_norm * (1.0 + scale_mlp) + shift_mlp).astype(jnp.bfloat16)
    upper_pre = jnp.dot(
        mlp_in, full_hidden, preferred_element_type=jnp.float32
    ) + full_hidden_bias.astype(jnp.float32)
    activated, gelu_pull = jax.vjp(partial(jax.nn.gelu, approximate=True), upper_pre)
    act_low = activated.astype(jnp.bfloat16)
    lower_out = jnp.dot(
        act_low, full_output, preferred_element_type=jnp.float32
    ) + full_output_bias.astype(jnp.float32)
    block_out = (after_attn + gate_mlp * lower_out).astype(jnp.bfloat16)
    grad_result = cotangent[0].astype(jnp.float32)
    grad_gate_mlp = grad_result * lower_out
    grad_lower = (grad_result * gate_mlp).astype(jnp.bfloat16)
    grad_output_weight = over_rows(act_low, grad_lower)
    grad_output_bias = jnp.sum(grad_lower.astype(jnp.float32), axis=0)
    grad_act = over_cols(grad_lower, full_output)
    grad_upper = gelu_pull(grad_act)[0].astype(jnp.bfloat16)
    grad_hidden_weight = over_rows(mlp_in, grad_upper)
    grad_hidden_bias = jnp.sum(grad_upper.astype(jnp.float32), axis=0)
    grad_mlp_in = over_cols(grad_upper, full_hidden)
    grad_scale_mlp = grad_mlp_in * second_norm
    grad_after = grad_result + norm_back(
        grad_mlp_in * (1.0 + scale_mlp), second_norm, second_inverse
    )
    grad_gate_attn = grad_after * branch
    grad_branch = (grad_after * gate_attn).astype(jnp.bfloat16)
    grad_proj_weight = over_rows(attn_low, grad_branch)
    grad_proj_bias = jnp.sum(grad_branch.astype(jnp.float32), axis=0)
    grad_attn = over_cols(grad_branch, whole_projection).astype(jnp.bfloat16).reshape(shape_heads)
    row_delta = jnp.sum(grad_attn.astype(jnp.float32) * attn_heads, axis=2).T

    def back_hop(hop_index, carry):
        key_now, value_now, grad_keys, grad_values, grad_queries = carry
        source = (own_index - hop_index) % size_blk
        part_queries, part_keys, part_values = attend_back(
            queries,
            token_seg,
            grad_attn,
            log_total,
            row_delta,
            key_now,
            value_now,
            key_segments(row_seg, source, rows_per_device, size_blk),
            score_scale,
        )
        key_now, value_now = shifted((key_now, value_now), "blk", 1)
        grad_keys, grad_values = pass_grads(grad_keys + part_keys, grad_values + part_values)
        return (key_now, value_now, grad_keys, grad_values, grad_queries + part_queries)

    zero_heads = jnp.zeros(shape_heads, jnp.float32)
    key_now, value_now, grad_keys, grad_values, grad_queries = lax.fori_loop(
        0, size_blk - 1, back_hop, (key_rows, value_rows, zero_heads, zero_heads, zero_heads)
    )
    source = (own_index + 1) % size_blk
    part_queries, part_keys, part_values = attend_back(
        queries,
        token_seg,
        grad_attn,
        log_total,
        row_delta,
        key_now,
        value_now,
        key_segments(row_seg, source, rows_per_device, size_blk),
        score_scale,
    )
    grad_queries = grad_queries + part_queries
    grad_keys, grad_values = pass_grads(grad_keys + part_keys, grad_values + part_values)
    grad_qkv = jnp.concatenate(
        [
            grad_queries.reshape(rows_per_device, model_width),
            grad_keys.reshape(rows_per_device, model_width),
            grad_values.reshape(rows_per_device, model_width),
        ],
        axis=1,
    ).astype(jnp.bfloat16)
    grad_qkv_weight = over_rows(attn_in, grad_qkv)
    grad_qkv_sum = jnp.sum(grad_qkv.astype(jnp.float32), axis=0)
    grad_query_bias = grad_qkv_sum[:model_width]
    grad_value_bias = grad_qkv_sum[2 * model_width :]
    grad_attn_in = over_cols(grad_qkv, full_qkv)
    grad_scale_attn = grad_attn_in * first_norm
    grad_tokens = grad_after + norm_back(
        grad_attn_in * (1.0 + scale_attn), first_norm, first_inverse
    )
    grad_per_token = jnp.concatenate(
        [grad_attn_in, grad_scale_attn, grad_gate_attn, grad_mlp_in, grad_scale_mlp, grad_gate_mlp],
        axis=1,
    )
    grad_modulation = lax.dot_general(
        pick_float, grad_per_token, (((0,), (0,)), ((), ())), precision=highest_mode
    )
    mod_upper, mod_rest = halves(grad_modulation)
    grad_ada_weight = over_rows(silu_low, mod_upper) + over_rows(silu_low, mod_rest)
    grad_ada_bias = jnp.sum(grad_modulation, axis=0)
    total_mod = lax.psum(grad_modulation.astype(jnp.bfloat16), "blk").astype(jnp.float32)
    total_upper, total_rest = halves(total_mod)
    grad_silu = over_cols(total_upper, full_ada) + over_cols(total_rest, full_ada)
    grad_seg_cond = silu_pull(grad_silu)[0]
    grad_image = lax.dot_general(
        pick_image.astype(jnp.float32),
        grad_seg_cond,
        (((0,), (0,)), ((), ())),
        precision=highest_mode,
    )
    row_share = (
        lax.psum_scatter(
            grad_ada_weight.astype(jnp.bfloat16), "dp", scatter_dimension=0, tiled=True
        ).astype(jnp.float32),
        lax.psum_scatter(
            grad_ada_bias.astype(jnp.bfloat16), "dp", scatter_dimension=0, tiled=True
        ).astype(jnp.float32),
        lax.psum_scatter(
            grad_qkv_weight.astype(jnp.bfloat16), "dp", scatter_dimension=0, tiled=True
        ).astype(jnp.float32),
        lax.psum_scatter(
            grad_query_bias.astype(jnp.bfloat16), "dp", scatter_dimension=0, tiled=True
        ).astype(jnp.float32),
        lax.psum_scatter(
            grad_value_bias.astype(jnp.bfloat16), "dp", scatter_dimension=0, tiled=True
        ).astype(jnp.float32),
        lax.psum_scatter(
            grad_proj_weight.astype(jnp.bfloat16), "dp", scatter_dimension=0, tiled=True
        ).astype(jnp.float32),
        lax.psum_scatter(
            grad_proj_bias.astype(jnp.bfloat16), "dp", scatter_dimension=0, tiled=True
        ).astype(jnp.float32),
        lax.psum_scatter(
            grad_hidden_weight.astype(jnp.bfloat16), "dp", scatter_dimension=0, tiled=True
        ).astype(jnp.float32),
        lax.psum_scatter(
            grad_hidden_bias.astype(jnp.bfloat16), "dp", scatter_dimension=0, tiled=True
        ).astype(jnp.float32),
        lax.psum_scatter(
            grad_output_weight.astype(jnp.bfloat16), "dp", scatter_dimension=0, tiled=True
        ).astype(jnp.float32),
        lax.psum_scatter(
            grad_output_bias.astype(jnp.bfloat16), "dp", scatter_dimension=0, tiled=True
        ).astype(jnp.float32),
    )
    summed = (
        lax.psum_scatter(
            row_share[0].astype(jnp.bfloat16), "blk", scatter_dimension=0, tiled=True
        ).astype(jnp.float32),
        lax.psum_scatter(
            row_share[1].astype(jnp.bfloat16), "blk", scatter_dimension=0, tiled=True
        ).astype(jnp.float32),
        lax.psum_scatter(
            row_share[2].astype(jnp.bfloat16), "blk", scatter_dimension=0, tiled=True
        ).astype(jnp.float32),
        lax.psum_scatter(
            row_share[3].astype(jnp.bfloat16), "blk", scatter_dimension=0, tiled=True
        ).astype(jnp.float32),
        lax.psum_scatter(
            row_share[4].astype(jnp.bfloat16), "blk", scatter_dimension=0, tiled=True
        ).astype(jnp.float32),
        lax.psum_scatter(
            row_share[5].astype(jnp.bfloat16), "blk", scatter_dimension=0, tiled=True
        ).astype(jnp.float32),
        lax.psum_scatter(
            row_share[6].astype(jnp.bfloat16), "blk", scatter_dimension=0, tiled=True
        ).astype(jnp.float32),
        lax.psum_scatter(
            row_share[7].astype(jnp.bfloat16), "blk", scatter_dimension=0, tiled=True
        ).astype(jnp.float32),
        lax.psum_scatter(
            row_share[8].astype(jnp.bfloat16), "blk", scatter_dimension=0, tiled=True
        ).astype(jnp.float32),
        lax.psum_scatter(
            row_share[9].astype(jnp.bfloat16), "blk", scatter_dimension=0, tiled=True
        ).astype(jnp.float32),
        lax.psum_scatter(
            row_share[10].astype(jnp.bfloat16), "blk", scatter_dimension=0, tiled=True
        ).astype(jnp.float32),
    )
    return (
        block_out[None],
        grad_tokens[None],
        grad_image[None],
        summed[0],
        summed[1],
        summed[2],
        summed[3],
        summed[4],
        summed[5],
        summed[6],
        summed[7],
        summed[8],
        summed[9],
        summed[10],
    )


def solution(mesh):
    placed = (
        P("dp", "blk", None),
        P("dp", None, None),
        P("dp", "blk", None),
        P("dp", "blk"),
        P("dp", "blk"),
        P("dp", None),
        P("dp", None),
        P(("dp", "blk"), None),
        P(("dp", "blk")),
        P(("dp", "blk"), None),
        P(("dp", "blk")),
        P(("dp", "blk")),
        P(("dp", "blk"), None),
        P(("dp", "blk")),
        P(("dp", "blk"), None),
        P(("dp", "blk")),
        P(("dp", "blk"), None),
        P(("dp", "blk")),
    )
    return jax.shard_map(
        per_device,
        mesh=mesh,
        in_specs=placed,
        out_specs=(
            P("dp", "blk", None),
            P("dp", "blk", None),
            P("dp", None, None),
            P(("dp", "blk"), None),
            P(("dp", "blk")),
            P(("dp", "blk"), None),
            P(("dp", "blk")),
            P(("dp", "blk")),
            P(("dp", "blk"), None),
            P(("dp", "blk")),
            P(("dp", "blk"), None),
            P(("dp", "blk")),
            P(("dp", "blk"), None),
            P(("dp", "blk")),
        ),
        check_vma=False,
    )
```

profile of v0, /device:TPU:0, one launch (start us, length us, event | category | flops | bytes accessed | tf_op | source)
XLA Modules:
  0.0 2231.3 jit_solution(2861152832170241787)
XLA Ops:
  11.4 27.8 %all-gather = s32[1,3072]{1,0:T(1,128)S(1)} all-gather(s32[1,384]{1,0:T(1,128)} %param.25), channel_id=2, replica_groups=mesh['dp'=4,'blk'=8] {'blk'}, dimensions={1}, use_global_device_ids=true | all-gather | bytes 13824 | tf_op jit(solution)/shard_map/all_gather | solution.py:178
  50.8 40.0 %all-reduce.26 = (bf16[6912]{0:T(1024)(128)(2,1)S(1)}, bf16[1152]{0:T(1024)(128)(2,1)S(1)}, bf16[1152]{0:T(1024)(128)(2,1)S(1)}, bf16[1152]{0:T(1024)(128)(2,1)S...) all-reduce(bf16[6912]{0:T(1024)(128)(2,1)S(1)} %dynamic-update-slic, ...), channel_id=1, replica_groups=mesh['dp'=4,'blk'=8] {'dp','blk'}, use_global_device_ids=true, to_apply=%add | all-reduce | flops 16128 | bytes 64512
  97.8 56.4 %all-gather.15.cloned.1.call-done = bf16[32,36,3456]{2,1,0:T(8,128)(2,1)} async-done(((bf16[1,36,3456]{2,1,0:T(8,128)(2,1)}), bf16[32,36,3456]{2,1,0:T(8,128)(2,1)}) %all-gather.15.cloned.1.call-update) | async-done | bytes 7962640 | tf_op jit(solution)/shard_map/all_gather | solution.py:147
  154.1 12.5 reshape.317
  166.6 81.4 %all-gather.19.cloned.1.call-done = bf16[32,36,4608]{2,1,0:T(8,128)(2,1)} async-done(((bf16[1,36,4608]{2,1,0:T(8,128)(2,1)}), bf16[32,36,4608]{2,1,0:T(8,128)(2,1)}) %all-gather.19.cloned.1.call-update) | async-done | bytes 10616848 | tf_op jit(solution)/shard_map/all_gather | solution.py:152
  248.0 14.1 reshape.321
  262.2 106.4 %all-gather.13.cloned.1.call-done = bf16[32,36,6912]{2,1,0:T(8,128)(2,1)} async-done(((bf16[1,36,6912]{2,1,0:T(8,128)(2,1)}), bf16[32,36,6912]{2,1,0:T(8,128)(2,1)}) %all-gather.13.cloned.1.call-update) | async-done | bytes 15925264 | tf_op jit(solution)/shard_map/all_gather | solution.py:145
  368.5 18.4 reshape.315
  432.4 343.0 %while.47 = (s32[]{:T(128)}, bf16[384,16,72]{0,2,1:T(8,128)(2,1)}, bf16[384,16,72]{0,2,1:T(8,128)(2,1)}, f32[16,384]{1,0:T(8,128)S(1)}, f32[16,384]{1,0:T(8,128)...) while((s32[]{:T(128)}, bf16[384,16,72]{0,2,1:T(8,128)(2,1)}, ...), condition=%wide.region_9.10_spmd, body=%wide.region_6.9_spmd.sunk | while | flops 711199104 | bytes 60270072 | solution.py:235
  434.3 39.0 %collective-permute-done = bf16[384,16,72]{0,2,1:T(8,128)(2,1)S(1)} collective-permute-done((bf16[384,16,72]{0,2,1:T(8,128)(2,1)}, bf16[384,16,72]{0,2,1:T(8,128)(2,1)S(1)}, u32[]{:S(2)}, u32[]{:S(2)}) %collective-permute-start) | collective-permute-done | bytes 884768 | tf_op jit(solution)/shard_map/while/body/eval_jaxpr/ppermute | solution.py:18
  478.4 13.7 collective-permute-done.1
  497.8 25.1 %collective-permute-done = bf16[384,16,72]{0,2,1:T(8,128)(2,1)S(1)} collective-permute-done((bf16[384,16,72]{0,2,1:T(8,128)(2,1)}, bf16[384,16,72]{0,2,1:T(8,128)(2,1)S(1)}, u32[]{:S(2)}, u32[]{:S(2)}) %collective-permute-start) | collective-permute-done | bytes 884768 | tf_op jit(solution)/shard_map/while/body/eval_jaxpr/ppermute | solution.py:18
  527.9 12.8 collective-permute-done.1
  546.2 25.2 %collective-permute-done = bf16[384,16,72]{0,2,1:T(8,128)(2,1)S(1)} collective-permute-done((bf16[384,16,72]{0,2,1:T(8,128)(2,1)}, bf16[384,16,72]{0,2,1:T(8,128)(2,1)S(1)}, u32[]{:S(2)}, u32[]{:S(2)}) %collective-permute-start) | collective-permute-done | bytes 884768 | tf_op jit(solution)/shard_map/while/body/eval_jaxpr/ppermute | solution.py:18
  576.5 11.9 collective-permute-done.1
  593.9 25.2 %collective-permute-done = bf16[384,16,72]{0,2,1:T(8,128)(2,1)S(1)} collective-permute-done((bf16[384,16,72]{0,2,1:T(8,128)(2,1)}, bf16[384,16,72]{0,2,1:T(8,128)(2,1)S(1)}, u32[]{:S(2)}, u32[]{:S(2)}) %collective-permute-start) | collective-permute-done | bytes 884768 | tf_op jit(solution)/shard_map/while/body/eval_jaxpr/ppermute | solution.py:18
  624.2 10.9 collective-permute-done.1
  640.7 25.2 %collective-permute-done = bf16[384,16,72]{0,2,1:T(8,128)(2,1)S(1)} collective-permute-done((bf16[384,16,72]{0,2,1:T(8,128)(2,1)}, bf16[384,16,72]{0,2,1:T(8,128)(2,1)S(1)}, u32[]{:S(2)}, u32[]{:S(2)}) %collective-permute-start) | collective-permute-done | bytes 884768 | tf_op jit(solution)/shard_map/while/body/eval_jaxpr/ppermute | solution.py:18
  671.0 10.0 collective-permute-done.1
  686.6 25.2 %collective-permute-done = bf16[384,16,72]{0,2,1:T(8,128)(2,1)S(1)} collective-permute-done((bf16[384,16,72]{0,2,1:T(8,128)(2,1)}, bf16[384,16,72]{0,2,1:T(8,128)(2,1)S(1)}, u32[]{:S(2)}, u32[]{:S(2)}) %collective-permute-start) | collective-permute-done | bytes 884768 | tf_op jit(solution)/shard_map/while/body/eval_jaxpr/ppermute | solution.py:18
  731.5 25.2 %collective-permute-done = bf16[384,16,72]{0,2,1:T(8,128)(2,1)S(1)} collective-permute-done((bf16[384,16,72]{0,2,1:T(8,128)(2,1)}, bf16[384,16,72]{0,2,1:T(8,128)(2,1)S(1)}, u32[]{:S(2)}, u32[]{:S(2)}) %collective-permute-start) | collective-permute-done | bytes 884768 | tf_op jit(solution)/shard_map/while/body/eval_jaxpr/ppermute | solution.py:18
  790.3 12.1 fusion.107
  802.4 15.0 fusion.97
  823.5 11.4 convolution_convert_fusion
  834.8 10.8 convolution_add_fusion.3
  863.3 607.0 %while.48 = (s32[]{:T(128)}, bf16[384,16,72]{0,2,1:T(8,128)(2,1)S(1)}, bf16[384,16,72]{0,2,1:T(8,128)(2,1)}, f32[384,16,72]{0,2,1:T(8,128)}, f32[384,16,72]{0,2,...) while((s32[]{:T(128)}, ...), condition=%wide.region_16.17_spmd.clone, body=%wide.region_15.16_spmd.clone.sunk | while | flops 1727742336 | bytes 110528120 | solution.py:297
  886.7 16.7 collective-permute-done.4
  905.9 16.4 collective-permute-done.5
  924.9 16.3 collective-permute-done.2
  941.2 12.5 collective-permute-done.3
  977.8 14.9 collective-permute-done.4
  995.2 16.5 collective-permute-done.5
  1014.2 16.3 collective-permute-done.2
  1030.5 11.5 collective-permute-done.3
  1066.2 14.9 collective-permute-done.4
  1083.6 16.5 collective-permute-done.5
  1102.6 16.3 collective-permute-done.2
  1118.9 10.6 collective-permute-done.3
  1153.6 14.9 collective-permute-done.4
  1171.1 16.5 collective-permute-done.5
  1190.1 16.3 collective-permute-done.2
  1206.4 9.7 collective-permute-done.3
  1240.2 14.9 collective-permute-done.4
  1257.6 16.5 collective-permute-done.5
  1276.6 15.5 collective-permute-done.2
  1292.1 9.6 collective-permute-done.3
  1325.8 14.9 collective-permute-done.4
  1343.3 16.5 collective-permute-done.5
  1362.3 14.5 collective-permute-done.2
  1410.4 14.9 collective-permute-done.4
  1427.9 16.5 collective-permute-done.5
  1446.9 13.4 collective-permute-done.2
  1483.0 16.9 collective-permute-done.6
  1529.8 12.8 fusion.89
  1542.6 18.2 add_convert_fusion
  1576.3 10.0 convolution_convert_fusion.1
  1594.8 10.5 all-reduce.28
  1605.8 33.0 %all-reduce.27 = (bf16[1728]{0:T(1024)(128)(2,1)S(1)}, bf16[288]{0:T(512)(128)(2,1)S(1)}, bf16[288]{0:T(512)(128)(2,1)S(1)}, bf16[288]{0:T(512)(128)(2,1)S(1)}, ...) all-reduce(bf16[1728]{0:T(1024)(128)(2,1)S(1)} %dynamic-slice.4, ...), channel_id=6, replica_groups=mesh['dp'=4,'blk'=8] {'blk'}, use_global_device_ids=true, to_apply=%region_24.25.clone | all-reduce | flops 4032 | bytes 16128
  1642.4 10.7 fusion.110
  1653.1 9.8 convolution_add_fusion.4
  1670.7 71.8 %reduce-scatter.17.cloned.1.call-done = bf16[288,3456]{1,0:T(8,128)(2,1)} async-done(((bf16[1152,3456]{1,0:T(8,128)(2,1)}), bf16[288,3456]{1,0:T(8,128)(2,1)}) %reduce-scatter.17.cloned.1.call-update) | async-done | bytes 1990672 | tf_op jit(solution)/shard_map/reduce_scatter | solution.py:358
  1742.4 88.6 %reduce-scatter.21.cloned.1.call-done = bf16[288,4608]{1,0:T(8,128)(2,1)} async-done(((bf16[1152,4608]{1,0:T(8,128)(2,1)}), bf16[288,4608]{1,0:T(8,128)(2,1)}) %reduce-scatter.21.cloned.1.call-update) | async-done | bytes 2654224 | tf_op jit(solution)/shard_map/reduce_scatter | solution.py:373
  1831.1 123.7 %reduce-scatter.15.cloned.1.call-done = bf16[288,6912]{1,0:T(8,128)(2,1)} async-done(((bf16[1152,6912]{1,0:T(8,128)(2,1)}), bf16[288,6912]{1,0:T(8,128)(2,1)}) %reduce-scatter.15.cloned.1.call-update) | async-done | bytes 3981328 | tf_op jit(solution)/shard_map/reduce_scatter | solution.py:352
  1954.7 234.4 %fusion.94 = (bf16[40,6912]{1,0:T(8,128)(2,1)S(1)}, bf16[48,3456]{1,0:T(8,128)(2,1)S(1)}, bf16[48,1152]{1,0:T(8,128)(2,1)S(1)}, bf16[40,4608]{1,0:T(8,128)(2,1)S(1)}) fusion(bf16[288,6912]{1,0:T(8,128)(2,1)} %reduce-scatter.15.cloned.1.call-done, bf16[288,3456]{1,0:T(8,128)(2,1)} %reduce-scatter.17.cloned.1.call-done, ...), kind=kCustom, calls=%all-reduce-scatter.4 | all-reduce-scatter fusion | flops 5455874 | bytes 10654208
  (577 shorter events, 528.1 us)
Async XLA Ops:
  7.2 85.4 %all-gather.17.cloned.1.call-start = ((), (), s32[]{:S(2)}) async-start(), calls=%async_computation.16 | async-start | bytes 3041280 | tf_op jit(solution)/shard_map/all_gather | solution.py:150
  7.9 146.2 %all-gather.15.cloned.1.call-start = ((), (), s32[]{:S(2)}) async-start(), calls=%async_computation.15 | async-start | bytes 9123840 | tf_op jit(solution)/shard_map/all_gather | solution.py:147
  8.7 239.4 %all-gather.19.cloned.1.call-start = ((), (), s32[]{:S(2)}) async-start(), calls=%async_computation.17 | async-start | bytes 12165120 | tf_op jit(solution)/shard_map/all_gather | solution.py:152
  9.4 359.1 %all-gather.13.cloned.1.call-start = ((), (), s32[]{:S(2)}) async-start(), calls=%async_computation.14 | async-start | bytes 18247680 | tf_op jit(solution)/shard_map/all_gather | solution.py:145
  10.0 780.3 %all-gather.11.cloned.1.call-start = ((), (), s32[]{:S(2)}) async-start(), calls=%async_computation.6 | async-start | bytes 10948608 | tf_op jit(solution)/shard_map/all_gather | solution.py:154
  10.6 1576.9 %reduce-scatter.23.cloned.1.call-start = ((), (), s32[]{:S(2)}) async-start(), calls=%async_computation.12 | async-start | bytes 13271040 | tf_op jit(solution)/shard_map/reduce_scatter | solution.py:379
  11.4 383.3 %copy-start.49 = (s32[384]{0:T(512)}, s32[384]{0:T(512)S(1)}, u32[]{:S(2)}) copy-start(s32[384]{0:T(512)S(1)} %reduce.7) | copy-start | bytes 4612
  432.4 40.9 %collective-permute-start = (bf16[384,16,72]{0,2,1:T(8,128)(2,1)}, bf16[384,16,72]{0,2,1:T(8,128)(2,1)S(1)}, u32[]{:S(2)}, u32[]{:S(2)}) collective-permute-start(bf16[384,16,72]{0,2,1:T(8,128)(2,1)} %get-tuple-element.989), channel_id=1, source_target_pairs={{0,1},{1,2},{2,3},{3,4},{4,5},{5,6},{6,7},{7,0},{8,9},{9,10},{10,1... | collective-permute-start | bytes 2654216 | tf_op jit(solution)/shard_map/while/body/eval_jaxpr/ppermute | solution.py:18
  433.8 58.4 %collective-permute-start.1 = (bf16[384,16,72]{0,2,1:T(8,128)(2,1)}, bf16[384,16,72]{0,2,1:T(8,128)(2,1)S(1)}, u32[]{:S(2)}, u32[]{:S(2)}) collective-permute-start(bf16[384,16,72]{0,2,1:T(8,128)(2,1)} %get-tuple-element.990), channel_id=1, source_target_pairs={{0,1},{1,2},{2,3},{3,4},{4,5},{5,6},{6,7},{7,0},{8,9},{9,10},{10,1... | collective-permute-start | bytes 2654216 | tf_op jit(solution)/shard_map/while/body/eval_jaxpr/ppermute | solution.py:18
  497.4 25.4 %collective-permute-start = (bf16[384,16,72]{0,2,1:T(8,128)(2,1)}, bf16[384,16,72]{0,2,1:T(8,128)(2,1)S(1)}, u32[]{:S(2)}, u32[]{:S(2)}) collective-permute-start(bf16[384,16,72]{0,2,1:T(8,128)(2,1)} %get-tuple-element.989), channel_id=1, source_target_pairs={{0,1},{1,2},{2,3},{3,4},{4,5},{5,6},{6,7},{7,0},{8,9},{9,10},{10,1... | collective-permute-start | bytes 2654216 | tf_op jit(solution)/shard_map/while/body/eval_jaxpr/ppermute | solution.py:18
  497.4 43.3 %collective-permute-start.1 = (bf16[384,16,72]{0,2,1:T(8,128)(2,1)}, bf16[384,16,72]{0,2,1:T(8,128)(2,1)S(1)}, u32[]{:S(2)}, u32[]{:S(2)}) collective-permute-start(bf16[384,16,72]{0,2,1:T(8,128)(2,1)} %get-tuple-element.990), channel_id=1, source_target_pairs={{0,1},{1,2},{2,3},{3,4},{4,5},{5,6},{6,7},{7,0},{8,9},{9,10},{10,1... | collective-permute-start | bytes 2654216 | tf_op jit(solution)/shard_map/while/body/eval_jaxpr/ppermute | solution.py:18
  546.0 25.5 %collective-permute-start = (bf16[384,16,72]{0,2,1:T(8,128)(2,1)}, bf16[384,16,72]{0,2,1:T(8,128)(2,1)S(1)}, u32[]{:S(2)}, u32[]{:S(2)}) collective-permute-start(bf16[384,16,72]{0,2,1:T(8,128)(2,1)} %get-tuple-element.989), channel_id=1, source_target_pairs={{0,1},{1,2},{2,3},{3,4},{4,5},{5,6},{6,7},{7,0},{8,9},{9,10},{10,1... | collective-permute-start | bytes 2654216 | tf_op jit(solution)/shard_map/while/body/eval_jaxpr/ppermute | solution.py:18
  546.0 42.4 %collective-permute-start.1 = (bf16[384,16,72]{0,2,1:T(8,128)(2,1)}, bf16[384,16,72]{0,2,1:T(8,128)(2,1)S(1)}, u32[]{:S(2)}, u32[]{:S(2)}) collective-permute-start(bf16[384,16,72]{0,2,1:T(8,128)(2,1)} %get-tuple-element.990), channel_id=1, source_target_pairs={{0,1},{1,2},{2,3},{3,4},{4,5},{5,6},{6,7},{7,0},{8,9},{9,10},{10,1... | collective-permute-start | bytes 2654216 | tf_op jit(solution)/shard_map/while/body/eval_jaxpr/ppermute | solution.py:18
  593.7 25.5 %collective-permute-start = (bf16[384,16,72]{0,2,1:T(8,128)(2,1)}, bf16[384,16,72]{0,2,1:T(8,128)(2,1)S(1)}, u32[]{:S(2)}, u32[]{:S(2)}) collective-permute-start(bf16[384,16,72]{0,2,1:T(8,128)(2,1)} %get-tuple-element.989), channel_id=1, source_target_pairs={{0,1},{1,2},{2,3},{3,4},{4,5},{5,6},{6,7},{7,0},{8,9},{9,10},{10,1... | collective-permute-start | bytes 2654216 | tf_op jit(solution)/shard_map/while/body/eval_jaxpr/ppermute | solution.py:18
  593.7 41.5 %collective-permute-start.1 = (bf16[384,16,72]{0,2,1:T(8,128)(2,1)}, bf16[384,16,72]{0,2,1:T(8,128)(2,1)S(1)}, u32[]{:S(2)}, u32[]{:S(2)}) collective-permute-start(bf16[384,16,72]{0,2,1:T(8,128)(2,1)} %get-tuple-element.990), channel_id=1, source_target_pairs={{0,1},{1,2},{2,3},{3,4},{4,5},{5,6},{6,7},{7,0},{8,9},{9,10},{10,1... | collective-permute-start | bytes 2654216 | tf_op jit(solution)/shard_map/while/body/eval_jaxpr/ppermute | solution.py:18
  640.4 25.5 %collective-permute-start = (bf16[384,16,72]{0,2,1:T(8,128)(2,1)}, bf16[384,16,72]{0,2,1:T(8,128)(2,1)S(1)}, u32[]{:S(2)}, u32[]{:S(2)}) collective-permute-start(bf16[384,16,72]{0,2,1:T(8,128)(2,1)} %get-tuple-element.989), channel_id=1, source_target_pairs={{0,1},{1,2},{2,3},{3,4},{4,5},{5,6},{6,7},{7,0},{8,9},{9,10},{10,1... | collective-permute-start | bytes 2654216 | tf_op jit(solution)/shard_map/while/body/eval_jaxpr/ppermute | solution.py:18
  640.5 40.6 %collective-permute-start.1 = (bf16[384,16,72]{0,2,1:T(8,128)(2,1)}, bf16[384,16,72]{0,2,1:T(8,128)(2,1)S(1)}, u32[]{:S(2)}, u32[]{:S(2)}) collective-permute-start(bf16[384,16,72]{0,2,1:T(8,128)(2,1)} %get-tuple-element.990), channel_id=1, source_target_pairs={{0,1},{1,2},{2,3},{3,4},{4,5},{5,6},{6,7},{7,0},{8,9},{9,10},{10,1... | collective-permute-start | bytes 2654216 | tf_op jit(solution)/shard_map/while/body/eval_jaxpr/ppermute | solution.py:18
  686.3 25.5 %collective-permute-start = (bf16[384,16,72]{0,2,1:T(8,128)(2,1)}, bf16[384,16,72]{0,2,1:T(8,128)(2,1)S(1)}, u32[]{:S(2)}, u32[]{:S(2)}) collective-permute-start(bf16[384,16,72]{0,2,1:T(8,128)(2,1)} %get-tuple-element.989), channel_id=1, source_target_pairs={{0,1},{1,2},{2,3},{3,4},{4,5},{5,6},{6,7},{7,0},{8,9},{9,10},{10,1... | collective-permute-start | bytes 2654216 | tf_op jit(solution)/shard_map/while/body/eval_jaxpr/ppermute | solution.py:18
  686.3 39.7 %collective-permute-start.1 = (bf16[384,16,72]{0,2,1:T(8,128)(2,1)}, bf16[384,16,72]{0,2,1:T(8,128)(2,1)S(1)}, u32[]{:S(2)}, u32[]{:S(2)}) collective-permute-start(bf16[384,16,72]{0,2,1:T(8,128)(2,1)} %get-tuple-element.990), channel_id=1, source_target_pairs={{0,1},{1,2},{2,3},{3,4},{4,5},{5,6},{6,7},{7,0},{8,9},{9,10},{10,1... | collective-permute-start | bytes 2654216 | tf_op jit(solution)/shard_map/while/body/eval_jaxpr/ppermute | solution.py:18
  731.2 25.5 %collective-permute-start = (bf16[384,16,72]{0,2,1:T(8,128)(2,1)}, bf16[384,16,72]{0,2,1:T(8,128)(2,1)S(1)}, u32[]{:S(2)}, u32[]{:S(2)}) collective-permute-start(bf16[384,16,72]{0,2,1:T(8,128)(2,1)} %get-tuple-element.989), channel_id=1, source_target_pairs={{0,1},{1,2},{2,3},{3,4},{4,5},{5,6},{6,7},{7,0},{8,9},{9,10},{10,1... | collective-permute-start | bytes 2654216 | tf_op jit(solution)/shard_map/while/body/eval_jaxpr/ppermute | solution.py:18
  731.2 38.7 %collective-permute-start.1 = (bf16[384,16,72]{0,2,1:T(8,128)(2,1)}, bf16[384,16,72]{0,2,1:T(8,128)(2,1)S(1)}, u32[]{:S(2)}, u32[]{:S(2)}) collective-permute-start(bf16[384,16,72]{0,2,1:T(8,128)(2,1)} %get-tuple-element.990), channel_id=1, source_target_pairs={{0,1},{1,2},{2,3},{3,4},{4,5},{5,6},{6,7},{7,0},{8,9},{9,10},{10,1... | collective-permute-start | bytes 2654216 | tf_op jit(solution)/shard_map/while/body/eval_jaxpr/ppermute | solution.py:18
  877.8 25.6 %collective-permute-start.4 = (bf16[384,16,72]{0,2,1:T(8,128)(2,1)}, bf16[384,16,72]{0,2,1:T(8,128)(2,1)}, u32[]{:S(2)}, u32[]{:S(2)}) collective-permute-start(bf16[384,16,72]{0,2,1:T(8,128)(2,1)} %fusion.200), channel_id=1, source_target_pairs={{0,1},{1,2},{2,3},{3,4},{4,5},{5,6},{6,7},{7,0},{8,9},{9,10},{10,1... | collective-permute-start | bytes 2654216 | tf_op jit(solution)/shard_map/while/body/eval_jaxpr/ppermute | solution.py:18
  881.1 41.3 %collective-permute-start.5 = (bf16[384,16,72]{0,2,1:T(8,128)(2,1)}, bf16[384,16,72]{0,2,1:T(8,128)(2,1)}, u32[]{:S(2)}, u32[]{:S(2)}) collective-permute-start(bf16[384,16,72]{0,2,1:T(8,128)(2,1)} %fusion.201), channel_id=1, source_target_pairs={{0,1},{1,2},{2,3},{3,4},{4,5},{5,6},{6,7},{7,0},{8,9},{9,10},{10,1... | collective-permute-start | bytes 2654216 | tf_op jit(solution)/shard_map/while/body/eval_jaxpr/ppermute | solution.py:18
  881.1 60.2 %collective-permute-start.2 = (bf16[384,16,72]{0,2,1:T(8,128)(2,1)S(1)}, bf16[384,16,72]{0,2,1:T(8,128)(2,1)S(1)}, u32[]{:S(2)}, u32[]{:S(2)}) collective-permute-start(bf16[384,16,72]{0,2,1:T(8,128)(2,1)S(1)} %copy.129), channel_id=1, source_target_pairs={{0,1},{1,2},{2,3},{3,4},{4,5},{5,6},{6,7},{7,0},{8,9},{9,10},{10,1... | collective-permute-start | bytes 2654216 | tf_op jit(solution)/shard_map/while/body/eval_jaxpr/ppermute | solution.py:18
  881.1 72.6 %collective-permute-start.3 = (bf16[384,16,72]{0,2,1:T(8,128)(2,1)}, bf16[384,16,72]{0,2,1:T(8,128)(2,1)}, u32[]{:S(2)}, u32[]{:S(2)}) collective-permute-start(bf16[384,16,72]{0,2,1:T(8,128)(2,1)} %copy.130), channel_id=1, source_target_pairs={{0,1},{1,2},{2,3},{3,4},{4,5},{5,6},{6,7},{7,0},{8,9},{9,10},{10,1... | collective-permute-start | bytes 2654216 | tf_op jit(solution)/shard_map/while/body/eval_jaxpr/ppermute | solution.py:18
  967.1 25.6 %collective-permute-start.4 = (bf16[384,16,72]{0,2,1:T(8,128)(2,1)}, bf16[384,16,72]{0,2,1:T(8,128)(2,1)}, u32[]{:S(2)}, u32[]{:S(2)}) collective-permute-start(bf16[384,16,72]{0,2,1:T(8,128)(2,1)} %fusion.200), channel_id=1, source_target_pairs={{0,1},{1,2},{2,3},{3,4},{4,5},{5,6},{6,7},{7,0},{8,9},{9,10},{10,1... | collective-permute-start | bytes 2654216 | tf_op jit(solution)/shard_map/while/body/eval_jaxpr/ppermute | solution.py:18
  971.5 40.1 %collective-permute-start.5 = (bf16[384,16,72]{0,2,1:T(8,128)(2,1)}, bf16[384,16,72]{0,2,1:T(8,128)(2,1)}, u32[]{:S(2)}, u32[]{:S(2)}) collective-permute-start(bf16[384,16,72]{0,2,1:T(8,128)(2,1)} %fusion.201), channel_id=1, source_target_pairs={{0,1},{1,2},{2,3},{3,4},{4,5},{5,6},{6,7},{7,0},{8,9},{9,10},{10,1... | collective-permute-start | bytes 2654216 | tf_op jit(solution)/shard_map/while/body/eval_jaxpr/ppermute | solution.py:18
  971.5 59.0 %collective-permute-start.2 = (bf16[384,16,72]{0,2,1:T(8,128)(2,1)S(1)}, bf16[384,16,72]{0,2,1:T(8,128)(2,1)S(1)}, u32[]{:S(2)}, u32[]{:S(2)}) collective-permute-start(bf16[384,16,72]{0,2,1:T(8,128)(2,1)S(1)} %copy.129), channel_id=1, source_target_pairs={{0,1},{1,2},{2,3},{3,4},{4,5},{5,6},{6,7},{7,0},{8,9},{9,10},{10,1... | collective-permute-start | bytes 2654216 | tf_op jit(solution)/shard_map/while/body/eval_jaxpr/ppermute | solution.py:18
  971.5 70.5 %collective-permute-start.3 = (bf16[384,16,72]{0,2,1:T(8,128)(2,1)}, bf16[384,16,72]{0,2,1:T(8,128)(2,1)}, u32[]{:S(2)}, u32[]{:S(2)}) collective-permute-start(bf16[384,16,72]{0,2,1:T(8,128)(2,1)} %copy.130), channel_id=1, source_target_pairs={{0,1},{1,2},{2,3},{3,4},{4,5},{5,6},{6,7},{7,0},{8,9},{9,10},{10,1... | collective-permute-start | bytes 2654216 | tf_op jit(solution)/shard_map/while/body/eval_jaxpr/ppermute | solution.py:18
  1055.5 25.6 %collective-permute-start.4 = (bf16[384,16,72]{0,2,1:T(8,128)(2,1)}, bf16[384,16,72]{0,2,1:T(8,128)(2,1)}, u32[]{:S(2)}, u32[]{:S(2)}) collective-permute-start(bf16[384,16,72]{0,2,1:T(8,128)(2,1)} %fusion.200), channel_id=1, source_target_pairs={{0,1},{1,2},{2,3},{3,4},{4,5},{5,6},{6,7},{7,0},{8,9},{9,10},{10,1... | collective-permute-start | bytes 2654216 | tf_op jit(solution)/shard_map/while/body/eval_jaxpr/ppermute | solution.py:18
  1059.9 40.1 %collective-permute-start.5 = (bf16[384,16,72]{0,2,1:T(8,128)(2,1)}, bf16[384,16,72]{0,2,1:T(8,128)(2,1)}, u32[]{:S(2)}, u32[]{:S(2)}) collective-permute-start(bf16[384,16,72]{0,2,1:T(8,128)(2,1)} %fusion.201), channel_id=1, source_target_pairs={{0,1},{1,2},{2,3},{3,4},{4,5},{5,6},{6,7},{7,0},{8,9},{9,10},{10,1... | collective-permute-start | bytes 2654216 | tf_op jit(solution)/shard_map/while/body/eval_jaxpr/ppermute | solution.py:18
  1059.9 59.0 %collective-permute-start.2 = (bf16[384,16,72]{0,2,1:T(8,128)(2,1)S(1)}, bf16[384,16,72]{0,2,1:T(8,128)(2,1)S(1)}, u32[]{:S(2)}, u32[]{:S(2)}) collective-permute-start(bf16[384,16,72]{0,2,1:T(8,128)(2,1)S(1)} %copy.129), channel_id=1, source_target_pairs={{0,1},{1,2},{2,3},{3,4},{4,5},{5,6},{6,7},{7,0},{8,9},{9,10},{10,1... | collective-permute-start | bytes 2654216 | tf_op jit(solution)/shard_map/while/body/eval_jaxpr/ppermute | solution.py:18
  1059.9 69.6 %collective-permute-start.3 = (bf16[384,16,72]{0,2,1:T(8,128)(2,1)}, bf16[384,16,72]{0,2,1:T(8,128)(2,1)}, u32[]{:S(2)}, u32[]{:S(2)}) collective-permute-start(bf16[384,16,72]{0,2,1:T(8,128)(2,1)} %copy.130), channel_id=1, source_target_pairs={{0,1},{1,2},{2,3},{3,4},{4,5},{5,6},{6,7},{7,0},{8,9},{9,10},{10,1... | collective-permute-start | bytes 2654216 | tf_op jit(solution)/shard_map/while/body/eval_jaxpr/ppermute | solution.py:18
  1143.0 25.6 %collective-permute-start.4 = (bf16[384,16,72]{0,2,1:T(8,128)(2,1)}, bf16[384,16,72]{0,2,1:T(8,128)(2,1)}, u32[]{:S(2)}, u32[]{:S(2)}) collective-permute-start(bf16[384,16,72]{0,2,1:T(8,128)(2,1)} %fusion.200), channel_id=1, source_target_pairs={{0,1},{1,2},{2,3},{3,4},{4,5},{5,6},{6,7},{7,0},{8,9},{9,10},{10,1... | collective-permute-start | bytes 2654216 | tf_op jit(solution)/shard_map/while/body/eval_jaxpr/ppermute | solution.py:18
  1147.4 40.1 %collective-permute-start.5 = (bf16[384,16,72]{0,2,1:T(8,128)(2,1)}, bf16[384,16,72]{0,2,1:T(8,128)(2,1)}, u32[]{:S(2)}, u32[]{:S(2)}) collective-permute-start(bf16[384,16,72]{0,2,1:T(8,128)(2,1)} %fusion.201), channel_id=1, source_target_pairs={{0,1},{1,2},{2,3},{3,4},{4,5},{5,6},{6,7},{7,0},{8,9},{9,10},{10,1... | collective-permute-start | bytes 2654216 | tf_op jit(solution)/shard_map/while/body/eval_jaxpr/ppermute | solution.py:18
  1147.4 59.0 %collective-permute-start.2 = (bf16[384,16,72]{0,2,1:T(8,128)(2,1)S(1)}, bf16[384,16,72]{0,2,1:T(8,128)(2,1)S(1)}, u32[]{:S(2)}, u32[]{:S(2)}) collective-permute-start(bf16[384,16,72]{0,2,1:T(8,128)(2,1)S(1)} %copy.129), channel_id=1, source_target_pairs={{0,1},{1,2},{2,3},{3,4},{4,5},{5,6},{6,7},{7,0},{8,9},{9,10},{10,1... | collective-permute-start | bytes 2654216 | tf_op jit(solution)/shard_map/while/body/eval_jaxpr/ppermute | solution.py:18
  1147.4 68.7 %collective-permute-start.3 = (bf16[384,16,72]{0,2,1:T(8,128)(2,1)}, bf16[384,16,72]{0,2,1:T(8,128)(2,1)}, u32[]{:S(2)}, u32[]{:S(2)}) collective-permute-start(bf16[384,16,72]{0,2,1:T(8,128)(2,1)} %copy.130), channel_id=1, source_target_pairs={{0,1},{1,2},{2,3},{3,4},{4,5},{5,6},{6,7},{7,0},{8,9},{9,10},{10,1... | collective-permute-start | bytes 2654216 | tf_op jit(solution)/shard_map/while/body/eval_jaxpr/ppermute | solution.py:18
  1229.5 25.6 %collective-permute-start.4 = (bf16[384,16,72]{0,2,1:T(8,128)(2,1)}, bf16[384,16,72]{0,2,1:T(8,128)(2,1)}, u32[]{:S(2)}, u32[]{:S(2)}) collective-permute-start(bf16[384,16,72]{0,2,1:T(8,128)(2,1)} %fusion.200), channel_id=1, source_target_pairs={{0,1},{1,2},{2,3},{3,4},{4,5},{5,6},{6,7},{7,0},{8,9},{9,10},{10,1... | collective-permute-start | bytes 2654216 | tf_op jit(solution)/shard_map/while/body/eval_jaxpr/ppermute | solution.py:18
  1233.9 40.1 %collective-permute-start.5 = (bf16[384,16,72]{0,2,1:T(8,128)(2,1)}, bf16[384,16,72]{0,2,1:T(8,128)(2,1)}, u32[]{:S(2)}, u32[]{:S(2)}) collective-permute-start(bf16[384,16,72]{0,2,1:T(8,128)(2,1)} %fusion.201), channel_id=1, source_target_pairs={{0,1},{1,2},{2,3},{3,4},{4,5},{5,6},{6,7},{7,0},{8,9},{9,10},{10,1... | collective-permute-start | bytes 2654216 | tf_op jit(solution)/shard_map/while/body/eval_jaxpr/ppermute | solution.py:18
  1233.9 58.2 %collective-permute-start.2 = (bf16[384,16,72]{0,2,1:T(8,128)(2,1)S(1)}, bf16[384,16,72]{0,2,1:T(8,128)(2,1)S(1)}, u32[]{:S(2)}, u32[]{:S(2)}) collective-permute-start(bf16[384,16,72]{0,2,1:T(8,128)(2,1)S(1)} %copy.129), channel_id=1, source_target_pairs={{0,1},{1,2},{2,3},{3,4},{4,5},{5,6},{6,7},{7,0},{8,9},{9,10},{10,1... | collective-permute-start | bytes 2654216 | tf_op jit(solution)/shard_map/while/body/eval_jaxpr/ppermute | solution.py:18
  1233.9 67.8 %collective-permute-start.3 = (bf16[384,16,72]{0,2,1:T(8,128)(2,1)}, bf16[384,16,72]{0,2,1:T(8,128)(2,1)}, u32[]{:S(2)}, u32[]{:S(2)}) collective-permute-start(bf16[384,16,72]{0,2,1:T(8,128)(2,1)} %copy.130), channel_id=1, source_target_pairs={{0,1},{1,2},{2,3},{3,4},{4,5},{5,6},{6,7},{7,0},{8,9},{9,10},{10,1... | collective-permute-start | bytes 2654216 | tf_op jit(solution)/shard_map/while/body/eval_jaxpr/ppermute | solution.py:18
  1315.2 25.6 %collective-permute-start.4 = (bf16[384,16,72]{0,2,1:T(8,128)(2,1)}, bf16[384,16,72]{0,2,1:T(8,128)(2,1)}, u32[]{:S(2)}, u32[]{:S(2)}) collective-permute-start(bf16[384,16,72]{0,2,1:T(8,128)(2,1)} %fusion.200), channel_id=1, source_target_pairs={{0,1},{1,2},{2,3},{3,4},{4,5},{5,6},{6,7},{7,0},{8,9},{9,10},{10,1... | collective-permute-start | bytes 2654216 | tf_op jit(solution)/shard_map/while/body/eval_jaxpr/ppermute | solution.py:18
  1319.6 40.1 %collective-permute-start.5 = (bf16[384,16,72]{0,2,1:T(8,128)(2,1)}, bf16[384,16,72]{0,2,1:T(8,128)(2,1)}, u32[]{:S(2)}, u32[]{:S(2)}) collective-permute-start(bf16[384,16,72]{0,2,1:T(8,128)(2,1)} %fusion.201), channel_id=1, source_target_pairs={{0,1},{1,2},{2,3},{3,4},{4,5},{5,6},{6,7},{7,0},{8,9},{9,10},{10,1... | collective-permute-start | bytes 2654216 | tf_op jit(solution)/shard_map/while/body/eval_jaxpr/ppermute | solution.py:18
  1319.6 57.2 %collective-permute-start.2 = (bf16[384,16,72]{0,2,1:T(8,128)(2,1)S(1)}, bf16[384,16,72]{0,2,1:T(8,128)(2,1)S(1)}, u32[]{:S(2)}, u32[]{:S(2)}) collective-permute-start(bf16[384,16,72]{0,2,1:T(8,128)(2,1)S(1)} %copy.129), channel_id=1, source_target_pairs={{0,1},{1,2},{2,3},{3,4},{4,5},{5,6},{6,7},{7,0},{8,9},{9,10},{10,1... | collective-permute-start | bytes 2654216 | tf_op jit(solution)/shard_map/while/body/eval_jaxpr/ppermute | solution.py:18
  1319.6 66.7 %collective-permute-start.3 = (bf16[384,16,72]{0,2,1:T(8,128)(2,1)}, bf16[384,16,72]{0,2,1:T(8,128)(2,1)}, u32[]{:S(2)}, u32[]{:S(2)}) collective-permute-start(bf16[384,16,72]{0,2,1:T(8,128)(2,1)} %copy.130), channel_id=1, source_target_pairs={{0,1},{1,2},{2,3},{3,4},{4,5},{5,6},{6,7},{7,0},{8,9},{9,10},{10,1... | collective-permute-start | bytes 2654216 | tf_op jit(solution)/shard_map/while/body/eval_jaxpr/ppermute | solution.py:18
  1399.8 25.6 %collective-permute-start.4 = (bf16[384,16,72]{0,2,1:T(8,128)(2,1)}, bf16[384,16,72]{0,2,1:T(8,128)(2,1)}, u32[]{:S(2)}, u32[]{:S(2)}) collective-permute-start(bf16[384,16,72]{0,2,1:T(8,128)(2,1)} %fusion.200), channel_id=1, source_target_pairs={{0,1},{1,2},{2,3},{3,4},{4,5},{5,6},{6,7},{7,0},{8,9},{9,10},{10,1... | collective-permute-start | bytes 2654216 | tf_op jit(solution)/shard_map/while/body/eval_jaxpr/ppermute | solution.py:18
  1404.2 40.1 %collective-permute-start.5 = (bf16[384,16,72]{0,2,1:T(8,128)(2,1)}, bf16[384,16,72]{0,2,1:T(8,128)(2,1)}, u32[]{:S(2)}, u32[]{:S(2)}) collective-permute-start(bf16[384,16,72]{0,2,1:T(8,128)(2,1)} %fusion.201), channel_id=1, source_target_pairs={{0,1},{1,2},{2,3},{3,4},{4,5},{5,6},{6,7},{7,0},{8,9},{9,10},{10,1... | collective-permute-start | bytes 2654216 | tf_op jit(solution)/shard_map/while/body/eval_jaxpr/ppermute | solution.py:18
  1404.2 56.1 %collective-permute-start.2 = (bf16[384,16,72]{0,2,1:T(8,128)(2,1)S(1)}, bf16[384,16,72]{0,2,1:T(8,128)(2,1)S(1)}, u32[]{:S(2)}, u32[]{:S(2)}) collective-permute-start(bf16[384,16,72]{0,2,1:T(8,128)(2,1)S(1)} %copy.129), channel_id=1, source_target_pairs={{0,1},{1,2},{2,3},{3,4},{4,5},{5,6},{6,7},{7,0},{8,9},{9,10},{10,1... | collective-permute-start | bytes 2654216 | tf_op jit(solution)/shard_map/while/body/eval_jaxpr/ppermute | solution.py:18
  1404.2 65.7 %collective-permute-start.3 = (bf16[384,16,72]{0,2,1:T(8,128)(2,1)}, bf16[384,16,72]{0,2,1:T(8,128)(2,1)}, u32[]{:S(2)}, u32[]{:S(2)}) collective-permute-start(bf16[384,16,72]{0,2,1:T(8,128)(2,1)} %copy.130), channel_id=1, source_target_pairs={{0,1},{1,2},{2,3},{3,4},{4,5},{5,6},{6,7},{7,0},{8,9},{9,10},{10,1... | collective-permute-start | bytes 2654216 | tf_op jit(solution)/shard_map/while/body/eval_jaxpr/ppermute | solution.py:18
  1478.5 21.4 collective-permute-start.6
  1480.8 28.6 %collective-permute-start.7 = (bf16[384,16,72]{0,2,1:T(8,128)(2,1)S(1)}, bf16[384,16,72]{0,2,1:T(8,128)(2,1)S(1)}, u32[]{:S(2)}, u32[]{:S(2)}) collective-permute-start(bf16[384,16,72]{0,2,1:T(8,128)(2,1)S(1)} %fusion.49), channel_id=1, source_target_pairs={{0,1},{1,2},{2,3},{3,4},{4,5},{5,6},{6,7},{7,0},{8,9},{9,10},{10,1... | collective-permute-start | bytes 2654216 | tf_op jit(solution)/shard_map/ppermute | solution.py:18
  1560.8 81.7 %all-reduce.32.cloned.1.call-start = ((), (), s32[]{:S(2)}) async-start(), calls=%async_computation.7 | async-start | bytes 442368 | tf_op jit(solution)/shard_map/psum | solution.py:341
  1561.5 109.1 %reduce-scatter.19.cloned.1.call-start = ((), (), s32[]{:S(2)}) async-start(), calls=%async_computation.10 | async-start | bytes 3317760 | tf_op jit(solution)/shard_map/reduce_scatter | solution.py:367
  1566.0 176.4 %reduce-scatter.17.cloned.1.call-start = ((), (), s32[]{:S(2)}) async-start(), calls=%async_computation.9 | async-start | bytes 9953280 | tf_op jit(solution)/shard_map/reduce_scatter | solution.py:358
  1575.2 255.9 %reduce-scatter.21.cloned.1.call-start = ((), (), s32[]{:S(2)}) async-start(), calls=%async_computation.11 | async-start | bytes 13271040 | tf_op jit(solution)/shard_map/reduce_scatter | solution.py:373
  1586.4 368.3 %reduce-scatter.15.cloned.1.call-start = ((), (), s32[]{:S(2)}) async-start(), calls=%async_computation.8 | async-start | bytes 19906560 | tf_op jit(solution)/shard_map/reduce_scatter | solution.py:352
  1587.2 610.7 %reduce-scatter.25.cloned.1.call-start = ((), (), s32[]{:S(2)}) async-start(), calls=%async_computation.13 | async-start | bytes 2985984 | tf_op jit(solution)/shard_map/reduce_scatter | solution.py:414
  1663.0 534.0 %copy-start.61 = (s32[1,12]{1,0:T(1,128)S(1)}, s32[1,12]{1,0:T(1,128)}, u32[]{:S(2)}) copy-start(s32[1,12]{1,0:T(1,128)} %param.28) | copy-start | bytes 148
  2189.2 21.7 collective-permute-start.11
  2190.6 21.6 collective-permute-start.13
  2194.2 14.7 collective-permute-start.12
  2200.6 15.0 collective-permute-start.9
  2202.8 12.7 collective-permute-start.10
  2208.9 11.0 collective-permute-start.8
  (102 other events, 2214.7 us)
Sparse Core Ops, SparseCore 0:
  11.0 61.7 all-gather.16
  75.6 78.4 all-gather.14
  157.1 90.8 all-gather.18
  250.9 117.6 all-gather.12
  371.4 90.7 all-gather.10
  862.3 83.3 reduce-scatter.22
  1565.5 68.1 all-reduce.31
  1636.4 34.1 reduce-scatter.18
  1673.3 69.1 reduce-scatter.16
  1744.9 86.1 reduce-scatter.20
  1833.7 120.9 reduce-scatter.14
  1958.7 140.4 reduce-scatter.24
where the time goes:
time: 2250 us; the launch traced here: 2230 us
  waiting for transfers between devices  1240 us (55%)
  matrix products  359 us (16%)
  blocking collectives  346 us (15%)
  local copies, waits for them, and re-layouts  142 us (6%)
  other arithmetic  103 us (5%)
    ppermute x44, waiting for transfers between devices, shifted(): lax.ppermute(shard, axis, [(i, (i + by) % count) for i in range(count)])  696 us
    unnamed x4, blocking collectives  318 us
    reduce_scatter x1, waiting for transfers between devices, per_device(): lax.psum_scatter(grad_ada_weight.astype(jnp.bfloat16), 'dp', scatter_dime...  124 us
    all_gather x1, waiting for transfers between devices, per_device(): lax.all_gather(ada_weight, ('dp', 'blk'), axis=0, tiled=True)  106 us
    reduce_scatter x1, waiting for transfers between devices, per_device(): lax.psum_scatter(grad_hidden_weight.astype(jnp.bfloat16), 'dp', scatter_d...  88.6 us
    all_gather x1, waiting for transfers between devices, per_device(): lax.all_gather(hidden_weight, ('dp', 'blk'), axis=0, tiled=True)  81.4 us
    unnamed x174, local copies, waits for them, and re-layouts  81.3 us
    reduce_scatter x1, waiting for transfers between devices, per_device(): lax.psum_scatter(grad_qkv_weight.astype(jnp.bfloat16), 'dp', scatter_dime...  71.8 us
  transfers between devices with their start and end apart: 62, of which 51 were waited for; matrix products, arithmetic and copies ran while one was open for 33% of the time, Pallas kernels for 0%

commit v1 on v0

v1 whole, which is shorter than its diff:
```python
import jax
import jax.numpy as jnp
from jax import lax
from jax.experimental import pallas as pl
from jax.experimental.pallas import tpu as pltpu
from jax.sharding import PartitionSpec as P

HEADS = 16
BIG_SIDE = 32
SMALL_SIDE = 16
BIG_LEN = 512
SMALL_LEN = 128
BLOCK = 128

BF = jnp.bfloat16
F32 = jnp.float32
HIGHEST = lax.Precision.HIGHEST
VMEM_LIMIT = 60 * 1024 * 1024


def cost(us):
    return pl.CostEstimate(flops=int(us * 1.1e9), transcendentals=0, bytes_accessed=1024)


def dot_nn(a, b):
    return lax.dot_general(a, b, (((1,), (0,)), ((), ())), preferred_element_type=F32)


def dot_nt(a, b):
    return lax.dot_general(a, b, (((1,), (1,)), ((), ())), preferred_element_type=F32)


def dot_tn(a, b):
    return lax.dot_general(a, b, (((0,), (0,)), ((), ())), preferred_element_type=F32)


def swap(v, axis, bit):
    count = lax.axis_size(axis)
    return lax.ppermute(v, axis, [(i, i ^ bit) for i in range(count)])


def swap_exact(v, bit, exact):
    at = v.shape[0] - exact
    high = lax.reduce_precision(v, 8, 7)
    rest = lax.reduce_precision(v[at:] - high[at:], 8, 7)
    got = swap(jnp.concatenate([high, rest], axis=0).astype(BF), "blk", bit).astype(F32)
    return jnp.concatenate([got[:at], got[at : v.shape[0]] + got[v.shape[0] :]], axis=0)


def dp_gather(v):
    core, y = lax.axis_index("dp") % 2, lax.axis_index("dp") // 2
    other = swap(v, "dp", 1)
    pair = jnp.stack([jnp.where(core == 0, v, other), jnp.where(core == 0, other, v)])
    across = swap(pair, "dp", 2)
    return jnp.concatenate([jnp.where(y == 0, pair, across), jnp.where(y == 0, across, pair)])


def pair_up(v, axis, bit_value, bit):
    got = swap(v, axis, bit)
    return jnp.concatenate(
        [jnp.where(bit_value == 0, v, got), jnp.where(bit_value == 0, got, v)], axis=0
    )


def gather_line(shard, z):
    line = pair_up(pair_up(shard, "blk", z // 2, 4), "blk", z % 2, 2)
    return line.reshape(4, *shard.shape)


def gather_cross(line, x, y):
    _, n, width = line.shape
    first = line[:, : n // 2].reshape(-1, width)
    last = line[:, n // 2 :].reshape(-1, width)
    return pair_up(first, "blk", x, 1), pair_up(last, "dp", y, 2)


def gather_wide(first, last, x, y):
    return pair_up(first, "dp", y, 2), pair_up(last, "blk", x, 1)


def both_cores(first, last):
    return first, last, swap(first, "dp", 1), swap(last, "dp", 1)


def unpack_weight(core, parts, rows, groups, name):
    width = parts[0].shape[1]
    half = len(groups) // 2
    n_out = max(o for o, _ in groups) + 1
    widths = [(max(c for o, c in groups if o == k) + 1) * width for k in range(n_out)]

    def body(core_ref, a_own, b_own, a_oth, b_oth, *outs):
        dp = pl.program_id(0)
        for a_ref, b_ref, own in ((a_own, b_own, True), (a_oth, b_oth, False)):

            @pl.when((dp % 2 == core_ref[0]) == own)
            def _(a_ref=a_ref, b_ref=b_ref):
                for z in range(4):
                    for x in range(2):
                        at = (z * 2 + x) * rows
                        for g, (o, c) in enumerate(groups):
                            ref = a_ref if g < half else b_ref
                            start = ((x * 4 + z_place(z)) * half + g % half) * rows
                            columns = slice(c * width, (c + 1) * width)
                            if g < half:
                                outs[o][at : at + rows, columns] = ref[start : start + rows, :]
                            else:
                                outs[o][at : at + rows, columns] = ref[x, 0][
                                    (z_place(z) * half + g % half)
                                    * rows : (z_place(z) * half + g % half + 1)
                                    * rows,
                                    :,
                                ]

    chunk = 8 * half * rows
    by_y = pl.BlockSpec((chunk, width), lambda i, c: (i // 2, 0))
    by_x = pl.BlockSpec((2, 1, chunk // 2, width), lambda i, c: (0, i // 2, 0, 0))
    turned = [p.reshape(2, 2, chunk // 2, width) for p in (parts[1], parts[3])]
    return pl.pallas_call(
        body,
        grid_spec=pltpu.PrefetchScalarGridSpec(
            num_scalar_prefetch=1,
            grid=(4,),
            in_specs=[by_y, by_x, by_y, by_x],
            out_specs=[pl.BlockSpec((8 * rows, w), lambda i, c: (i, 0)) for w in widths],
        ),
        out_shape=[jax.ShapeDtypeStruct((32 * rows, w), BF) for w in widths],
        compiler_params=pltpu.CompilerParams(vmem_limit_bytes=VMEM_LIMIT),
        cost_estimate=cost(10),
        name=name,
    )(core, parts[0], turned[0], parts[2], turned[1])


def unpack_rows(core, parts, rows, name):
    width = parts[0].shape[1]
    half = rows // 2

    def body(core_ref, a_own, b_own, a_oth, b_oth, out):
        dp = pl.program_id(0)
        for a_ref, b_ref, own in ((a_own, b_own, True), (a_oth, b_oth, False)):

            @pl.when((dp % 2 == core_ref[0]) == own)
            def _(a_ref=a_ref, b_ref=b_ref):
                for z in range(4):
                    for x in range(2):
                        at = (z * 2 + x) * rows
                        start = (x * 4 + z_place(z)) * half
                        out[at : at + half, :] = a_ref[start : start + half, :]
                        start = z_place(z) * half
                        out[at + half : at + rows, :] = b_ref[x, 0][start : start + half, :]

    by_y = pl.BlockSpec((8 * half, width), lambda i, c: (i // 2, 0))
    by_x = pl.BlockSpec((2, 1, 4 * half, width), lambda i, c: (0, i // 2, 0, 0))
    turned = [p.reshape(2, 2, 4 * half, width) for p in (parts[1], parts[3])]
    return pl.pallas_call(
        body,
        grid_spec=pltpu.PrefetchScalarGridSpec(
            num_scalar_prefetch=1,
            grid=(4,),
            in_specs=[by_y, by_x, by_y, by_x],
            out_specs=pl.BlockSpec((8 * rows, width), lambda i, c: (i, 0)),
        ),
        out_shape=jax.ShapeDtypeStruct((32 * rows, width), BF),
        compiler_params=pltpu.CompilerParams(vmem_limit_bytes=VMEM_LIMIT),
        cost_estimate=cost(10),
        name=name,
    )(core, parts[0], turned[0], parts[2], turned[1])


def z_place(z):
    return z % 2 * 2 + z // 2


def chip_grads(lefts, rights, products, orders, turned, shape, name):
    tokens, width = shape
    parts = [own.shape[0] // 2 if turned else own.shape[1] for own, _ in lefts]
    height = [
        sum(n for _, _, _, pieces in products for _, n, out, _ in pieces if out == o)
        for o in range(len(orders))
    ]
    n_left, n_right = len(lefts), len(rights)
    product_of = dot_nn if turned else dot_tn

    def body(*refs):
        lefts_own, lefts_oth = refs[:n_left], refs[n_left : 2 * n_left]
        rights_own = refs[2 * n_left : 2 * n_left + n_right]
        rights_oth = refs[2 * n_left + n_right : 2 * n_left + 2 * n_right]
        outs, acc = refs[2 * n_left + 2 * n_right : -1], refs[-1]
        y = pl.program_id(0)
        for li, ri, chunk, pieces in products:
            acc[: 8 * chunk, :] = product_of(
                lefts_own[li][...], rights_own[ri][...]
            ) + product_of(lefts_oth[li][...], rights_oth[ri][...])
            for j in range(8):
                z, x = j // 2, j % 2
                for start, n, out, at in pieces:
                    value = acc[j * chunk + start : j * chunk + start + n, :].astype(BF)
                    if orders[out] == "yxz":
                        row = (x * 4 + z_place(z)) * height[out] + at
                        outs[out][row : row + n, :] = value
                    else:
                        for yy in range(2):
                            row = ((x * 2 + yy) * 4 + z_place(z)) * height[out] + at

                            @pl.when(y == yy)
                            def _(row=row, value=value, out=out, n=n):
                                outs[out][row : row + n, :] = value

    left_specs = [
        pl.BlockSpec((p, tokens) if turned else (tokens, p), lambda i: (i, 0)) for p in parts
    ]
    right_specs = [
        pl.BlockSpec((tokens, width), lambda i, r=r, k=k: (r, k)) for _, _, r, k in rights
    ]
    out_specs, out_shape = [], []
    for order, h in zip(orders, height):
        if order == "yxz":
            out_specs.append(pl.BlockSpec((8 * h, width), lambda i: (i, 0)))
        else:
            out_specs.append(pl.BlockSpec((16 * h, width), lambda i: (0, 0)))
        out_shape.append(jax.ShapeDtypeStruct((16 * h, width), BF))
    total = sum(16 * h for h in height)
    return pl.pallas_call(
        body,
        grid=(2,),
        in_specs=left_specs * 2 + right_specs * 2,
        out_specs=out_specs,
        out_shape=out_shape,
        scratch_shapes=[pltpu.VMEM((max(parts), width), F32)],
        compiler_params=pltpu.CompilerParams(vmem_limit_bytes=VMEM_LIMIT),
        cost_estimate=cost(10),
        name=name,
    )(
        *[own for own, _ in lefts],
        *[oth for _, oth in lefts],
        *[r[0] for r in rights],
        *[r[1] for r in rights],
    )


def split_by(v, bit):
    both = v.reshape(2, v.shape[0] // 2, v.shape[1])
    return (
        lax.dynamic_index_in_dim(both, 1 - bit, 0, keepdims=False),
        lax.dynamic_index_in_dim(both, bit, 0, keepdims=False),
    )


def add(a, b):
    return a.astype(F32) + b.astype(F32)


def send(halves, axis, bit):
    sent, kept = halves
    return kept, swap(sent, axis, bit)


def joined(pair):
    return add(*pair).astype(BF)


def side_by_side(v_a, v_b):
    shape = (4, 1, v_a.shape[0] // 4, v_a.shape[1])
    return jnp.concatenate([v_a.reshape(shape), v_b.reshape(shape)], axis=1).reshape(
        2 * v_a.shape[0], v_a.shape[1]
    )


def head_window(h, size):
    first = h * size // 128
    last = ((h + 1) * size - 1) // 128
    return first * 128, (last + 1) * 128, h * size - first * 128


def lane_mask(shape, start, size):
    lane = lax.broadcasted_iota(jnp.int32, shape, 1)
    return (lane >= start) & (lane < start + size)


def attend_forward(info, queries, keys, values, heads):
    tokens, width = queries.shape[0] // 3, queries.shape[1]
    size = width // heads
    scale = size**-0.5
    blocks = tokens // BLOCK

    def body(info_ref, q_ref, k_ref, v_ref, o_ref, lse_ref):
        def one_block(i, carry):
            row = pl.multiple_of(i * BLOCK, BLOCK)
            start = pl.multiple_of(info_ref[i], BLOCK)

            def run(length):
                lse_all = jnp.zeros((BLOCK, 128), F32)
                for h in range(heads):
                    lo, hi, off = head_window(h, size)
                    q = q_ref[pl.ds(row, BLOCK), lo:hi]
                    mask = lane_mask(q.shape, off, size)
                    q = jnp.where(mask, q, jnp.zeros_like(q))
                    k = k_ref[pl.ds(start, length), lo:hi]
                    v = v_ref[pl.ds(start, length), lo:hi]
                    s = dot_nt(q, k) * scale
                    peak = jnp.max(s, axis=1, keepdims=True)
                    p = jnp.exp(s - peak)
                    total = jnp.sum(p, axis=1, keepdims=True)
                    o = (dot_nn(p.astype(BF), v) * (1.0 / total)).astype(BF)
                    if off == 0:
                        o_ref[pl.ds(row, BLOCK), lo:hi] = o
                    else:
                        o_ref[pl.ds(row, BLOCK), lo:hi] = jnp.where(
                            mask, o, o_ref[pl.ds(row, BLOCK), lo:hi]
                        )
                    lse_all = jnp.where(
                        lane_mask(lse_all.shape, h, 1), peak + jnp.log(total), lse_all
                    )
                lse_ref[pl.ds(row, BLOCK), :] = lse_all

            @pl.when(info_ref[blocks + i] == 1)
            def _():
                run(BIG_LEN)

            @pl.when(info_ref[blocks + i] == 0)
            def _():
                run(SMALL_LEN)

            return carry

        lax.fori_loop(0, blocks, one_block, 0)

    return pl.pallas_call(
        body,
        grid_spec=pltpu.PrefetchScalarGridSpec(
            num_scalar_prefetch=1,
            grid=(1,),
            in_specs=[
                pl.BlockSpec((tokens, width), lambda i, s: (1, 0)),
                pl.BlockSpec((3 * tokens, width), lambda i, s: (0, 0)),
                pl.BlockSpec((3 * tokens, width), lambda i, s: (0, 0)),
            ],
            out_specs=[
                pl.BlockSpec((tokens, width), lambda i, s: (0, 0)),
                pl.BlockSpec((tokens, 128), lambda i, s: (0, 0)),
            ],
        ),
        out_shape=[
            jax.ShapeDtypeStruct((tokens, width), BF),
            jax.ShapeDtypeStruct((tokens, 128), F32),
        ],
        compiler_params=pltpu.CompilerParams(vmem_limit_bytes=VMEM_LIMIT),
        cost_estimate=cost(15),
        name="attend_forward",
    )(info, queries, keys, values)


def backward_pairs(q_ref, g_ref, k_ref, v_ref, dk, dv, heads, size):
    scale = size**-0.5
    width = heads * size

    def term(row, lane):
        at = [width + lane + 2 * heads * k for k in range(3)]
        return sum(g_ref[pl.ds(row, BLOCK), i : i + 1].astype(F32) for i in at)

    def pairs(row, start, length, at, dq, dq_at):
        for h in range(heads):
            lo, hi, off = head_window(h, size)
            q = q_ref[pl.ds(row, BLOCK), lo:hi]
            mask = lane_mask(q.shape, off, size)
            q = jnp.where(mask, q, jnp.zeros_like(q))
            g = g_ref[pl.ds(row, BLOCK), lo:hi]
            g = jnp.where(mask, g, jnp.zeros_like(g))
            k = k_ref[pl.ds(start, length), lo:hi]
            v = v_ref[pl.ds(start, length), lo:hi]
            lse, delta = term(row, h), term(row, heads + h)
            p = jnp.exp(dot_nt(q, k) * scale - lse)
            ds = (p * (dot_nt(g, v) - delta)).astype(BF)
            dv[pl.ds(at, length), lo:hi] += dot_tn(p.astype(BF), g)
            dk[pl.ds(at, length), lo:hi] += dot_tn(ds, q)
            if dq is not None:
                part = dot_nn(ds, k)
                dq[pl.ds(dq_at, BLOCK), lo:hi] += jnp.where(mask, part, jnp.zeros_like(part))

    return pairs


def attend_backward_own(info, queries, keys, values, grads, heads):
    tokens, width = grads.shape[0], queries.shape[1]
    size = width // heads
    scale = size**-0.5
    blocks = tokens // BLOCK

    def body(info_ref, q_ref, k_ref, v_ref, g_ref, dq_ref, dk_ref, dv_ref, dq, dk, dv):
        dq[...] = jnp.zeros_like(dq)
        dk[...] = jnp.zeros_like(dk)
        dv[...] = jnp.zeros_like(dv)
        pairs = backward_pairs(q_ref, g_ref, k_ref, v_ref, dk, dv, heads, size)

        def own_block(i, carry):
            row = pl.multiple_of(i * BLOCK, BLOCK)
            start = pl.multiple_of(info_ref[i], BLOCK)

            @pl.when(info_ref[blocks + i] == 1)
            def _():
                pairs(row, start, BIG_LEN, start, dq, row)

            @pl.when(info_ref[blocks + i] == 0)
            def _():
                pairs(row, start, SMALL_LEN, start, dq, row)

            return carry

        lax.fori_loop(0, blocks, own_block, 0)
        dq_ref[...] = (dq[...] * scale).astype(BF)
        dk_ref[...] = dk[tokens : 2 * tokens, :]
        dv_ref[...] = dv[tokens : 2 * tokens, :]

    full = pl.BlockSpec((3 * tokens, width), lambda i, s: (0, 0))
    own = pl.BlockSpec((tokens, width), lambda i, s: (0, 0))
    return pl.pallas_call(
        body,
        grid_spec=pltpu.PrefetchScalarGridSpec(
            num_scalar_prefetch=1,
            grid=(1,),
            in_specs=[pl.BlockSpec((tokens, width), lambda i, s: (1, 0)), full, full, pl.BlockSpec((tokens, width + 128), lambda i, s: (0, 0))],
            out_specs=[own] * 3,
            scratch_shapes=[
                pltpu.VMEM((tokens, width), F32),
                pltpu.VMEM((3 * tokens, width), F32),
                pltpu.VMEM((3 * tokens, width), F32),
            ],
        ),
        out_shape=[
            jax.ShapeDtypeStruct((tokens, width), BF),
            jax.ShapeDtypeStruct((tokens, width), F32),
            jax.ShapeDtypeStruct((tokens, width), F32),
        ],
        compiler_params=pltpu.CompilerParams(vmem_limit_bytes=VMEM_LIMIT),
        cost_estimate=cost(24),
        name="attend_backward_own",
    )(info, queries, keys, values, grads)


def attend_backward_other(info, queries, keys, values, g_near, g_far, dk_own, dv_own, heads):
    tokens, width = g_near.shape[0], queries.shape[1]
    size = width // heads
    scale = size**-0.5
    blocks = tokens // BLOCK

    def body(
        info_ref, q_near, q_far, k_ref, v_ref, gn, gf, dk_in, dv_in, out_ref, dk, dv
    ):
        dk[...] = dk_in[...]
        dv[...] = dv_in[...]
        for side, (q_ref, g_ref) in enumerate(((q_near, gn), (q_far, gf))):
            pairs = backward_pairs(q_ref, g_ref, k_ref, v_ref, dk, dv, heads, size)

            def one(t, carry, pairs=pairs, side=side):
                a, own = t // blocks, t % blocks

                @pl.when(info_ref[a + 2 * blocks * side] == info_ref[blocks + own])
                def _():
                    at = pl.multiple_of(own * BLOCK, BLOCK)
                    pairs(pl.multiple_of(a * BLOCK, BLOCK), at, BLOCK, at, None, 0)

                return carry

            lax.fori_loop(0, blocks * blocks, one, 0)
        out_ref[:, :width] = (dk[...] * scale).astype(BF)
        out_ref[:, width:] = dv[...].astype(BF)

    own = pl.BlockSpec((tokens, width), lambda i, s: (0, 0))
    near = pl.BlockSpec((tokens, width), lambda i, s: (2 - 2 * s[3 * blocks], 0))
    far = pl.BlockSpec((tokens, width), lambda i, s: (2 * s[3 * blocks], 0))
    middle = pl.BlockSpec((tokens, width), lambda i, s: (1, 0))
    wide = pl.BlockSpec((tokens, width + 128), lambda i, s: (0, 0))
    return pl.pallas_call(
        body,
        grid_spec=pltpu.PrefetchScalarGridSpec(
            num_scalar_prefetch=1,
            grid=(1,),
            in_specs=[near, far, middle, middle, wide, wide, own, own],
            out_specs=pl.BlockSpec((tokens, 2 * width), lambda i, s: (0, 0)),
            scratch_shapes=[pltpu.VMEM((tokens, width), F32), pltpu.VMEM((tokens, width), F32)],
        ),
        out_shape=jax.ShapeDtypeStruct((tokens, 2 * width), BF),
        compiler_params=pltpu.CompilerParams(vmem_limit_bytes=VMEM_LIMIT),
        cost_estimate=cost(22),
        name="attend_backward_other",
    )(info, queries, queries, keys, values, g_near, g_far, dk_own, dv_own)


def layer_norm(v):
    centered = v - jnp.mean(v, axis=1, keepdims=True)
    spread = jnp.mean(centered * centered, axis=1, keepdims=True)
    inverse = lax.rsqrt(spread + 1e-06)
    return centered * inverse, inverse


def norm_back(grad_in, normed, inverse):
    mean_grad = jnp.mean(grad_in, axis=1, keepdims=True)
    mean_proj = jnp.mean(grad_in * normed, axis=1, keepdims=True)
    return inverse * (grad_in - mean_grad - normed * mean_proj)


def column_sum(v):
    return jnp.sum(v.astype(F32), axis=0, keepdims=True)


def whole(shape, dtype=None):
    return pl.BlockSpec(shape, lambda *_: (0,) * len(shape))


def store_turned(core, value, keep_ref, send_ref):
    turned = value.astype(F32).T.astype(BF)
    part = turned.shape[0] // 4
    for c in range(2):

        @pl.when(core == c)
        def _():
            for y in range(2):
                keep_ref[y * part : (y + 1) * part, :] = turned[
                    (2 * y + c) * part : (2 * y + c + 1) * part, :
                ]
                send_ref[y * part : (y + 1) * part, :] = turned[
                    (2 * y + 1 - c) * part : (2 * y + 2 - c) * part, :
                ]


def attention_input(core, parts, places, table, mods):
    tokens, width = parts[0].shape
    blocks = tokens // BLOCK

    def body(core_ref, near, own, far, place_ref, table_ref, mod_ref, in_ref, hid_ref, keep, send):
        steps = lax.broadcasted_iota(jnp.int32, (BIG_SIDE, BLOCK), 0)
        flip = core_ref[1]
        bases = (2 * blocks * (1 - flip), blocks, 2 * blocks * flip)
        for source, base in zip((near, own, far), bases):
            for i in range(blocks):
                b = base + i
                at = pl.ds(pl.multiple_of(b * BLOCK, BLOCK), BLOCK)
                place = jnp.concatenate(
                    [
                        lax.dot_general(
                            (steps == place_ref[r : r + 1, at]).astype(F32),
                            table_ref[...],
                            (((0,), (0,)), ((), ())),
                            precision=HIGHEST,
                            preferred_element_type=F32,
                        )
                        for r in range(2)
                    ],
                    axis=1,
                )
                hidden = source[i * BLOCK : (i + 1) * BLOCK, :].astype(F32) + place
                normed, _ = layer_norm(hidden)
                value = (
                    normed * (1.0 + mod_ref[pl.ds(b, 1), width : 2 * width])
                    + mod_ref[pl.ds(b, 1), :width]
                )
                in_ref[at, :] = value.astype(BF)
                if source is own:
                    hid_ref[i * BLOCK : (i + 1) * BLOCK, :] = hidden
        store_turned(core_ref[0], in_ref[tokens : 2 * tokens, :], keep, send)

    half = jax.ShapeDtypeStruct((width // 2, tokens), BF)
    return pl.pallas_call(
        body,
        grid_spec=pltpu.PrefetchScalarGridSpec(
            num_scalar_prefetch=1,
            grid=(1,),
            in_specs=[whole((tokens, width))] * 3
            + [whole(places.shape), whole(table.shape), whole(mods.shape)],
            out_specs=[
                whole((3 * tokens, width)),
                whole((tokens, width)),
                whole(half.shape),
                whole(half.shape),
            ],
        ),
        out_shape=[
            jax.ShapeDtypeStruct((3 * tokens, width), BF),
            jax.ShapeDtypeStruct((tokens, width), F32),
            half,
            half,
        ],
        compiler_params=pltpu.CompilerParams(vmem_limit_bytes=VMEM_LIMIT),
        cost_estimate=cost(10),
        name="attention_input",
    )(core, *parts, places, table, mods)


def after_attention(core, attn_low, proj, proj_bias, hidden, mods):
    tokens, width = hidden.shape
    blocks = tokens // BLOCK

    def body(
        core_ref, low, w_ref, b_ref, hid, mod, branch, after, mlp_in, keep_m, keep_a, send
    ):
        for b in range(blocks):
            rows = slice(b * BLOCK, (b + 1) * BLOCK)
            value = dot_nn(low[rows, :], w_ref[...]) + b_ref[0:1, :]
            branch[rows, :] = value
            done = hid[rows, :] + mod[b : b + 1, 2 * width : 3 * width] * value
            after[rows, :] = done
            normed, _ = layer_norm(done)
            mlp_in[rows, :] = (
                normed * (1.0 + mod[b : b + 1, 4 * width : 5 * width])
                + mod[b : b + 1, 3 * width : 4 * width]
            ).astype(BF)
        store_turned(core_ref[0], mlp_in[...], keep_m, send.at[: width // 2, :])
        store_turned(core_ref[0], low[...], keep_a, send.at[width // 2 :, :])

    half = jax.ShapeDtypeStruct((width // 2, tokens), BF)
    full = jax.ShapeDtypeStruct((tokens, width), F32)
    return pl.pallas_call(
        body,
        grid_spec=pltpu.PrefetchScalarGridSpec(
            num_scalar_prefetch=1,
            grid=(1,),
            in_specs=[
                whole((tokens, width)),
                whole((width, width)),
                whole((8, width)),
                whole((tokens, width)),
                whole(mods.shape),
            ],
            out_specs=[whole((tokens, width))] * 3 + [whole(half.shape)] * 2 + [whole((width, tokens))],
        ),
        out_shape=[full, full, jax.ShapeDtypeStruct((tokens, width), BF)] + [half] * 2
        + [jax.ShapeDtypeStruct((width, tokens), BF)],
        compiler_params=pltpu.CompilerParams(vmem_limit_bytes=VMEM_LIMIT),
        cost_estimate=cost(8),
        name="after_attention",
    )(core, attn_low, proj, proj_bias, hidden, mods)


def feed_forward_up(order, mlp_in, hidden_w, hidden_b):
    tokens, width = mlp_in.shape

    def body(order_ref, x, wh, bh, keep, send, slope):
        t = pl.program_id(0)
        up = dot_nn(x[...], wh[...]) + bh[0:1, :]
        square = up * up
        wave = jnp.tanh(0.7978845608028654 * up * (1.0 + 0.044715 * square))
        act = (0.5 * up * (1.0 + wave)).astype(BF)
        slope[...] = (
            0.5 * (1.0 + wave)
            + 0.5 * up * (1.0 - wave * wave) * 0.7978845608028654 * (1.0 + 0.134145 * square)
        ).astype(BF)

        @pl.when(t < 2)
        def _():
            send[...] = act

        @pl.when(t >= 2)
        def _():
            keep[...] = act

    return pl.pallas_call(
        body,
        grid_spec=pltpu.PrefetchScalarGridSpec(
            num_scalar_prefetch=1,
            grid=(4,),
            in_specs=[
                whole((tokens, width)),
                pl.BlockSpec((width, width), lambda t, o: (0, o[t])),
                pl.BlockSpec((8, width), lambda t, o: (0, o[t])),
            ],
            out_specs=[
                pl.BlockSpec((tokens, width), lambda t, o: (jnp.maximum(t - 2, 0), 0)),
                pl.BlockSpec((tokens, width), lambda t, o: (jnp.minimum(t, 1), 0)),
                pl.BlockSpec((tokens, width), lambda t, o: (0, o[t])),
            ],
        ),
        out_shape=[
            jax.ShapeDtypeStruct((2 * tokens, width), BF),
            jax.ShapeDtypeStruct((3 * tokens, width), BF),
            jax.ShapeDtypeStruct((tokens, 4 * width), BF),
        ],
        compiler_params=pltpu.CompilerParams(vmem_limit_bytes=VMEM_LIMIT),
        cost_estimate=cost(1),
        name="feed_forward_up",
    )(order, mlp_in, hidden_w, hidden_b)


def feed_forward_down(order, keep, send, output_w, output_b, after, cotangent, mods):
    tokens, width = after.shape
    blocks = tokens // BLOCK

    def body(order_ref, keep_ref, send_ref, wo, bo, after_ref, cot, mod, low, out, sums, acc):
        t = pl.program_id(0)

        @pl.when(t == 0)
        def _():
            acc[...] = dot_nn(send_ref[...], wo[...])

        @pl.when(t == 1)
        def _():
            acc[...] += dot_nn(send_ref[...], wo[...])

        @pl.when(t >= 2)
        def _():
            acc[...] += dot_nn(keep_ref[...], wo[...])

        @pl.when(t == 3)
        def _():
            sums[...] = jnp.zeros_like(sums)
            for b in range(blocks):
                rows = slice(b * BLOCK, (b + 1) * BLOCK)
                gate = mod[b : b + 1, 5 * width : 6 * width]
                lower = acc[rows, :] + bo[0:1, :]
                g = cot[rows, :].astype(F32)
                out[rows, :] = (after_ref[rows, :] + gate * lower).astype(BF)
                low[rows, :] = (g * gate).astype(BF)
                sums[b : b + 1, :] = column_sum(g * lower)
            sums[blocks : blocks + 1, :] = column_sum(low[...])

    row = whole((tokens, width))
    return pl.pallas_call(
        body,
        grid_spec=pltpu.PrefetchScalarGridSpec(
            num_scalar_prefetch=1,
            grid=(4,),
            in_specs=[
                pl.BlockSpec((tokens, width), lambda t, o: (jnp.maximum(t - 2, 0), 0)),
                pl.BlockSpec((tokens, width), lambda t, o: (jnp.minimum(t, 1), 0)),
                pl.BlockSpec((width, width), lambda t, o: (o[t], 0)),
                whole((8, width)),
                row,
                row,
                whole(mods.shape),
            ],
            out_specs=[
                pl.BlockSpec((tokens, width), lambda t, o: (2, 0)),
                row,
                whole((8, width)),
            ],
            scratch_shapes=[pltpu.VMEM((tokens, width), F32)],
        ),
        out_shape=[
            jax.ShapeDtypeStruct((3 * tokens, width), BF),
            jax.ShapeDtypeStruct((tokens, width), BF),
            jax.ShapeDtypeStruct((8, width), F32),
        ],
        input_output_aliases={2: 0},
        compiler_params=pltpu.CompilerParams(vmem_limit_bytes=VMEM_LIMIT),
        cost_estimate=cost(12),
        name="feed_forward_down",
    )(order, keep, send, output_w, output_b, after, cotangent, mods)


def feed_forward_back(
    act_and_lower, slope, hidden_w, output_w, proj, after, branch, attn_low, lse, cotangent, mods, heads
):
    tokens, width = after.shape
    blocks = tokens // BLOCK
    size = width // heads

    def body(
        gl,
        sl,
        wh,
        wo,
        wp,
        after_ref,
        br,
        low,
        lse_ref,
        cot,
        mod,
        gu,
        ga,
        gat,
        up_sums,
        sums,
        acc,
    ):
        t = pl.program_id(0)
        up = (dot_nt(gl[...], wo[...]) * sl[...].astype(F32)).astype(BF)
        gu[:, pl.ds(pl.multiple_of(t * width, 128), width)] = up
        up_sums[...] = jnp.broadcast_to(column_sum(up), up_sums.shape)
        part = dot_nt(up, wh[...])

        @pl.when(t == 0)
        def _():
            acc[...] = part

        @pl.when(t > 0)
        def _():
            acc[...] += part

        @pl.when(t == 3)
        def _():
            sums[...] = jnp.zeros_like(sums)
            head = lax.broadcasted_iota(jnp.int32, (width, 128), 0)
            first = (lax.broadcasted_iota(jnp.int32, (width, 128), 1) - heads) * size
            pick = ((head >= first) & (head < first + size)).astype(BF)
            total = jnp.zeros((1, width), F32)
            for b in range(blocks):
                rows = slice(b * BLOCK, (b + 1) * BLOCK)
                gin = acc[rows, :]
                normed, inverse = layer_norm(after_ref[rows, :])
                value = cot[rows, :].astype(F32) + norm_back(
                    gin * (1.0 + mod[b : b + 1, 4 * width : 5 * width]), normed, inverse
                )
                ga[rows, :] = value
                sums[b : b + 1, :width] = column_sum(value * br[rows, :])
                sums[b : b + 1, width : 2 * width] = column_sum(gin)
                sums[b : b + 1, 2 * width : 3 * width] = column_sum(gin * normed)
                low_branch = (value * mod[b : b + 1, 2 * width : 3 * width]).astype(BF)
                gu[rows, 4 * width :] = low_branch
                total = total + column_sum(low_branch)
                grad = dot_nt(low_branch, wp[...]).astype(BF)
                gat[rows, :width] = grad
                product = grad.astype(F32) * low[rows, :].astype(F32)
                high = product.astype(BF)
                rest = (product - high.astype(F32)).astype(BF)
                value = lse_ref[rows, :] + dot_nn(high, pick) + dot_nn(rest, pick)
                terms = jnp.zeros((BLOCK, 128), F32)
                for k in range(3):
                    term = value.astype(BF).astype(F32)
                    terms = terms + (pltpu.roll(term, 2 * heads * k, axis=1) if k else term)
                    value = value - term
                gat[rows, width:] = terms.astype(BF)
            sums[blocks : blocks + 1, :width] = total

    row = whole((tokens, width))
    return pl.pallas_call(
        body,
        grid=(4,),
        in_specs=[
            pl.BlockSpec((tokens, width), lambda t: (2, 0)),
            pl.BlockSpec((tokens, width), lambda t: (0, t)),
            pl.BlockSpec((width, width), lambda t: (0, t)),
            pl.BlockSpec((width, width), lambda t: (t, 0)),
            whole((width, width)),
            row,
            row,
            row,
            whole((tokens, 128)),
            row,
            whole(mods.shape),
        ],
        out_specs=[
            whole((tokens, 5 * width)),
            row,
            whole((tokens, width + 128)),
            pl.BlockSpec((8, width), lambda t: (0, t)),
            whole((8, 3 * width)),
        ],
        out_shape=[
            jax.ShapeDtypeStruct((tokens, 5 * width), BF),
            jax.ShapeDtypeStruct((tokens, width), F32),
            jax.ShapeDtypeStruct((tokens, width + 128), BF),
            jax.ShapeDtypeStruct((8, 4 * width), F32),
            jax.ShapeDtypeStruct((8, 3 * width), F32),
        ],
        scratch_shapes=[pltpu.VMEM((tokens, width), F32)],
        compiler_params=pltpu.CompilerParams(vmem_limit_bytes=VMEM_LIMIT),
        cost_estimate=cost(24),
        name="feed_forward_back",
    )(
        act_and_lower,
        slope,
        hidden_w,
        output_w,
        proj,
        after,
        branch,
        attn_low,
        lse,
        cotangent,
        mods,
    )


def input_gradient(grads, qkv, hidden, grad_after, mods):
    tokens, width = hidden.shape
    blocks = tokens // BLOCK

    def body(gq, gkv, w_ref, hid, ga, mod, out, sums):
        sums[...] = jnp.zeros_like(sums)
        for b in range(blocks):
            rows = slice(b * BLOCK, (b + 1) * BLOCK)
            gin = (
                dot_nt(gq[rows, :], w_ref[:, :width])
                + dot_nt(gkv[rows, :], w_ref[:, width:])
            )
            normed, inverse = layer_norm(hid[rows, :])
            out[rows, :] = ga[rows, :] + norm_back(
                gin * (1.0 + mod[b : b + 1, width : 2 * width]), normed, inverse
            )
            sums[b : b + 1, :width] = column_sum(gin)
            sums[b : b + 1, width : 2 * width] = column_sum(gin * normed)
        sums[blocks : blocks + 1, :width] = column_sum(gq[...])
        sums[blocks : blocks + 1, width : 2 * width] = column_sum(gkv[:, width:])

    row = whole((tokens, width))
    return pl.pallas_call(
        body,
        grid=(1,),
        in_specs=[row, whole((tokens, 2 * width)), whole(qkv.shape), row, row, whole(mods.shape)],
        out_specs=[row, whole((8, 2 * width))],
        out_shape=[
            jax.ShapeDtypeStruct((tokens, width), F32),
            jax.ShapeDtypeStruct((8, 2 * width), F32),
        ],
        compiler_params=pltpu.CompilerParams(vmem_limit_bytes=VMEM_LIMIT),
        cost_estimate=cost(14),
        name="input_gradient",
    )(*grads, qkv, hidden, grad_after, mods)


def halo(v, fast, after=None):
    count = lax.axis_size("blk")
    if not fast:
        right = lax.ppermute(v, "blk", [(i + 1, i) for i in range(count - 1)])
        return right, lax.ppermute(v, "blk", [(i, i + 1) for i in range(count - 1)])
    near = swap(v, "blk", 1)
    if after is not None:
        near, _ = lax.optimization_barrier((near, after))
    return near, lax.ppermute(near, "blk", halo_hops())


def halo_hops():
    count = lax.axis_size("blk")
    return [(i, i + 2) for i in range(0, count - 2, 2)] + [(i + 2, i) for i in range(1, count - 2, 2)]


def halo_flip(fast):
    return lax.axis_index("blk") % 2 if fast else jnp.int32(0)


def place_table(width):
    quarter = width // 4
    frequency = 1.0 / 10000.0 ** (jnp.arange(quarter, dtype=F32) / quarter)
    angle = jnp.arange(BIG_SIDE, dtype=F32)[:, None] * frequency[None, :]
    return jnp.concatenate([jnp.sin(angle), jnp.cos(angle)], axis=1)


def put_slices(pieces, at, total):
    out = []
    for piece, whole in zip(pieces, total):
        out.append(
            lax.dynamic_update_slice_in_dim(
                jnp.zeros((whole,), F32), piece.astype(F32), at * piece.shape[0], 0
            )
        )
    return jnp.concatenate(out)


def per_device(
    tokens,
    condition,
    cotangent,
    segments,
    kept_patch,
    res_class,
    pack_order,
    ada_weight,
    ada_bias,
    qkv_weight,
    query_bias,
    value_bias,
    proj_weight,
    proj_bias,
    hidden_weight,
    hidden_bias,
    output_weight,
    output_bias,
):
    tokens_dev, width = tokens.shape[1], tokens.shape[2]
    segs = condition.shape[1]
    size_dp, size_blk = lax.axis_size("dp"), lax.axis_size("blk")
    own_dp, own_blk = lax.axis_index("dp"), lax.axis_index("blk")
    own_dev = own_dp * size_blk + own_blk
    count = size_dp * size_blk
    rows = width // count
    barrier = lax.optimization_barrier
    fast = size_dp == 4 and size_blk == 8 and rows % 4 == 0
    everyone = ("dp", "blk")
    blocks = tokens_dev // BLOCK

    first = jnp.concatenate(
        [qkv_weight[:, g * width : (g + 1) * width] for g in range(3)] + [proj_weight], axis=0
    )
    second = jnp.concatenate(
        [hidden_weight[:, g * width : (g + 1) * width] for g in range(4)] + [output_weight], axis=0
    )
    x, z = own_blk % 2, own_blk // 2
    core, y = own_dp % 2, own_dp // 2
    image_ids = jnp.arange(segs, dtype=jnp.int32)
    pick_image = pack_order[0][:, None] == image_ids[None, :]
    seg_cond = jnp.dot(pick_image.astype(BF), condition[0], preferred_element_type=F32)
    seg_big = jnp.sum(jnp.where(pick_image, res_class[0][None, :], 0), axis=1)
    seg_len = jnp.where(seg_big == 1, BIG_LEN, SMALL_LEN).astype(jnp.int32)
    earlier = image_ids[None, :] < image_ids[:, None]
    seg_start = jnp.sum(jnp.where(earlier, seg_len[None, :], 0), axis=1)
    window_start = (own_blk - 1) * tokens_dev
    block_pos = window_start + BLOCK * jnp.arange(3 * blocks, dtype=jnp.int32)
    block_seg = jnp.sum((seg_start[None, :] <= block_pos[:, None]).astype(jnp.int32), axis=1) - 1
    block_seg = jnp.clip(block_seg, 0, segs - 1)
    block_pick = block_seg[:, None] == image_ids[None, :]
    block_big = jnp.sum(jnp.where(block_pick, seg_big[None, :], 0), axis=1)
    block_start = jnp.sum(jnp.where(block_pick, seg_start[None, :], 0), axis=1) - window_start
    inside = (block_pos >= 0) & (block_pos < size_blk * tokens_dev)
    block_id = jnp.where(inside, block_seg, -1)
    block_start = jnp.clip(block_start, 0, 3 * tokens_dev - BLOCK)
    own_pick = block_pick[blocks : 2 * blocks].astype(F32)

    silu_cond, silu_pull = jax.vjp(jax.nn.silu, seg_cond)
    silu_low = silu_cond.astype(BF)
    if fast:
        silu_all = dp_gather(silu_low).reshape(4 * segs, width)
    else:
        silu_all = lax.all_gather(silu_low, "dp", axis=0, tiled=True)
    silu_own = lax.dynamic_slice_in_dim(silu_all.T, own_dev * rows, rows, axis=0)
    partial_mod = dot_tn(silu_own, ada_weight).reshape(size_dp, segs, 6 * width)
    bias_rows = put_slices(
        (query_bias, value_bias, proj_bias, hidden_bias, output_bias, ada_bias),
        own_dev,
        (width, width, width, 4 * width, width, 6 * width),
    )
    bias_rows = jnp.pad(bias_rows, (0, 24 * width - bias_rows.shape[0])).reshape(1, 4, 6 * width)
    partial_mod = jnp.concatenate(
        [partial_mod, jnp.broadcast_to(bias_rows, (size_dp, 4, 6 * width))], axis=1
    )
    if fast:
        by_core = partial_mod.reshape(2, 2, segs + 4, 6 * width)
        sent = lax.dynamic_index_in_dim(by_core, 1 - core, 1, keepdims=False)
        kept = lax.dynamic_index_in_dim(by_core, core, 1, keepdims=False)
        kept = kept + swap(sent, "dp", 1)
        sent = lax.dynamic_index_in_dim(kept, 1 - y, 0, keepdims=False).astype(BF)
        kept = lax.dynamic_index_in_dim(kept, y, 0, keepdims=False)
        row_mod = kept + swap(sent, "dp", 2).astype(F32)
        for bit in (1, 2, 4):
            low = row_mod.astype(BF)
            row_mod = low.astype(F32) + swap(low, "blk", bit).astype(F32)
    else:
        row_mod = lax.psum_scatter(partial_mod, "dp", scatter_dimension=0, tiled=True)[0]
        row_mod = lax.psum(row_mod, "blk")
    if fast:
        core_only = core.reshape(1).astype(jnp.int32)
        first_line = gather_line(first, z)
        first_line, second_shard = barrier((first_line, second[: 4 * rows]))
        first_halves = gather_cross(first_line, x, y)
        second_pair = pair_up(second_shard, "blk", z // 2, 4)
        first_halves, second_pair = barrier((first_halves, second_pair))
        first_halves = gather_wide(*first_halves, x, y)
        second_line = pair_up(second_pair, "blk", z % 2, 2).reshape(4, 4 * rows, width)
    else:
        first_all = lax.all_gather(first, everyone, axis=0, tiled=True)
        second_all = lax.all_gather(second, everyone, axis=0, tiled=True)
        groups = first_all.reshape(count, 4, rows, width).transpose(1, 0, 2, 3)
        groups = groups.reshape(4, width, width)
        full_qkv = jnp.concatenate([groups[0], groups[1], groups[2]], axis=1)
        full_proj = groups[3]
        pair = second_all.reshape(count, 8 * rows, width)
        hid = pair[:, : 4 * rows].reshape(count, 4, rows, width).transpose(0, 2, 1, 3)
        full_hidden = hid.reshape(width, 4 * width)
        full_output = pair[:, 4 * rows :].reshape(4 * width, width)
    bias_flat = row_mod[segs:].reshape(-1)
    full_query_bias = bias_flat[:width]
    full_value_bias = bias_flat[width : 2 * width]
    full_proj_bias = bias_flat[2 * width : 3 * width]
    full_hidden_bias = bias_flat[3 * width : 7 * width]
    full_output_bias = bias_flat[7 * width : 8 * width]
    modulation = row_mod[:segs] + bias_flat[8 * width : 14 * width][None, :]
    block_pick = jnp.pad(block_pick.astype(F32), ((0, 16 - 3 * blocks), (0, 0)))
    mods = jnp.dot(block_pick, modulation, precision=HIGHEST)
    own_mods = mods[blocks : blocks + 8]

    big = jnp.broadcast_to(block_big[:, None], (3 * blocks, BLOCK)).reshape(-1) == 1
    flip = halo_flip(fast)
    kept_near, kept_far = halo(kept_patch[0], fast)
    kept_all = jnp.concatenate(
        [
            jnp.where(flip == 0, kept_far, kept_near),
            kept_patch[0],
            jnp.where(flip == 0, kept_near, kept_far),
        ]
    )
    row_pos = jnp.where(big, kept_all // BIG_SIDE, kept_all // SMALL_SIDE)
    col_pos = kept_all - row_pos * jnp.where(big, BIG_SIDE, SMALL_SIDE)
    places = jnp.concatenate(
        [col_pos[None], row_pos[None], jnp.zeros((6, 3 * tokens_dev), jnp.int32)], axis=0
    )
    own_tokens, _ = barrier((tokens[0], kept_near))
    tokens_near, tokens_far = halo(own_tokens, fast, second_pair if fast else None)
    core = core if fast else jnp.int32(0)
    core_arg = jnp.stack([core, flip]).astype(jnp.int32)
    attn_in_all, hidden, attn_in_keep, attn_in_send = attention_input(
        core_arg, (tokens_near, tokens[0], tokens_far), places, place_table(width), mods
    )

    if fast:
        attn_in_all, first_halves, second_line, third_shard = barrier(
            (attn_in_all, first_halves, second_line, second[4 * rows :])
        )
        first_parts = both_cores(*first_halves)
        second_halves = gather_cross(second_line, x, y)
        third_pair = pair_up(third_shard, "blk", z // 2, 4)
        first_parts, second_halves, third_pair = barrier((first_parts, second_halves, third_pair))
        second_halves = gather_wide(*second_halves, x, y)
        third_line = pair_up(third_pair, "blk", z % 2, 2).reshape(4, 4 * rows, width)
        full_qkv, full_proj = unpack_weight(
            core_only,
            first_parts,
            rows,
            [(0, 0), (0, 1), (0, 2), (1, 0)],
            "unpack_first",
        )
    queries = (dot_nn(attn_in_all, full_qkv[:, :width]) + full_query_bias).astype(BF)
    keys = dot_nn(attn_in_all, full_qkv[:, width : 2 * width]).astype(BF)
    values = (dot_nn(attn_in_all, full_qkv[:, 2 * width :]) + full_value_bias).astype(BF)
    own = slice(tokens_dev, 2 * tokens_dev)
    forward_info = jnp.concatenate(
        [block_start[blocks : 2 * blocks], block_big[blocks : 2 * blocks]]
    ).astype(jnp.int32)
    left_id, own_id, right_id = jnp.split(block_id, 3)
    backward_info = jnp.concatenate(
        [
            jnp.where(flip == 0, right_id, left_id),
            own_id,
            jnp.where(flip == 0, left_id, right_id),
            flip[None],
        ]
    ).astype(jnp.int32)
    if fast:
        queries, second_halves, third_line = barrier((queries, second_halves, third_line))
        second_parts = both_cores(*second_halves)
        third_halves = gather_cross(third_line, x, y)
    attn_low, lse = attend_forward(forward_info, queries, keys, values, HEADS)

    def eight(v):
        return jnp.broadcast_to(v[None, :], (8, v.shape[0]))

    if fast:
        attn_low, second_parts, third_halves = barrier((attn_low, second_parts, third_halves))
        third_halves = gather_wide(*third_halves, x, y)
    branch, after_attn, mlp_in, mlp_keep, low_keep, mlp_low_send = after_attention(
        core_arg, attn_low, full_proj, eight(full_proj_bias), hidden, own_mods
    )
    if fast:
        (full_hidden,) = unpack_weight(
            core_only,
            second_parts,
            rows,
            [(0, 0), (0, 1), (0, 2), (0, 3)],
            "unpack_hidden",
        )
        attn_in_send, mlp_low_send, ada_rows = barrier((attn_in_send, mlp_low_send, ada_weight))
        attn_in_oth, mlp_low_oth = swap(attn_in_send, "dp", 1), swap(mlp_low_send, "dp", 1)
        mlp_in, attn_in_oth, mlp_low_oth = lax.optimization_barrier(
            (mlp_in, attn_in_oth, mlp_low_oth)
        )
    order = jnp.stack([1 - core, 3 - core, core, 2 + core]).astype(jnp.int32)
    act_keep, act_send, slope = feed_forward_up(order, mlp_in, full_hidden, eight(full_hidden_bias))
    if fast:
        act_keep, third_halves = barrier((act_keep, third_halves))
        full_output = unpack_rows(core_only, both_cores(*third_halves), 4 * rows, "unpack_output")
        full_output, ada_rows = barrier((full_output, ada_rows))
        ada_rows = pair_up(ada_rows[None], "dp", core, 1)
    act_and_lower, block_out, lower_sums = feed_forward_down(
        order,
        act_keep,
        act_send,
        full_output,
        eight(full_output_bias),
        after_attn,
        cotangent[0],
        own_mods,
    )

    shape = (tokens_dev, width)
    orders = ["yxz", "xyz"]
    if fast:
        act_and_lower, ada_pair = barrier((act_and_lower, ada_rows))
        act_and_lower_oth = swap(act_and_lower, "dp", 1)
    grad_upper, grad_after, grad_attn, upper_sums, branch_sums = feed_forward_back(
        act_and_lower,
        slope,
        full_hidden,
        full_output,
        full_proj,
        after_attn,
        branch,
        attn_low,
        lse,
        cotangent[0],
        own_mods,
        HEADS,
    )

    def to_segments(sums):
        return lax.dot_general(
            own_pick, sums[:blocks], (((0,), (0,)), ((), ())), precision=HIGHEST
        )

    def early_message():
        bias = jnp.concatenate(
            [
                branch_sums[blocks, :width],
                upper_sums[0],
                lower_sums[blocks],
                jnp.zeros((2 * width,), F32),
            ]
        )
        return jnp.concatenate(
            [
                to_segments(jnp.concatenate([branch_sums, lower_sums], axis=1)),
                bias.reshape(2, 4 * width),
            ],
            axis=0,
        )

    def late_message(sums):
        return jnp.concatenate([to_segments(sums), sums[blocks : blocks + 1]], axis=0)

    if not fast:
        grad_near, grad_far = halo(grad_attn, fast)
    else:

        def half_1(group):
            return split_by(group[0], y), split_by(group[1], x)

        def step_1(halves):
            return send(halves[0], "dp", 2), send(halves[1], "blk", 1)

        def half_2(got):
            return split_by(joined(got[0]), x), split_by(joined(got[1]), y)

        def step_2(halves):
            return send(halves[0], "blk", 1), send(halves[1], "dp", 2)

        def half_3(got):
            return split_by(side_by_side(joined(got[0]), joined(got[1])), z % 2)

        def step_3(halves):
            return send(halves, "blk", 2)

        def half_4(got):
            return split_by(joined(got), z // 2)

        def step_4(halves):
            return send(halves, "blk", 4)

        early = early_message()
        act_keep, grad_upper, grad_attn, early, act_and_lower_oth, ada_pair = barrier(
            (act_keep, grad_upper, grad_attn, early, act_and_lower_oth, ada_pair)
        )
        ada_got = swap(ada_pair, "dp", 2)
        grad_upper_oth = swap(grad_upper, "dp", 1)
        early_got = swap_exact(early, 1, 2)
        grad_near = swap(grad_attn, "blk", 1)
        third = chip_grads(
            [(act_keep, act_and_lower_oth)],
            [(act_and_lower, act_and_lower_oth, 2, 0)],
            [(0, 0, 4 * rows, [(0, 2 * rows, 0, 0), (2 * rows, 2 * rows, 1, 0)])],
            orders,
            False,
            shape,
            "grad_output_weight",
        )

        mlp_keep, third, grad_upper_oth, early, early_got = barrier(
            (mlp_keep, half_1(third), grad_upper_oth, early, early_got)
        )
        third = step_1(third)
        early = early + early_got
        early_got = swap_exact(early, 2, 2)
        second = chip_grads(
            [(mlp_keep, mlp_low_oth)],
            [(grad_upper, grad_upper_oth, 0, g) for g in range(4)],
            [(0, g, rows, [(0, rows, g // 2, g % 2 * rows)]) for g in range(4)],
            orders,
            True,
            shape,
            "grad_hidden_weight",
        )

        grad_attn, second, grad_near, early, early_got = barrier(
            (grad_attn, half_1(second), grad_near, early, early_got)
        )
        grad_far = lax.ppermute(grad_near, "blk", halo_hops())
        early = early + early_got
        early_got = swap_exact(early, 4, 2)
    grad_q, grad_k_own, grad_v_own = attend_backward_own(
        forward_info, queries, keys, values, grad_attn, HEADS
    )
    if fast:
        grad_q, third, grad_far, early, early_got, ada_got = barrier(
            (grad_q, third, grad_far, early, early_got, ada_got)
        )
        grad_q_oth = swap(grad_q, "dp", 1)
        second = step_1(second)
        third = step_2(half_2(third))

        attn_in_keep, grad_q_oth = barrier((attn_in_keep, grad_q_oth))
        early_row = early + early_got
        early_pair = pair_up(early_row[None], "dp", core, 1)
        first = chip_grads(
            [(attn_in_keep, attn_in_oth), (low_keep, mlp_low_oth[width // 2 :])],
            [(grad_q, grad_q_oth, 0, 0), (grad_upper, grad_upper_oth, 0, 4)],
            [(0, 0, rows, [(0, rows, 0, 0)]), (1, 1, rows, [(0, rows, 1, 0)])],
            orders,
            True,
            shape,
            "grad_query_weight",
        )

        grad_near, first, early_pair = barrier((grad_near, half_1(first), early_pair))
        early_all = pair_up(early_pair, "dp", y, 2)
    grad_kv = attend_backward_other(
        backward_info,
        queries,
        keys,
        values,
        grad_near,
        grad_far,
        grad_k_own,
        grad_v_own,
        HEADS,
    )
    if fast:
        grad_kv, hidden, second, third, first, early_all = barrier(
            (grad_kv, hidden, second, third, first, early_all)
        )
        grad_kv_oth = swap(grad_kv, "dp", 1)
        first = step_1(first)
        third = step_3(half_3(third))
    grad_tokens, input_sums = input_gradient(
        (grad_q, grad_kv), full_qkv, hidden, grad_after, own_mods
    )
    if fast:
        late = late_message(input_sums)
        attn_in_keep, grad_kv_oth, third, first, late = barrier(
            (attn_in_keep, grad_kv_oth, third, first, late)
        )
        second = step_2(half_2(second))
        third = step_4(half_4(third))
        late_got = swap_exact(late, 1, 1)
        last = chip_grads(
            [(attn_in_keep, attn_in_oth)],
            [(grad_kv, grad_kv_oth, 0, 0), (grad_kv, grad_kv_oth, 0, 1)],
            [(0, 0, rows, [(0, rows, 0, 0)]), (0, 1, rows, [(0, rows, 1, 0)])],
            orders,
            True,
            shape,
            "grad_key_weight",
        )

        last, second, late, late_got = barrier((half_1(last), second, late, late_got))
        last = step_1(last)
        second = step_3(half_3(second))
        late = late + late_got
        late_got = swap_exact(late, 2, 1)

        last, second, third, late, late_got = barrier((last, second, third, late, late_got))
        third_sum = add(*third)
        first = step_2(half_2(first))
        second = step_4(half_4(second))
        late = late + late_got
        late_got = swap_exact(late, 4, 1)

        last, first, second, late, late_got = barrier((last, first, second, late, late_got))
        second_sum = add(*second)
        last = step_2(half_2(last))
        first = step_3(half_3(first))
        late_row = late + late_got
        ada_rows = jnp.concatenate(
            [jnp.where(y == 0, ada_pair, ada_got), jnp.where(y == 0, ada_got, ada_pair)], axis=0
        ).reshape(4 * rows, 6 * width)
        own_row = jnp.concatenate([late_row[:segs], early_row[:segs]], axis=1)
        row_high = lax.reduce_precision(own_row, 8, 7)
        row_rest = (own_row - row_high).astype(BF)
        part = dot_nt(ada_rows, row_high.astype(BF)) + dot_nt(ada_rows, row_rest)
        part = pair_up(part[None], "blk", z // 2, 4)
        late_pair = pair_up(late_row[None], "dp", core, 1)

        last, first, part, late_pair = barrier((last, first, part, late_pair))
        last = step_3(half_3(last))
        first = step_4(half_4(first))
        part = pair_up(part[None], "blk", z % 2, 2)
        late_all = pair_up(late_pair, "dp", y, 2)

        last, first, part, late_all = barrier((last, first, part, late_all))
        first_sum = add(*first)
        last = step_4(half_4(last))
        part = pair_up(part[None], "blk", x, 1)
        last_sum = add(*last)

    if not fast:
        early_row, late_row = (
            lax.psum(v, "blk") for v in (early_message(), late_message(input_sums))
        )
        early_all, late_all = (
            lax.all_gather(v, "dp", axis=0, tiled=False) for v in (early_row, late_row)
        )
    mod_all = jnp.concatenate([late_all[:, :segs], early_all[:, :segs]], axis=2)
    mod_all = mod_all.reshape(-1, 6 * width)
    early_bias = jnp.sum(early_all[:, segs:], axis=0).reshape(-1)
    late_bias = jnp.sum(late_all[:, segs:], axis=0).reshape(-1)

    def take(v, n):
        return lax.dynamic_slice_in_dim(v, own_dev * n, n)

    grad_query_bias = take(late_bias[:width], rows)
    grad_value_bias = take(late_bias[width:], rows)
    grad_proj_bias = take(early_bias[:width], rows)
    grad_hidden_bias = take(early_bias[width : 5 * width], 4 * rows)
    grad_output_bias = take(early_bias[5 * width : 6 * width], rows)
    grad_ada_bias = take(jnp.sum(mod_all, axis=0), 6 * rows)
    mod_high = mod_all.astype(BF)
    mod_rest = (mod_all - mod_high.astype(F32)).astype(BF)
    grad_ada_weight = dot_nn(silu_own, mod_high) + dot_nn(silu_own, mod_rest)
    if fast:
        part = part.reshape(2, 2, 2, 4, rows, segs).transpose(5, 3, 2, 1, 0, 4)
        own_silu = part.reshape(segs, width)
    else:
        silu_grad = dot_nt(ada_weight, mod_high) + dot_nt(ada_weight, mod_rest)
        silu_rows = lax.all_gather(silu_grad, everyone, axis=0, tiled=True)
        own_silu = lax.dynamic_slice_in_dim(silu_rows, own_dp * segs, segs, axis=1).T
    grad_seg_cond = silu_pull(own_silu)[0]
    grad_image = lax.dot_general(
        pick_image.astype(F32), grad_seg_cond, (((0,), (0,)), ((), ())), precision=HIGHEST
    )

    if fast:
        grad_qkv_weight = jnp.concatenate(
            [first_sum[:rows], last_sum[:rows], last_sum[rows:]], axis=1
        )
        grad_proj_weight = first_sum[rows:]
        grad_hidden_weight = jnp.concatenate(
            [second_sum[g * rows : (g + 1) * rows] for g in range(4)], axis=1
        )
        grad_output_weight = third_sum
    else:

        def scattered(left_t, right):
            product = dot_nn(left_t, right).astype(BF)
            product = lax.psum_scatter(product, "dp", scatter_dimension=0, tiled=True)
            return lax.psum_scatter(product, "blk", scatter_dimension=0, tiled=True).astype(F32)

        def in_order(keep, send):
            both = jnp.stack([keep.reshape(2, -1, tokens_dev), send.reshape(2, -1, tokens_dev)], axis=1)
            return both.reshape(-1, tokens_dev)

        attn_in_t = in_order(attn_in_keep, attn_in_send)
        mlp_send, low_send = mlp_low_send[: width // 2], mlp_low_send[width // 2 :]
        grad_qkv_weight = scattered(attn_in_t, jnp.concatenate([grad_q, grad_kv], axis=1))
        grad_proj_weight = scattered(in_order(low_keep, low_send), grad_upper[:, 4 * width :])
        grad_hidden_weight = scattered(in_order(mlp_keep, mlp_send), grad_upper[:, : 4 * width])
        act_send = act_and_lower[: 2 * tokens_dev]
        grad_lower = act_and_lower[2 * tokens_dev :]
        act = jnp.stack(
            [act_keep.reshape(2, tokens_dev, width), act_send.reshape(2, tokens_dev, width)], axis=1
        ).reshape(4, tokens_dev, width)
        act_t = act.transpose(0, 2, 1).reshape(4 * width, tokens_dev)
        grad_output_weight = scattered(act_t, grad_lower)
    return (
        block_out[None],
        grad_tokens[None],
        grad_image[None],
        grad_ada_weight,
        grad_ada_bias,
        grad_qkv_weight,
        grad_query_bias,
        grad_value_bias,
        grad_proj_weight,
        grad_proj_bias,
        grad_hidden_weight,
        grad_hidden_bias,
        grad_output_weight,
        grad_output_bias,
    )


def solution(mesh):
    row = P("dp", "blk", None)
    ints = P("dp", "blk")
    image = P("dp", None)
    matrix = P(("dp", "blk"), None)
    vector = P(("dp", "blk"))
    return jax.shard_map(
        per_device,
        mesh=mesh,
        in_specs=(
            row,
            P("dp", None, None),
            row,
            ints,
            ints,
            image,
            image,
            matrix,
            vector,
            matrix,
            vector,
            vector,
            matrix,
            vector,
            matrix,
            vector,
            matrix,
            vector,
        ),
        out_specs=(
            row,
            row,
            P("dp", None, None),
            matrix,
            vector,
            matrix,
            vector,
            vector,
            matrix,
            vector,
            matrix,
            vector,
            matrix,
            vector,
        ),
        check_vma=False,
    )
```

time: 2250 us -> 626 us (0.28)
  waiting for transfers between devices: 1240 us -> 141 us
  blocking collectives: 346 us -> 0 us
  matrix products: 359 us -> 31 us
  Pallas kernels: 0 us -> 213 us
  starting transfers between devices: 21.1 us -> 106 us
  local copies, waits for them, and re-layouts: 142 us -> 59.6 us
  other arithmetic: 103 us -> 63.4 us
    ppermute x44 -> x82, waiting for transfers between devices: 696 us -> 141 us  [the longest x79 107 us: swap(): return lax.ppermute(v, axis, [(i, i ^ bit) for i in range(count)])]
    dot_general x77 -> x13, matrix products: 359 us -> 31 us  [the longest x5 21.8 us: dot_nn(): lax.dot_general(a, b, (((1,), (0,)), ((), ())), preferred_element_type=F32)]
    unnamed x4 -> x0, blocking collectives: 318 us -> none
    reduce_scatter x6 -> x0, waiting for transfers between devices: 292 us -> none  [the longest x1 124 us: per_device(): lax.psum_scatter(grad_ada_weight.astype(jnp.bfloat16), 'dp', scatter_dime...]
    all_gather x5 -> x0, waiting for transfers between devices: 244 us -> none  [the longest x1 106 us: per_device(): lax.all_gather(ada_weight, ('dp', 'blk'), axis=0, tiled=True)]
    pallas_call x0 -> x16, Pallas kernels: none -> 213 us  [the longest x4 38.8 us: chip_grads(): pl.pallas_call(body, grid=(2,), in_specs=left_specs * 2 + right_specs * 2...]
    ppermute x44 -> x82, starting transfers between devices: 2.58 us -> 106 us  [the longest x79 91.4 us: swap(): return lax.ppermute(v, axis, [(i, i ^ bit) for i in range(count)])]
    unnamed x174 -> x145, local copies, waits for them, and re-layouts: 81.3 us -> 6.16 us
  transfers between devices with their start and end apart: 62 -> 82, of which waited for: 51 -> 25; matrix products, arithmetic and copies ran while one was open for 33% -> 22% of each run, Pallas kernels for 0% -> 33%
where the time goes in v1:
time: 626 us; the launch traced here: 618 us
  Pallas kernels  213 us (34%)
  waiting for transfers between devices  141 us (23%)
  starting transfers between devices  106 us (17%)
  other arithmetic  63.4 us (10%)
  local copies, waits for them, and re-layouts  59.6 us (10%)
  matrix products  31 us (5%)
    ppermute x79, waiting for transfers between devices, swap(): return lax.ppermute(v, axis, [(i, i ^ bit) for i in range(count)])  107 us
    ppermute x79, starting transfers between devices, swap(): return lax.ppermute(v, axis, [(i, i ^ bit) for i in range(count)])  91.4 us
    pallas_call x4, Pallas kernels, chip_grads(): pl.pallas_call(body, grid=(2,), in_specs=left_specs * 2 + right_specs * 2...  38.8 us
    pallas_call x1, Pallas kernels, feed_forward_back(): pl.pallas_call(body, grid=(4,), in_specs=[pl.BlockSpec((tokens, width), l...  25.2 us
    pallas_call x1, Pallas kernels, attend_backward_own(): pl.pallas_call(body, grid_spec=pltpu.PrefetchScalarGridSpec(num_scalar_pr...  23.7 us
    pallas_call x1, Pallas kernels, attend_backward_other(): pl.pallas_call(body, grid_spec=pltpu.PrefetchScalarGridSpec(num_scalar_pr...  22 us
    dot_general x5, matrix products, dot_nn(): lax.dot_general(a, b, (((1,), (0,)), ((), ())), preferred_element_type=F32)  21.8 us
    pallas_call x2, Pallas kernels, unpack_weight(): pl.pallas_call(body, grid_spec=pltpu.PrefetchScalarGridSpec(num_scalar_pr...  20.3 us
  transfers between devices with their start and end apart: 82, of which 25 were waited for; matrix products, arithmetic and copies ran while one was open for 22% of the time, Pallas kernels for 33%

profile of v1, /device:TPU:0, one launch (start us, length us, event | category | flops | bytes accessed | tf_op | source)
XLA Modules:
  0.0 617.5 jit_solution(9672402770541896653)
XLA Ops:
  1.5 3.0 collective-permute-start
  7.8 2.6 collective-permute-start.2
  17.9 3.5 collective-permute-start.8
  24.5 2.8 collective-permute-done.10
  31.7 3.4 collective-permute-start.3
  36.9 13.8 %collective-permute-done.3 = bf16[288,1152]{1,0:T(8,128)(2,1)S(1)} collective-permute-done((bf16[288,1152]{1,0:T(8,128)(2,1)S(1)}, bf16[288,1152]{1,0:T(8,128)(2,1)S(1)}, u32[]{:S(2)}, u32[]{:S(2)}) %collective-permute-start.3) | collective-permute-done | bytes 663584 | tf_op jit(solution)/shard_map/ppermute | solution.py:39
  53.1 3.3 collective-permute-start.6
  56.4 2.0 collective-permute-start.13
  58.5 12.4 %collective-permute-done.6 = bf16[144,1152]{1,0:T(8,128)(2,1)S(1)} collective-permute-done((bf16[144,1152]{1,0:T(8,128)(2,1)S(1)}, bf16[144,1152]{1,0:T(8,128)(2,1)S(1)}, u32[]{:S(2)}, u32[]{:S(2)}) %collective-permute-start.6) | collective-permute-done | bytes 331808 | tf_op jit(solution)/shard_map/ppermute | solution.py:39
  74.4 4.7 collective-permute-done.14
  79.1 3.4 collective-permute-start.15
  83.8 4.9 collective-permute-start.7
  97.6 5.1 collective-permute-done.18
  104.0 14.4 %collective-permute-done.7.far = bf16[384,1152]{1,0:T(8,128)(2,1)} collective-permute-done((bf16[384,1152]{1,0:T(8,128)(2,1)}, bf16[384,1152]{1,0:T(8,128)(2,1)}, u32[]{:S(2)}, u32[]{:S(2)}) %collective-permute-start.7) | collective-permute-done | bytes 884768 | tf_op jit(solution)/shard_map/ppermute | solution.py:918
  118.4 10.8 %attention_input.1 = (bf16[1152,1152]{1,0:T(8,128)(2,1)}, f32[384,1152]{1,0:T(8,128)}, bf16[576,384]{1,0:T(8,128)(2,1)}, bf16[576,384]{1,0:T(8,128)(2,1)}) custom-call(s32[2]{0:T(128)} %pad_add_fusion.1.core_ref, bf16[384,1152]{1,0:T(8,128)(2,1)} %collective-permute-done.1.near, bf16[384,1152]{1,0:T(8,128)(2,1)} %bitcast.7.own, ...), custom_call_target="tpu_custom_call" | custom-call | flops 11000000512 | bytes 1024 | tf_op jit(solution)/shard_map/attention_input/pallas_call | solution.py:562
  131.1 2.6 broadcast_select_fusion.5
  136.4 2.3 collective-permute-start.21
  140.2 12.1 %collective-permute-done.23 = bf16[144,1152]{1,0:T(8,128)(2,1)S(1)} collective-permute-done((bf16[144,1152]{1,0:T(8,128)(2,1)S(1)}, bf16[144,1152]{1,0:T(8,128)(2,1)S(1)}, u32[]{:S(2)}, u32[]{:S(2)}) %collective-permute-start.23) | collective-permute-done | bytes 331808 | tf_op jit(solution)/shard_map/ppermute | solution.py:39
  157.2 1.8 collective-permute-start.26
  159.0 9.9 %unpack_first.1 = (bf16[1152,3456]{1,0:T(8,128)(2,1)}, bf16[1152,1152]{1,0:T(8,128)(2,1)}) custom-call(s32[1]{0:T(128)} %bitcast.2.core_ref, bf16[1152,1152]{1,0:T(8,128)(2,1)} %copy-done.6, bf16[2,2,288,1152]{3,2,1,0:T(8,128)(2,1)} %bitcast.239, bf16[1152,1152]{1,0:T(8,128)(2,1)} %copy-done.56, bf16[2,2,288,1152]{3,2,1,0:T(8,128)(2,1)} %bitcast.276), custom_call_target="tpu_custom_call" | custom-call | flops 11000000512 | bytes 1024 | tf_op jit(solution)/shard_map/unpack_first/pallas_call | solution.py:118
  169.0 8.1 %fusion.q_ref.q_near.q_far = bf16[1152,1152]{1,0:T(8,128)(2,1)} fusion(bf16[1152,1152]{1,0:T(8,128)(2,1)} %get-tuple-element.212, f32[1152]{0:T(1024)S(1)} %get-tuple-element.604, bf16[1152,3456]{1,0:T(8,128)(2,1)} %get-tuple-element.221.w_ref), kind=kOutput, calls=%fused_computation.4 | convolution fusion | flops 3060301824 | bytes 7967232 | tf_op jit(solution)/shard_map/dot_general | solution.py:26
  177.1 5.2 fusion.1.v_ref
  182.3 5.2 convolution_convert_fusion.k_ref
  197.4 14.9 %attend_forward.1 = (bf16[384,1152]{1,0:T(8,128)(2,1)}, f32[384,128]{1,0:T(8,128)}) custom-call(s32[6]{0:T(128)} %pad_add_fusion.2.info_ref, bf16[1152,1152]{1,0:T(8,128)(2,1)} %fusion.q_ref.q_near.q_far, bf16[1152,1152]{1,0:T(8,128)(2,1)} %convolution_convert_fusion.k_ref, bf16[1152,1152]{1,0:T(8,128)(2,1)} %fusion.1.v_ref), custom_call_target="tpu_custom_call" | custom-call | flops 16499999744 | bytes 1024 | tf_op jit(solution)/shard_map/attend_forward/pallas_call | solution.py:327
  214.9 8.3 %after_attention.1 = (f32[384,1152]{1,0:T(8,128)}, f32[384,1152]{1,0:T(8,128)}, bf16[384,1152]{1,0:T(8,128)(2,1)}, bf16[576,384]{1,0:T(8,128)(2,1)}, bf16[576,38...) custom-call(s32[2]{0:T(128)} %pad_add_fusion.1.core_ref, bf16[384,1152]{1,0:T(8,128)(2,1)} %get-tuple-element.230.low, ...), custom_call_target="tpu_custom_call" | custom-call | flops 8800000000 | bytes 1024 | tf_op jit(solution)/shard_map/after_attention/pallas_call | solution.py:611
  225.0 10.4 %unpack_hidden.1.wh = bf16[1152,4608]{1,0:T(8,128)(2,1)} custom-call(s32[1]{0:T(128)} %bitcast.2.core_ref, bf16[1152,1152]{1,0:T(8,128)(2,1)} %pad_maximum_fusion.2.a_own, bf16[2,2,288,1152]{3,2,1,0:T(8,128)(2,1)} %bitcast.26.b_own, bf16[1152,1152]{1,0:T(8,128)(2,1)} %collective-permute-done.27.a_oth, bf16[2,2,288,1152]{3,2,1,0:T(8,128)(2,1)} %bitcast.27.b_oth), custom_call_target="tpu_custom_call" | custom-call | flops 11000000512 | bytes 1024 | tf_op jit(solution)/shard_map/unpack_hidden/pallas_call | solution.py:118
  236.1 12.8 %feed_forward_up.1 = (bf16[768,1152]{1,0:T(8,128)(2,1)}, bf16[1152,1152]{1,0:T(8,128)(2,1)}, bf16[384,4608]{1,0:T(8,128)(2,1)}) custom-call(s32[4]{0:T(128)} %pad_add_fusion.order_ref, bf16[384,1152]{1,0:T(8,128)(2,1)} %get-tuple-element.238.x, bf16[1152,4608]{1,0:T(8,128)(2,1)} %unpack_hidden.1.wh, f32[8,4608]{1,0:T(8,128)} %broadcast_in_dim.153.bh), custom_call_target="tpu_custom_call" | custom-call | flops 1100000000 | bytes 1024 | tf_op jit(solution)/shard_map/feed_forward_up/pallas_call | solution.py:655
  250.8 4.1 collective-permute-done.34
  258.2 1.8 slice.301.refs_3_
  260.0 5.2 collective-permute-done.35.a_oth
  265.8 9.8 %unpack_output.1.wo = bf16[4608,1152]{1,0:T(8,128)(2,1)} custom-call(s32[1]{0:T(128)} %bitcast.2.core_ref, bf16[1152,1152]{1,0:T(8,128)(2,1)} %pad_maximum_fusion.4.a_own, bf16[2,2,288,1152]{3,2,1,0:T(8,128)(2,1)} %bitcast.240, bf16[1152,1152]{1,0:T(8,128)(2,1)} %collective-permute-done.35.a_oth, bf16[2,2,288,1152]{3,2,1,0:T(8,128)(2,1)} %bitcast.29.b_oth), custom_call_target="tpu_custom_call" | custom-call | flops 11000000512 | bytes 1024 | tf_op jit(solution)/shard_map/unpack_output/pallas_call | solution.py:154
  276.3 12.8 %feed_forward_down.1 = (bf16[1152,1152]{1,0:T(8,128)(2,1)}, bf16[384,1152]{1,0:T(8,128)(2,1)}, f32[8,1152]{1,0:T(8,128)}) custom-call(s32[4]{0:T(128)} %pad_add_fusion.order_ref, bf16[768,1152]{1,0:T(8,128)(2,1)} %get-tuple-element.268.keep_ref.refs_0_, bf16[1152,1152]{1,0:T(8,128)(2,1)} %get-tuple-element.247.send_ref, ...), custom_call_target="tpu_custom_call", output_to_operand_aliasing={{0}: (2, {})} | custom-call | flops 13200000000 | bytes 1024 | tf_op jit(solution)/shard_map/feed_forward_down/pallas_call | solution.py:715
  290.6 25.2 %feed_forward_back.1 = (bf16[384,5760]{1,0:T(8,128)(2,1)}, f32[384,1152]{1,0:T(8,128)}, bf16[384,1280]{1,0:T(8,128)(2,1)}, f32[8,4608]{1,0:T(8,128)}, f32[8,3456]{1,0:T(8,128)}) custom-call(bf16[1152,1152]{1,0:T(8,128)(2,1)} %get-tuple-element.256.gl.refs_2_, bf16[384,4608]{1,0:T(8,128)(2,1)} %get-tuple-element.257.sl, bf16[1152,4608]{1,0:T(8,128)(2,1)} %unpack_hidden.1.wh, ...), custom_call_target="tpu_custom_call" | custom-call | flops 26400000000 | bytes 1024 | tf_op jit(solution)/shard_map/feed_forward_back/pallas_call | solution.py:824
  324.5 10.7 %grad_output_weight.1 = (bf16[1152,1152]{1,0:T(8,128)(2,1)}, bf16[1152,1152]{1,0:T(8,128)(2,1)}) custom-call(bf16[768,1152]{1,0:T(8,128)(2,1)} %get-tuple-element.268.keep_ref.refs_0_, bf16[1152,1152]{1,0:T(8,128)(2,1)} %collective-permute-done.38.refs_1_.refs_3_, bf16[1152,1152]{1,0:T(8,128)(2,1)} %get-tuple-element.256.gl.refs_2_, ...), custom_call_target="tpu_custom_call" | custom-call | flops 11000000512 | bytes 1024 | tf_op jit(solution)/shard_map/grad_output_weight/pallas_call | solution.py:222
  335.1 3.6 dynamic-slice_bitcast_fusion.6
  340.2 12.9 %grad_hidden_weight.1 = (bf16[1152,1152]{1,0:T(8,128)(2,1)}, bf16[1152,1152]{1,0:T(8,128)(2,1)}) custom-call(bf16[576,384]{1,0:T(8,128)(2,1)} %get-tuple-element.274.refs_0_, bf16[1152,384]{1,0:T(8,128)(2,1)} %collective-permute-done.32.refs_1_, bf16[384,5760]{1,0:T(8,128)(2,1)} %get-tuple-element.272.refs_2_.refs_3_.refs_4_.refs_5_, ...), custom_call_target="tpu_custom_call" | custom-call | flops 11000000512 | bytes 1024 | tf_op jit(solution)/shard_map/grad_hidden_weight/pallas_call | solution.py:222
  353.1 3.6 dynamic-slice_bitcast_fusion.2
  364.0 23.7 %attend_backward_own.1 = (bf16[384,1152]{1,0:T(8,128)(2,1)}, f32[384,1152]{1,0:T(8,128)}, f32[384,1152]{1,0:T(8,128)}) custom-call(s32[6]{0:T(128)} %pad_add_fusion.2.info_ref, bf16[1152,1152]{1,0:T(8,128)(2,1)} %fusion.q_ref.q_near.q_far, bf16[1152,1152]{1,0:T(8,128)(2,1)} %convolution_convert_fusion.k_ref, bf16[1152,1152]{1,0:T(8,128)(2,1)} %fusion.1.v_ref, ...), custom_call_target="tpu_custom_call" | custom-call | flops 26400000000 | bytes 1024 | tf_op jit(solution)/shard_map/attend_backward_own/pallas_call | solution.py:415
  387.7 6.8 %collective-permute-start.45 = (bf16[384,1280]{1,0:T(8,128)(2,1)}, bf16[384,1280]{1,0:T(8,128)(2,1)}, u32[]{:S(2)}, u32[]{:S(2)}) collective-permute-start(bf16[384,1280]{1,0:T(8,128)(2,1)} %collective-permute-done.41.gn), channel_id=1, source_target_pairs={{0,2},{2,4},{4,6},{3,1},{5,3},{7,5},{8,10},{10,12},{12,14},{11,9},... | collective-permute-start | bytes 2949128 | tf_op jit(solution)/shard_map/ppermute | solution.py:1281
  394.7 18.6 %collective-permute-done.45.gf = bf16[384,1280]{1,0:T(8,128)(2,1)} collective-permute-done((bf16[384,1280]{1,0:T(8,128)(2,1)}, bf16[384,1280]{1,0:T(8,128)(2,1)}, u32[]{:S(2)}, u32[]{:S(2)}) %collective-permute-start.45) | collective-permute-done | bytes 983072 | tf_op jit(solution)/shard_map/ppermute | solution.py:1281
  420.9 2.2 reshape.594
  426.0 2.5 collective-permute-start.53
  429.7 7.6 %grad_query_weight.1 = (bf16[576,1152]{1,0:T(8,128)(2,1)}, bf16[576,1152]{1,0:T(8,128)(2,1)}) custom-call(bf16[576,384]{1,0:T(8,128)(2,1)} %get-tuple-element.331.refs_0_, bf16[576,384]{1,0:T(8,128)(2,1)} %get-tuple-element.294.refs_1_, bf16[576,384]{1,0:T(8,128)(2,1)} %collective-permute-done.31.refs_2_.refs_1_, bf16[576,384]{1,0:T(8,128)(2,1)} %slice.301.refs_3_, ...), custom_call_target="tpu_custom_call" | custom-call | flops 11000000512 | bytes 1024 | tf_op jit(solution)/shard_map/grad_query_weight/pallas_call | solution.py:222
  437.3 2.6 dynamic-slice_bitcast_fusion.26
  441.6 22.0 %attend_backward_other.1.gkv.refs_2_.refs_3_ = bf16[384,2304]{1,0:T(8,128)(2,1)} custom-call(s32[10]{0:T(128)} %pad_add_fusion.3.info_ref, bf16[1152,1152]{1,0:T(8,128)(2,1)} %fusion.q_ref.q_near.q_far, bf16[1152,1152]{1,0:T(8,128)(2,1)} %fusion.q_ref.q_near.q_far, bf16[1152,1152]{1,0:T(8,128)(2,1)} %convolution_convert_fusion.k_ref, ...), custom_call_target="tpu_custom_call" | custom-call | flops 24199999488 | bytes 1024 | tf_op jit(solution)/shard_map/attend_backward_other/pallas_call | solution.py:472
  469.0 3.6 collective-permute-start.57
  472.5 9.0 %collective-permute-start.58 = (bf16[288,1152]{1,0:T(8,128)(2,1)}, bf16[288,1152]{1,0:T(8,128)(2,1)}, u32[]{:S(2)}, u32[]{:S(2)}) collective-permute-start(bf16[288,1152]{1,0:T(8,128)(2,1)} %get-tuple-element.329), channel_id=1, source_target_pairs={{0,1},{1,0},{2,3},{3,2},{4,5},{5,4},{6,7},{7,6},{8,9},{9,8},{10,11... | collective-permute-start | bytes 1990664 | tf_op jit(solution)/shard_map/ppermute | solution.py:39
  481.6 14.0 %input_gradient.1 = (f32[384,1152]{1,0:T(8,128)}, f32[8,2304]{1,0:T(8,128)}) custom-call(bf16[384,1152]{1,0:T(8,128)(2,1)} %get-tuple-element.291.refs_4_.gq, bf16[384,2304]{1,0:T(8,128)(2,1)} %attend_backward_other.1.gkv.refs_2_.refs_3_, bf16[1152,3456]{1,0:T(8,128)(2,1)} %get-tuple-element.221.w_ref, f32[384,1152]{1,0:T(8,128)} %get-tuple-element.319.hid, ...), custom_call_target="tpu_custom_call" | custom-call | flops 15399999488 | bytes 1024 | tf_op jit(solution)/shard_map/input_gradient/pallas_call | solution.py:895
  496.8 3.1 add_convert_fusion.1
  500.0 2.4 dynamic-slice_bitcast_fusion.12
  507.8 2.1 collective-permute-start.60
  509.9 7.5 %grad_key_weight.1 = (bf16[576,1152]{1,0:T(8,128)(2,1)}, bf16[576,1152]{1,0:T(8,128)(2,1)}) custom-call(bf16[576,384]{1,0:T(8,128)(2,1)} %get-tuple-element.331.refs_0_, bf16[576,384]{1,0:T(8,128)(2,1)} %collective-permute-done.31.refs_2_.refs_1_, bf16[384,2304]{1,0:T(8,128)(2,1)} %attend_backward_other.1.gkv.refs_2_.refs_3_, ...), custom_call_target="tpu_custom_call" | custom-call | flops 11000000512 | bytes 1024 | tf_op jit(solution)/shard_map/grad_key_weight/pallas_call | solution.py:222
  519.3 2.1 collective-permute-start.61
  527.5 2.1 collective-permute-start.62
  533.6 6.4 %collective-permute-done.66 = bf16[14,2304]{1,0:T(8,128)(2,1)S(1)} collective-permute-done((bf16[14,2304]{1,0:T(8,128)(2,1)S(1)}, bf16[14,2304]{1,0:T(8,128)(2,1)S(1)}, u32[]{:S(2)}, u32[]{:S(2)}) %collective-permute-start.66) | collective-permute-done | bytes 64544 | tf_op jit(solution)/shard_map/ppermute | solution.py:39
  541.1 4.3 collective-permute-done.62
  545.4 3.0 collective-permute-done.63
  548.4 5.2 collective-permute-done.64
  555.3 3.0 collective-permute-start.70
  559.2 11.0 %collective-permute-done.70 = bf16[14,2304]{1,0:T(8,128)(2,1)S(1)} collective-permute-done((bf16[14,2304]{1,0:T(8,128)(2,1)S(1)}, bf16[14,2304]{1,0:T(8,128)(2,1)S(1)}, u32[]{:S(2)}, u32[]{:S(2)}) %collective-permute-start.70) | collective-permute-done | bytes 64544 | tf_op jit(solution)/shard_map/ppermute | solution.py:39
  583.1 2.2 collective-permute-done.74
  594.3 6.9 %collective-permute-done.78 = f32[1,2,144,12]{2,3,1,0:T(8,128)S(1)} collective-permute-done((f32[1,2,144,12]{2,3,1,0:T(8,128)S(1)}, f32[1,2,144,12]{2,3,1,0:T(8,128)S(1)}, u32[]{:S(2)}, u32[]{:S(2)}) %collective-permute-start.78) | collective-permute-done | bytes 13856 | tf_op jit(solution)/shard_map/ppermute | solution.py:39
  604.6 2.2 convolution_add_fusion.2
  614.5 1.9 collective-permute-done.81
  (545 shorter events, 163.1 us)
Async XLA Ops:
  1.5 16.4 %collective-permute-start = (s32[384]{0:T(512)S(1)}, s32[384]{0:T(512)S(1)}, u32[]{:S(2)}, u32[]{:S(2)}) collective-permute-start(s32[384]{0:T(512)S(1)} %reduce.2), channel_id=1, source_target_pairs={{0,1},{1,0},{2,3},{3,2},{4,5},{5,4},{6,7},{7,6},{8,9},{9,8},{10,11... | collective-permute-start | bytes 4616 | tf_op jit(solution)/shard_map/ppermute | solution.py:39
  7.8 22.6 %collective-permute-start.2 = (bf16[144,1152]{1,0:T(8,128)(2,1)}, bf16[144,1152]{1,0:T(8,128)(2,1)}, u32[]{:S(2)}, u32[]{:S(2)}) collective-permute-start(bf16[144,1152]{1,0:T(8,128)(2,1)} %pad_maximum_fusion.31), channel_id=1, source_target_pairs={{0,4},{1,5},{2,6},{3,7},{4,0},{5,1},{6,2},{7,3},{8,12},{9,13},{10,... | collective-permute-start | bytes 995336 | tf_op jit(solution)/shard_map/ppermute | solution.py:39
  22.3 61.5 %collective-permute-start.1 = (bf16[384,1152]{1,0:T(8,128)(2,1)}, bf16[384,1152]{1,0:T(8,128)(2,1)}, u32[]{:S(2)}, u32[]{:S(2)}) collective-permute-start(bf16[384,1152]{1,0:T(8,128)(2,1)} %bitcast.7.own), channel_id=1, source_target_pairs={{0,1},{1,0},{2,3},{3,2},{4,5},{5,4},{6,7},{7,6},{8,9},{9,8},{10,11... | collective-permute-start | bytes 2654216 | tf_op jit(solution)/shard_map/ppermute | solution.py:39
  31.7 18.9 %collective-permute-start.3 = (bf16[288,1152]{1,0:T(8,128)(2,1)S(1)}, bf16[288,1152]{1,0:T(8,128)(2,1)S(1)}, u32[]{:S(2)}, u32[]{:S(2)}) collective-permute-start(bf16[288,1152]{1,0:T(8,128)(2,1)S(1)} %pad_maximum_fusion.24), channel_id=1, source_target_pairs={{0,2},{1,3},{2,0},{3,1},{4,6},{5,7},{6,4},{7,5},{8,10},{9,11},{10,... | collective-permute-start | bytes 1990664 | tf_op jit(solution)/shard_map/ppermute | solution.py:39
  35.3 21.1 %collective-permute-start.12 = (bf16[16,6912]{1,0:T(8,128)(2,1)S(1)}, bf16[16,6912]{1,0:T(8,128)(2,1)S(1)}, u32[]{:S(2)}, u32[]{:S(2)}) collective-permute-start(bf16[16,6912]{1,0:T(8,128)(2,1)S(1)} %fusion.17), channel_id=1, source_target_pairs={{0,16},{8,24},{16,0},{24,8},{1,17},{9,25},{17,1},{25,9},{2,18},{10... | collective-permute-start | bytes 663560 | tf_op jit(solution)/shard_map/ppermute | solution.py:39
  51.1 31.4 %collective-permute-start.4 = (bf16[288,1152]{1,0:T(8,128)(2,1)S(1)}, bf16[288,1152]{1,0:T(8,128)(2,1)S(1)}, u32[]{:S(2)}, u32[]{:S(2)}) collective-permute-start(bf16[288,1152]{1,0:T(8,128)(2,1)S(1)} %bitcast.252), channel_id=1, source_target_pairs={{0,1},{1,0},{2,3},{3,2},{4,5},{5,4},{6,7},{7,6},{8,9},{9,8},{10,11... | collective-permute-start | bytes 1990664 | tf_op jit(solution)/shard_map/ppermute | solution.py:39
  51.5 31.2 %collective-permute-start.5 = (bf16[288,1152]{1,0:T(8,128)(2,1)S(1)}, bf16[288,1152]{1,0:T(8,128)(2,1)S(1)}, u32[]{:S(2)}, u32[]{:S(2)}) collective-permute-start(bf16[288,1152]{1,0:T(8,128)(2,1)S(1)} %bitcast.251), channel_id=1, source_target_pairs={{0,16},{8,24},{16,0},{24,8},{1,17},{9,25},{17,1},{25,9},{2,18},{10... | collective-permute-start | bytes 1990664 | tf_op jit(solution)/shard_map/ppermute | solution.py:39
  53.1 17.8 %collective-permute-start.6 = (bf16[144,1152]{1,0:T(8,128)(2,1)S(1)}, bf16[144,1152]{1,0:T(8,128)(2,1)S(1)}, u32[]{:S(2)}, u32[]{:S(2)}) collective-permute-start(bf16[144,1152]{1,0:T(8,128)(2,1)S(1)} %pad_maximum_fusion.32), channel_id=1, source_target_pairs={{0,4},{1,5},{2,6},{3,7},{4,0},{5,1},{6,2},{7,3},{8,12},{9,13},{10,... | collective-permute-start | bytes 995336 | tf_op jit(solution)/shard_map/ppermute | solution.py:39
  56.4 16.2 %collective-permute-start.13 = (bf16[16,6912]{1,0:T(8,128)(2,1)S(1)}, bf16[16,6912]{1,0:T(8,128)(2,1)S(1)}, u32[]{:S(2)}, u32[]{:S(2)}) collective-permute-start(bf16[16,6912]{1,0:T(8,128)(2,1)S(1)} %fusion.13), channel_id=1, source_target_pairs={{0,1},{1,0},{2,3},{3,2},{4,5},{5,4},{6,7},{7,6},{8,9},{9,8},{10,11... | collective-permute-start | bytes 663560 | tf_op jit(solution)/shard_map/ppermute | solution.py:39
  79.1 11.5 %collective-permute-start.15 = (bf16[16,6912]{1,0:T(8,128)(2,1)S(1)}, bf16[16,6912]{1,0:T(8,128)(2,1)S(1)}, u32[]{:S(2)}, u32[]{:S(2)}) collective-permute-start(bf16[16,6912]{1,0:T(8,128)(2,1)S(1)} %add_convert_fusion.20), channel_id=1, source_target_pairs={{0,4},{1,5},{2,6},{3,7},{4,0},{5,1},{6,2},{7,3},{8,12},{9,13},{10,... | collective-permute-start | bytes 663560 | tf_op jit(solution)/shard_map/ppermute | solution.py:39
  83.2 19.5 %collective-permute-start.18 = (bf16[288,1152]{1,0:T(8,128)(2,1)S(1)}, bf16[288,1152]{1,0:T(8,128)(2,1)}, u32[]{:S(2)}, u32[]{:S(2)}) collective-permute-start(bf16[288,1152]{1,0:T(8,128)(2,1)S(1)} %pad_maximum_fusion.25), channel_id=1, source_target_pairs={{0,2},{1,3},{2,0},{3,1},{4,6},{5,7},{6,4},{7,5},{8,10},{9,11},{10,... | collective-permute-start | bytes 1990664 | tf_op jit(solution)/shard_map/ppermute | solution.py:39
  83.8 34.6 %collective-permute-start.7 = (bf16[384,1152]{1,0:T(8,128)(2,1)}, bf16[384,1152]{1,0:T(8,128)(2,1)}, u32[]{:S(2)}, u32[]{:S(2)}) collective-permute-start(bf16[384,1152]{1,0:T(8,128)(2,1)} %collective-permute-done.1.near), channel_id=1, source_target_pairs={{0,2},{2,4},{4,6},{3,1},{5,3},{7,5},{8,10},{10,12},{12,14},{11,9},... | collective-permute-start | bytes 2654216 | tf_op jit(solution)/shard_map/ppermute | solution.py:918
  88.6 40.6 %collective-permute-start.16 = (bf16[576,1152]{1,0:T(8,128)(2,1)S(1)}, bf16[576,1152]{1,0:T(8,128)(2,1)}, u32[]{:S(2)}, u32[]{:S(2)}) collective-permute-start(bf16[576,1152]{1,0:T(8,128)(2,1)S(1)} %get-tuple-element.210), channel_id=1, source_target_pairs={{0,16},{8,24},{16,0},{24,8},{1,17},{9,25},{17,1},{25,9},{2,18},{10... | collective-permute-start | bytes 3981320 | tf_op jit(solution)/shard_map/ppermute | solution.py:39
  90.2 40.8 %collective-permute-start.17 = (bf16[576,1152]{1,0:T(8,128)(2,1)S(1)}, bf16[576,1152]{1,0:T(8,128)(2,1)}, u32[]{:S(2)}, u32[]{:S(2)}) collective-permute-start(bf16[576,1152]{1,0:T(8,128)(2,1)S(1)} %get-tuple-element.211), channel_id=1, source_target_pairs={{0,1},{1,0},{2,3},{3,2},{4,5},{5,4},{6,7},{7,6},{8,9},{9,8},{10,11... | collective-permute-start | bytes 3981320 | tf_op jit(solution)/shard_map/ppermute | solution.py:39
  133.9 21.0 %collective-permute-start.19 = (bf16[1152,1152]{1,0:T(8,128)(2,1)S(1)}, bf16[1152,1152]{1,0:T(8,128)(2,1)S(1)}, u32[]{:S(2)}, u32[]{:S(2)}) collective-permute-start(bf16[1152,1152]{1,0:T(8,128)(2,1)S(1)} %pad_maximum_fusion.a_own), channel_id=1, source_target_pairs={{0,8},{8,0},{16,24},{24,16},{1,9},{9,1},{17,25},{25,17},{2,10},{10... | collective-permute-start | bytes 7962632 | tf_op jit(solution)/shard_map/ppermute | solution.py:39
  134.0 20.9 %collective-permute-start.20 = (bf16[1152,1152]{1,0:T(8,128)(2,1)S(1)}, bf16[1152,1152]{1,0:T(8,128)(2,1)S(1)}, u32[]{:S(2)}, u32[]{:S(2)}) collective-permute-start(bf16[1152,1152]{1,0:T(8,128)(2,1)S(1)} %pad_maximum_fusion.1), channel_id=1, source_target_pairs={{0,8},{8,0},{16,24},{24,16},{1,9},{9,1},{17,25},{25,17},{2,10},{10... | collective-permute-start | bytes 7962632 | tf_op jit(solution)/shard_map/ppermute | solution.py:39
  134.7 17.6 %collective-permute-start.23 = (bf16[144,1152]{1,0:T(8,128)(2,1)S(1)}, bf16[144,1152]{1,0:T(8,128)(2,1)S(1)}, u32[]{:S(2)}, u32[]{:S(2)}) collective-permute-start(bf16[144,1152]{1,0:T(8,128)(2,1)S(1)} %copy-done.37), channel_id=1, source_target_pairs={{0,4},{1,5},{2,6},{3,7},{4,0},{5,1},{6,2},{7,3},{8,12},{9,13},{10,... | collective-permute-start | bytes 995336 | tf_op jit(solution)/shard_map/ppermute | solution.py:39
  136.4 16.8 %collective-permute-start.21 = (bf16[288,1152]{1,0:T(8,128)(2,1)S(1)}, bf16[288,1152]{1,0:T(8,128)(2,1)S(1)}, u32[]{:S(2)}, u32[]{:S(2)}) collective-permute-start(bf16[288,1152]{1,0:T(8,128)(2,1)S(1)} %bitcast.255), channel_id=1, source_target_pairs={{0,1},{1,0},{2,3},{3,2},{4,5},{5,4},{6,7},{7,6},{8,9},{9,8},{10,11... | collective-permute-start | bytes 1990664 | tf_op jit(solution)/shard_map/ppermute | solution.py:39
  138.7 15.9 %collective-permute-start.22 = (bf16[288,1152]{1,0:T(8,128)(2,1)S(1)}, bf16[288,1152]{1,0:T(8,128)(2,1)S(1)}, u32[]{:S(2)}, u32[]{:S(2)}) collective-permute-start(bf16[288,1152]{1,0:T(8,128)(2,1)S(1)} %bitcast.253), channel_id=1, source_target_pairs={{0,16},{8,24},{16,0},{24,8},{1,17},{9,25},{17,1},{25,9},{2,18},{10... | collective-permute-start | bytes 1990664 | tf_op jit(solution)/shard_map/ppermute | solution.py:39
  154.9 32.8 %collective-permute-start.24 = (bf16[576,1152]{1,0:T(8,128)(2,1)S(1)}, bf16[576,1152]{1,0:T(8,128)(2,1)}, u32[]{:S(2)}, u32[]{:S(2)}) collective-permute-start(bf16[576,1152]{1,0:T(8,128)(2,1)S(1)} %pad_maximum_fusion.12), channel_id=1, source_target_pairs={{0,16},{8,24},{16,0},{24,8},{1,17},{9,25},{17,1},{25,9},{2,18},{10... | collective-permute-start | bytes 3981320 | tf_op jit(solution)/shard_map/ppermute | solution.py:39
  156.5 34.5 %collective-permute-start.25 = (bf16[576,1152]{1,0:T(8,128)(2,1)S(1)}, bf16[576,1152]{1,0:T(8,128)(2,1)}, u32[]{:S(2)}, u32[]{:S(2)}) collective-permute-start(bf16[576,1152]{1,0:T(8,128)(2,1)S(1)} %pad_maximum_fusion.13), channel_id=1, source_target_pairs={{0,1},{1,0},{2,3},{3,2},{4,5},{5,4},{6,7},{7,6},{8,9},{9,8},{10,11... | collective-permute-start | bytes 3981320 | tf_op jit(solution)/shard_map/ppermute | solution.py:39
  157.2 30.3 %collective-permute-start.26 = (bf16[288,1152]{1,0:T(8,128)(2,1)S(1)}, bf16[288,1152]{1,0:T(8,128)(2,1)S(1)}, u32[]{:S(2)}, u32[]{:S(2)}) collective-permute-start(bf16[288,1152]{1,0:T(8,128)(2,1)S(1)} %pad_maximum_fusion.26), channel_id=1, source_target_pairs={{0,2},{1,3},{2,0},{3,1},{4,6},{5,7},{6,4},{7,5},{8,10},{9,11},{10,... | collective-permute-start | bytes 1990664 | tf_op jit(solution)/shard_map/ppermute | solution.py:39
  194.5 18.4 %collective-permute-start.27 = (bf16[1152,1152]{1,0:T(8,128)(2,1)}, bf16[1152,1152]{1,0:T(8,128)(2,1)}, u32[]{:S(2)}, u32[]{:S(2)}) collective-permute-start(bf16[1152,1152]{1,0:T(8,128)(2,1)} %pad_maximum_fusion.2.a_own), channel_id=1, source_target_pairs={{0,8},{8,0},{16,24},{24,16},{1,9},{9,1},{17,25},{25,17},{2,10},{10... | collective-permute-start | bytes 7962632 | tf_op jit(solution)/shard_map/ppermute | solution.py:39
  194.5 18.4 %collective-permute-start.28 = (bf16[1152,1152]{1,0:T(8,128)(2,1)}, bf16[1152,1152]{1,0:T(8,128)(2,1)}, u32[]{:S(2)}, u32[]{:S(2)}) collective-permute-start(bf16[1152,1152]{1,0:T(8,128)(2,1)} %pad_maximum_fusion.3), channel_id=1, source_target_pairs={{0,8},{8,0},{16,24},{24,16},{1,9},{9,1},{17,25},{25,17},{2,10},{10... | collective-permute-start | bytes 7962632 | tf_op jit(solution)/shard_map/ppermute | solution.py:39
  195.1 17.2 %collective-permute-start.29 = (bf16[288,1152]{1,0:T(8,128)(2,1)S(1)}, bf16[288,1152]{1,0:T(8,128)(2,1)S(1)}, u32[]{:S(2)}, u32[]{:S(2)}) collective-permute-start(bf16[288,1152]{1,0:T(8,128)(2,1)S(1)} %bitcast.256), channel_id=1, source_target_pairs={{0,1},{1,0},{2,3},{3,2},{4,5},{5,4},{6,7},{7,6},{8,9},{9,8},{10,11... | collective-permute-start | bytes 1990664 | tf_op jit(solution)/shard_map/ppermute | solution.py:39
  195.9 16.7 %collective-permute-start.30 = (bf16[288,1152]{1,0:T(8,128)(2,1)S(1)}, bf16[288,1152]{1,0:T(8,128)(2,1)S(1)}, u32[]{:S(2)}, u32[]{:S(2)}) collective-permute-start(bf16[288,1152]{1,0:T(8,128)(2,1)S(1)} %bitcast.254), channel_id=1, source_target_pairs={{0,16},{8,24},{16,0},{24,8},{1,17},{9,25},{17,1},{25,9},{2,18},{10... | collective-permute-start | bytes 1990664 | tf_op jit(solution)/shard_map/ppermute | solution.py:39
  212.9 36.0 %collective-permute-start.33 = (bf16[576,1152]{1,0:T(8,128)(2,1)S(1)}, bf16[576,1152]{1,0:T(8,128)(2,1)S(1)}, u32[]{:S(2)}, u32[]{:S(2)}) collective-permute-start(bf16[576,1152]{1,0:T(8,128)(2,1)S(1)} %pad_maximum_fusion.15), channel_id=1, source_target_pairs={{0,16},{8,24},{16,0},{24,8},{1,17},{9,25},{17,1},{25,9},{2,18},{10... | collective-permute-start | bytes 3981320 | tf_op jit(solution)/shard_map/ppermute | solution.py:39
  223.3 12.1 %collective-permute-start.31 = (bf16[576,384]{1,0:T(8,128)(2,1)}, bf16[576,384]{1,0:T(8,128)(2,1)}, u32[]{:S(2)}, u32[]{:S(2)}) collective-permute-start(bf16[576,384]{1,0:T(8,128)(2,1)} %get-tuple-element.236), channel_id=1, source_target_pairs={{0,8},{8,0},{16,24},{24,16},{1,9},{9,1},{17,25},{25,17},{2,10},{10... | collective-permute-start | bytes 1327112 | tf_op jit(solution)/shard_map/ppermute | solution.py:39
  223.3 12.1 %collective-permute-start.32 = (bf16[1152,384]{1,0:T(8,128)(2,1)}, bf16[1152,384]{1,0:T(8,128)(2,1)}, u32[]{:S(2)}, u32[]{:S(2)}) collective-permute-start(bf16[1152,384]{1,0:T(8,128)(2,1)} %get-tuple-element.237), channel_id=1, source_target_pairs={{0,8},{8,0},{16,24},{24,16},{1,9},{9,1},{17,25},{25,17},{2,10},{10... | collective-permute-start | bytes 2654216 | tf_op jit(solution)/shard_map/ppermute | solution.py:39
  223.8 31.1 %collective-permute-start.34 = (bf16[576,1152]{1,0:T(8,128)(2,1)S(1)}, bf16[576,1152]{1,0:T(8,128)(2,1)}, u32[]{:S(2)}, u32[]{:S(2)}) collective-permute-start(bf16[576,1152]{1,0:T(8,128)(2,1)S(1)} %pad_maximum_fusion.16), channel_id=1, source_target_pairs={{0,1},{1,0},{2,3},{3,2},{4,5},{5,4},{6,7},{7,6},{8,9},{9,8},{10,11... | collective-permute-start | bytes 3981320 | tf_op jit(solution)/shard_map/ppermute | solution.py:39
  275.5 14.4 %collective-permute-start.37 = (bf16[1,36,6912]{2,1,0:T(8,128)(2,1)S(1)}, bf16[1,36,6912]{2,1,0:T(8,128)(2,1)S(1)}, u32[]{:S(2)}, u32[]{:S(2)}) collective-permute-start(bf16[1,36,6912]{2,1,0:T(8,128)(2,1)S(1)} %bitcast.265), channel_id=1, source_target_pairs={{0,8},{8,0},{16,24},{24,16},{1,9},{9,1},{17,25},{25,17},{2,10},{10... | collective-permute-start | bytes 1493000 | tf_op jit(solution)/shard_map/ppermute | solution.py:39
  290.1 28.8 %collective-permute-start.38 = (bf16[1152,1152]{1,0:T(8,128)(2,1)}, bf16[1152,1152]{1,0:T(8,128)(2,1)}, u32[]{:S(2)}, u32[]{:S(2)}) collective-permute-start(bf16[1152,1152]{1,0:T(8,128)(2,1)} %get-tuple-element.256.gl.refs_2_), channel_id=1, source_target_pairs={{0,8},{8,0},{16,24},{24,16},{1,9},{9,1},{17,25},{25,17},{2,10},{10... | collective-permute-start | bytes 7962632 | tf_op jit(solution)/shard_map/ppermute | solution.py:39
  319.0 21.2 %collective-permute-start.39 = (bf16[384,5760]{1,0:T(8,128)(2,1)}, bf16[384,5760]{1,0:T(8,128)(2,1)}, u32[]{:S(2)}, u32[]{:S(2)}) collective-permute-start(bf16[384,5760]{1,0:T(8,128)(2,1)} %get-tuple-element.272.refs_2_.refs_3_.refs_4_.refs_5_), channel_id=1, source_target_pairs={{0,8},{8,0},{16,24},{24,16},{1,9},{9,1},{17,25},{25,17},{2,10},{10... | collective-permute-start | bytes 13271048 | tf_op jit(solution)/shard_map/ppermute | solution.py:39
  319.3 20.8 %collective-permute-start.40 = (bf16[16,4608]{1,0:T(8,128)(2,1)S(1)}, bf16[16,4608]{1,0:T(8,128)(2,1)S(1)}, u32[]{:S(2)}, u32[]{:S(2)}) collective-permute-start(bf16[16,4608]{1,0:T(8,128)(2,1)S(1)} %pad_maximum_fusion.39), channel_id=1, source_target_pairs={{0,1},{1,0},{2,3},{3,2},{4,5},{5,4},{6,7},{7,6},{8,9},{9,8},{10,11... | collective-permute-start | bytes 442376 | tf_op jit(solution)/shard_map/ppermute | solution.py:39
  320.6 41.8 %collective-permute-start.41 = (bf16[384,1280]{1,0:T(8,128)(2,1)}, bf16[384,1280]{1,0:T(8,128)(2,1)}, u32[]{:S(2)}, u32[]{:S(2)}) collective-permute-start(bf16[384,1280]{1,0:T(8,128)(2,1)} %get-tuple-element.281.g_ref), channel_id=1, source_target_pairs={{0,1},{1,0},{2,3},{3,2},{4,5},{5,4},{6,7},{7,6},{8,9},{9,8},{10,11... | collective-permute-start | bytes 2949128 | tf_op jit(solution)/shard_map/ppermute | solution.py:39
  323.1 71.5 %collective-permute-start.47 = (bf16[2,36,6912]{2,0,1:T(2,128)(2,1)}, bf16[2,36,6912]{2,0,1:T(2,128)(2,1)}, u32[]{:S(2)}, u32[]{:S(2)}) collective-permute-start(bf16[2,36,6912]{2,0,1:T(2,128)(2,1)} %copy.59), channel_id=1, source_target_pairs={{0,16},{8,24},{16,0},{24,8},{1,17},{9,25},{17,1},{25,9},{2,18},{10... | collective-permute-start | bytes 2985992 | tf_op jit(solution)/shard_map/ppermute | solution.py:39
  359.9 53.4 %collective-permute-start.43 = (bf16[576,1152]{1,0:T(8,128)(2,1)}, bf16[576,1152]{1,0:T(8,128)(2,1)}, u32[]{:S(2)}, u32[]{:S(2)}) collective-permute-start(bf16[576,1152]{1,0:T(8,128)(2,1)} %get-tuple-element.284), channel_id=1, source_target_pairs={{0,16},{8,24},{16,0},{24,8},{1,17},{9,25},{17,1},{25,9},{2,18},{10... | collective-permute-start | bytes 3981320 | tf_op jit(solution)/shard_map/ppermute | solution.py:39
  360.1 53.2 %collective-permute-start.44 = (bf16[576,1152]{1,0:T(8,128)(2,1)}, bf16[576,1152]{1,0:T(8,128)(2,1)}, u32[]{:S(2)}, u32[]{:S(2)}) collective-permute-start(bf16[576,1152]{1,0:T(8,128)(2,1)} %get-tuple-element.286), channel_id=1, source_target_pairs={{0,1},{1,0},{2,3},{3,2},{4,5},{5,4},{6,7},{7,6},{8,9},{9,8},{10,11... | collective-permute-start | bytes 3981320 | tf_op jit(solution)/shard_map/ppermute | solution.py:39
  362.6 31.8 %collective-permute-start.46 = (bf16[16,4608]{1,0:T(8,128)(2,1)S(1)}, bf16[16,4608]{1,0:T(8,128)(2,1)S(1)}, u32[]{:S(2)}, u32[]{:S(2)}) collective-permute-start(bf16[16,4608]{1,0:T(8,128)(2,1)S(1)} %pad_maximum_fusion.41), channel_id=1, source_target_pairs={{0,4},{1,5},{2,6},{3,7},{4,0},{5,1},{6,2},{7,3},{8,12},{9,13},{10,... | collective-permute-start | bytes 442376 | tf_op jit(solution)/shard_map/ppermute | solution.py:39
  387.7 25.7 %collective-permute-start.45 = (bf16[384,1280]{1,0:T(8,128)(2,1)}, bf16[384,1280]{1,0:T(8,128)(2,1)}, u32[]{:S(2)}, u32[]{:S(2)}) collective-permute-start(bf16[384,1280]{1,0:T(8,128)(2,1)} %collective-permute-done.41.gn), channel_id=1, source_target_pairs={{0,2},{2,4},{4,6},{3,1},{5,3},{7,5},{8,10},{10,12},{12,14},{11,9},... | collective-permute-start | bytes 2949128 | tf_op jit(solution)/shard_map/ppermute | solution.py:1281
  394.4 69.4 %collective-permute-start.50 = (bf16[576,1152]{1,0:T(8,128)(2,1)}, bf16[576,1152]{1,0:T(8,128)(2,1)}, u32[]{:S(2)}, u32[]{:S(2)}) collective-permute-start(bf16[576,1152]{1,0:T(8,128)(2,1)} %get-tuple-element.306), channel_id=1, source_target_pairs={{0,16},{8,24},{16,0},{24,8},{1,17},{9,25},{17,1},{25,9},{2,18},{10... | collective-permute-start | bytes 3981320 | tf_op jit(solution)/shard_map/ppermute | solution.py:39
  394.6 69.3 %collective-permute-start.51 = (bf16[576,1152]{1,0:T(8,128)(2,1)}, bf16[576,1152]{1,0:T(8,128)(2,1)}, u32[]{:S(2)}, u32[]{:S(2)}) collective-permute-start(bf16[576,1152]{1,0:T(8,128)(2,1)} %get-tuple-element.308), channel_id=1, source_target_pairs={{0,1},{1,0},{2,3},{3,2},{4,5},{5,4},{6,7},{7,6},{8,9},{9,8},{10,11... | collective-permute-start | bytes 3981320 | tf_op jit(solution)/shard_map/ppermute | solution.py:39
  413.3 16.4 %collective-permute-start.48 = (bf16[384,1152]{1,0:T(8,128)(2,1)}, bf16[384,1152]{1,0:T(8,128)(2,1)}, u32[]{:S(2)}, u32[]{:S(2)}) collective-permute-start(bf16[384,1152]{1,0:T(8,128)(2,1)} %get-tuple-element.291.refs_4_.gq), channel_id=1, source_target_pairs={{0,8},{8,0},{16,24},{24,16},{1,9},{9,1},{17,25},{25,17},{2,10},{10... | collective-permute-start | bytes 2654216 | tf_op jit(solution)/shard_map/ppermute | solution.py:39
  414.1 11.9 %collective-permute-start.49 = (f32[1,14,4608]{2,1,0:T(8,128)}, f32[1,14,4608]{2,1,0:T(8,128)}, u32[]{:S(2)}, u32[]{:S(2)}) collective-permute-start(f32[1,14,4608]{2,1,0:T(8,128)} %bitcast.51), channel_id=1, source_target_pairs={{0,8},{8,0},{16,24},{24,16},{1,9},{9,1},{17,25},{25,17},{2,10},{10... | collective-permute-start | bytes 774152 | tf_op jit(solution)/shard_map/ppermute | solution.py:39
  417.4 46.5 %collective-permute-start.52 = (bf16[288,1152]{1,0:T(8,128)(2,1)}, bf16[288,1152]{1,0:T(8,128)(2,1)}, u32[]{:S(2)}, u32[]{:S(2)}) collective-permute-start(bf16[288,1152]{1,0:T(8,128)(2,1)} %get-tuple-element.514), channel_id=1, source_target_pairs={{0,1},{1,0},{2,3},{3,2},{4,5},{5,4},{6,7},{7,6},{8,9},{9,8},{10,11... | collective-permute-start | bytes 1990664 | tf_op jit(solution)/shard_map/ppermute | solution.py:39
  426.0 37.9 %collective-permute-start.53 = (bf16[288,1152]{1,0:T(8,128)(2,1)}, bf16[288,1152]{1,0:T(8,128)(2,1)}, u32[]{:S(2)}, u32[]{:S(2)}) collective-permute-start(bf16[288,1152]{1,0:T(8,128)(2,1)} %get-tuple-element.512), channel_id=1, source_target_pairs={{0,16},{8,24},{16,0},{24,8},{1,17},{9,25},{17,1},{25,9},{2,18},{10... | collective-permute-start | bytes 1990664 | tf_op jit(solution)/shard_map/ppermute | solution.py:39
  441.5 22.1 %collective-permute-start.54 = (f32[2,14,4608]{2,0,1:T(2,128)S(1)}, f32[2,14,4608]{2,0,1:T(2,128)S(1)}, u32[]{:S(2)}, u32[]{:S(2)}) collective-permute-start(f32[2,14,4608]{2,0,1:T(2,128)S(1)} %copy.60), channel_id=1, source_target_pairs={{0,16},{8,24},{16,0},{24,8},{1,17},{9,25},{17,1},{25,9},{2,18},{10... | collective-permute-start | bytes 1548296 | tf_op jit(solution)/shard_map/ppermute | solution.py:39
  463.9 46.0 %collective-permute-start.55 = (bf16[384,2304]{1,0:T(8,128)(2,1)}, bf16[384,2304]{1,0:T(8,128)(2,1)}, u32[]{:S(2)}, u32[]{:S(2)}) collective-permute-start(bf16[384,2304]{1,0:T(8,128)(2,1)} %attend_backward_other.1.gkv.refs_2_.refs_3_), channel_id=1, source_target_pairs={{0,8},{8,0},{16,24},{24,16},{1,9},{9,1},{17,25},{25,17},{2,10},{10... | collective-permute-start | bytes 5308424 | tf_op jit(solution)/shard_map/ppermute | solution.py:39
  469.0 38.8 %collective-permute-start.56 = (bf16[288,1152]{1,0:T(8,128)(2,1)}, bf16[288,1152]{1,0:T(8,128)(2,1)}, u32[]{:S(2)}, u32[]{:S(2)}) collective-permute-start(bf16[288,1152]{1,0:T(8,128)(2,1)} %get-tuple-element.510), channel_id=1, source_target_pairs={{0,2},{1,3},{2,0},{3,1},{4,6},{5,7},{6,4},{7,5},{8,10},{9,11},{10,... | collective-permute-start | bytes 1990664 | tf_op jit(solution)/shard_map/ppermute | solution.py:39
  469.0 40.9 %collective-permute-start.57 = (bf16[288,1152]{1,0:T(8,128)(2,1)}, bf16[288,1152]{1,0:T(8,128)(2,1)}, u32[]{:S(2)}, u32[]{:S(2)}) collective-permute-start(bf16[288,1152]{1,0:T(8,128)(2,1)} %get-tuple-element.327), channel_id=1, source_target_pairs={{0,16},{8,24},{16,0},{24,8},{1,17},{9,25},{17,1},{25,9},{2,18},{10... | collective-permute-start | bytes 1990664 | tf_op jit(solution)/shard_map/ppermute | solution.py:39
  472.5 37.4 %collective-permute-start.58 = (bf16[288,1152]{1,0:T(8,128)(2,1)}, bf16[288,1152]{1,0:T(8,128)(2,1)}, u32[]{:S(2)}, u32[]{:S(2)}) collective-permute-start(bf16[288,1152]{1,0:T(8,128)(2,1)} %get-tuple-element.329), channel_id=1, source_target_pairs={{0,1},{1,0},{2,3},{3,2},{4,5},{5,4},{6,7},{7,6},{8,9},{9,8},{10,11... | collective-permute-start | bytes 1990664 | tf_op jit(solution)/shard_map/ppermute | solution.py:39
  504.9 22.5 %collective-permute-start.59 = (bf16[288,1152]{1,0:T(8,128)(2,1)}, bf16[288,1152]{1,0:T(8,128)(2,1)}, u32[]{:S(2)}, u32[]{:S(2)}) collective-permute-start(bf16[288,1152]{1,0:T(8,128)(2,1)} %get-tuple-element.504), channel_id=1, source_target_pairs={{0,1},{1,0},{2,3},{3,2},{4,5},{5,4},{6,7},{7,6},{8,9},{9,8},{10,11... | collective-permute-start | bytes 1990664 | tf_op jit(solution)/shard_map/ppermute | solution.py:39
  507.8 19.7 %collective-permute-start.60 = (bf16[288,1152]{1,0:T(8,128)(2,1)}, bf16[288,1152]{1,0:T(8,128)(2,1)}, u32[]{:S(2)}, u32[]{:S(2)}) collective-permute-start(bf16[288,1152]{1,0:T(8,128)(2,1)} %get-tuple-element.502), channel_id=1, source_target_pairs={{0,16},{8,24},{16,0},{24,8},{1,17},{9,25},{17,1},{25,9},{2,18},{10... | collective-permute-start | bytes 1990664 | tf_op jit(solution)/shard_map/ppermute | solution.py:39
  522.8 17.4 %collective-permute-start.65 = (bf16[144,1152]{1,0:T(8,128)(2,1)S(1)}, bf16[144,1152]{1,0:T(8,128)(2,1)S(1)}, u32[]{:S(2)}, u32[]{:S(2)}) collective-permute-start(bf16[144,1152]{1,0:T(8,128)(2,1)S(1)} %get-tuple-element.566), channel_id=1, source_target_pairs={{0,4},{1,5},{2,6},{3,7},{4,0},{5,1},{6,2},{7,3},{8,12},{9,13},{10,... | collective-permute-start | bytes 995336 | tf_op jit(solution)/shard_map/ppermute | solution.py:39
  525.0 46.0 %collective-permute-start.67 = (bf16[144,1152]{1,0:T(8,128)(2,1)S(1)}, bf16[144,1152]{1,0:T(8,128)(2,1)S(1)}, u32[]{:S(2)}, u32[]{:S(2)}) collective-permute-start(bf16[144,1152]{1,0:T(8,128)(2,1)S(1)} %get-tuple-element.564), channel_id=1, source_target_pairs={{0,1},{1,0},{2,3},{3,2},{4,5},{5,4},{6,7},{7,6},{8,9},{9,8},{10,11... | collective-permute-start | bytes 995336 | tf_op jit(solution)/shard_map/ppermute | solution.py:39
  527.5 17.9 %collective-permute-start.62 = (bf16[288,1152]{1,0:T(8,128)(2,1)S(1)}, bf16[288,1152]{1,0:T(8,128)(2,1)S(1)}, u32[]{:S(2)}, u32[]{:S(2)}) collective-permute-start(bf16[288,1152]{1,0:T(8,128)(2,1)S(1)} %get-tuple-element.341), channel_id=1, source_target_pairs={{0,16},{8,24},{16,0},{24,8},{1,17},{9,25},{17,1},{25,9},{2,18},{10... | collective-permute-start | bytes 1990664 | tf_op jit(solution)/shard_map/ppermute | solution.py:39
  529.5 18.8 %collective-permute-start.63 = (bf16[288,1152]{1,0:T(8,128)(2,1)S(1)}, bf16[288,1152]{1,0:T(8,128)(2,1)S(1)}, u32[]{:S(2)}, u32[]{:S(2)}) collective-permute-start(bf16[288,1152]{1,0:T(8,128)(2,1)S(1)} %get-tuple-element.343), channel_id=1, source_target_pairs={{0,1},{1,0},{2,3},{3,2},{4,5},{5,4},{6,7},{7,6},{8,9},{9,8},{10,11... | collective-permute-start | bytes 1990664 | tf_op jit(solution)/shard_map/ppermute | solution.py:39
  540.1 13.5 %collective-permute-start.64 = (bf16[288,1152]{1,0:T(8,128)(2,1)S(1)}, bf16[288,1152]{1,0:T(8,128)(2,1)S(1)}, u32[]{:S(2)}, u32[]{:S(2)}) collective-permute-start(bf16[288,1152]{1,0:T(8,128)(2,1)S(1)} %get-tuple-element.500), channel_id=1, source_target_pairs={{0,2},{1,3},{2,0},{3,1},{4,6},{5,7},{6,4},{7,5},{8,10},{9,11},{10,... | collective-permute-start | bytes 1990664 | tf_op jit(solution)/shard_map/ppermute | solution.py:39
  540.2 30.8 %collective-permute-start.68 = (bf16[144,1152]{1,0:T(8,128)(2,1)S(1)}, bf16[144,1152]{1,0:T(8,128)(2,1)S(1)}, u32[]{:S(2)}, u32[]{:S(2)}) collective-permute-start(bf16[144,1152]{1,0:T(8,128)(2,1)S(1)} %get-tuple-element.562), channel_id=1, source_target_pairs={{0,16},{8,24},{16,0},{24,8},{1,17},{9,25},{17,1},{25,9},{2,18},{10... | collective-permute-start | bytes 995336 | tf_op jit(solution)/shard_map/ppermute | solution.py:39
  554.6 16.4 %collective-permute-start.69 = (bf16[144,1152]{1,0:T(8,128)(2,1)S(1)}, bf16[144,1152]{1,0:T(8,128)(2,1)S(1)}, u32[]{:S(2)}, u32[]{:S(2)}) collective-permute-start(bf16[144,1152]{1,0:T(8,128)(2,1)S(1)} %get-tuple-element.560), channel_id=1, source_target_pairs={{0,4},{1,5},{2,6},{3,7},{4,0},{5,1},{6,2},{7,3},{8,12},{9,13},{10,... | collective-permute-start | bytes 995336 | tf_op jit(solution)/shard_map/ppermute | solution.py:39
  555.3 14.9 %collective-permute-start.70 = (bf16[14,2304]{1,0:T(8,128)(2,1)S(1)}, bf16[14,2304]{1,0:T(8,128)(2,1)S(1)}, u32[]{:S(2)}, u32[]{:S(2)}) collective-permute-start(bf16[14,2304]{1,0:T(8,128)(2,1)S(1)} %pad_maximum_fusion.53), channel_id=1, source_target_pairs={{0,4},{1,5},{2,6},{3,7},{4,0},{5,1},{6,2},{7,3},{8,12},{9,13},{10,... | collective-permute-start | bytes 193544 | tf_op jit(solution)/shard_map/ppermute | solution.py:39
  572.1 13.3 %collective-permute-start.71 = (bf16[144,1152]{1,0:T(8,128)(2,1)}, bf16[144,1152]{1,0:T(8,128)(2,1)}, u32[]{:S(2)}, u32[]{:S(2)}) collective-permute-start(bf16[144,1152]{1,0:T(8,128)(2,1)} %get-tuple-element.558), channel_id=1, source_target_pairs={{0,1},{1,0},{2,3},{3,2},{4,5},{5,4},{6,7},{7,6},{8,9},{9,8},{10,11... | collective-permute-start | bytes 995336 | tf_op jit(solution)/shard_map/ppermute | solution.py:39
  574.3 11.1 %collective-permute-start.72 = (bf16[144,1152]{1,0:T(8,128)(2,1)}, bf16[144,1152]{1,0:T(8,128)(2,1)}, u32[]{:S(2)}, u32[]{:S(2)}) collective-permute-start(bf16[144,1152]{1,0:T(8,128)(2,1)} %get-tuple-element.556), channel_id=1, source_target_pairs={{0,16},{8,24},{16,0},{24,8},{1,17},{9,25},{17,1},{25,9},{2,18},{10... | collective-permute-start | bytes 995336 | tf_op jit(solution)/shard_map/ppermute | solution.py:39
  588.8 12.5 %collective-permute-start.76 = (bf16[144,1152]{1,0:T(8,128)(2,1)S(1)}, bf16[144,1152]{1,0:T(8,128)(2,1)S(1)}, u32[]{:S(2)}, u32[]{:S(2)}) collective-permute-start(bf16[144,1152]{1,0:T(8,128)(2,1)S(1)} %get-tuple-element.552), channel_id=1, source_target_pairs={{0,2},{1,3},{2,0},{3,1},{4,6},{5,7},{6,4},{7,5},{8,10},{9,11},{10,... | collective-permute-start | bytes 995336 | tf_op jit(solution)/shard_map/ppermute | solution.py:39
  (86 other events, 564.2 us)

commit v2 on v1

--- a/solution.py
+++ b/solution.py
@@ -170,7 +170,7 @@
     return z % 2 * 2 + z // 2
 
 
-def chip_grads(lefts, rights, products, orders, turned, shape, name):
+def chip_grads(bits, lefts, rights, products, orders, turned, shape, name):
     tokens, width = shape
     parts = [own.shape[0] // 2 if turned else own.shape[1] for own, _ in lefts]
     height = [
@@ -180,12 +180,13 @@
     n_left, n_right = len(lefts), len(rights)
     product_of = dot_nn if turned else dot_tn
 
-    def body(*refs):
+    def body(bits_ref, *refs):
         lefts_own, lefts_oth = refs[:n_left], refs[n_left : 2 * n_left]
         rights_own = refs[2 * n_left : 2 * n_left + n_right]
         rights_oth = refs[2 * n_left + n_right : 2 * n_left + 2 * n_right]
         outs, acc = refs[2 * n_left + 2 * n_right : -1], refs[-1]
-        y = pl.program_id(0)
+        keep = pl.program_id(0)
+        y = jnp.where(keep == 1, bits_ref[1], 1 - bits_ref[1])
         for li, ri, chunk, pieces in products:
             acc[: 8 * chunk, :] = product_of(
                 lefts_own[li][...], rights_own[ri][...]
@@ -196,45 +197,58 @@
                     value = acc[j * chunk + start : j * chunk + start + n, :].astype(BF)
                     if orders[out] == "yxz":
                         row = (x * 4 + z_place(z)) * height[out] + at
-                        outs[out][row : row + n, :] = value
+                        chosen = keep
                     else:
-                        for yy in range(2):
-                            row = ((x * 2 + yy) * 4 + z_place(z)) * height[out] + at
-
-                            @pl.when(y == yy)
-                            def _(row=row, value=value, out=out, n=n):
-                                outs[out][row : row + n, :] = value
+                        row = z_place(z) * height[out] + at
+                        chosen = jnp.where(bits_ref[0] == x, 1, 0)
+                    for k in range(2):
+
+                        @pl.when(chosen == k)
+                        def _(row=row, value=value, out=out, n=n, k=k):
+                            ref = outs[2 * out + k]
+                            if orders[out] == "yxz":
+                                ref[row : row + n, :] = value
+                            else:
+                                ref[y, row : row + n, :] = value
 
     left_specs = [
-        pl.BlockSpec((p, tokens) if turned else (tokens, p), lambda i: (i, 0)) for p in parts
+        pl.BlockSpec(
+            (p, tokens) if turned else (tokens, p), lambda i, b: (jnp.where(i == 1, b[1], 1 - b[1]), 0)
+        )
+        for p in parts
     ]
     right_specs = [
-        pl.BlockSpec((tokens, width), lambda i, r=r, k=k: (r, k)) for _, _, r, k in rights
+        pl.BlockSpec((tokens, width), lambda i, b, r=r, k=k: (r, k)) for _, _, r, k in rights
     ]
     out_specs, out_shape = [], []
     for order, h in zip(orders, height):
-        if order == "yxz":
-            out_specs.append(pl.BlockSpec((8 * h, width), lambda i: (i, 0)))
-        else:
-            out_specs.append(pl.BlockSpec((16 * h, width), lambda i: (0, 0)))
-        out_shape.append(jax.ShapeDtypeStruct((16 * h, width), BF))
+        half = (8 * h, width) if order == "yxz" else (2, 4 * h, width)
+        out_specs += [whole(half)] * 2
+        out_shape += [jax.ShapeDtypeStruct(half, BF)] * 2
     total = sum(16 * h for h in height)
-    return pl.pallas_call(
+    results = pl.pallas_call(
         body,
-        grid=(2,),
-        in_specs=left_specs * 2 + right_specs * 2,
-        out_specs=out_specs,
+        grid_spec=pltpu.PrefetchScalarGridSpec(
+            num_scalar_prefetch=1,
+            grid=(2,),
+            in_specs=left_specs * 2 + right_specs * 2,
+            out_specs=out_specs,
+            scratch_shapes=[pltpu.VMEM((max(parts), width), F32)],
+        ),
         out_shape=out_shape,
-        scratch_shapes=[pltpu.VMEM((max(parts), width), F32)],
         compiler_params=pltpu.CompilerParams(vmem_limit_bytes=VMEM_LIMIT),
         cost_estimate=cost(10),
         name=name,
     )(
+        bits,
         *[own for own, _ in lefts],
         *[oth for _, oth in lefts],
         *[r[0] for r in rights],
         *[r[1] for r in rights],
     )
+    return [
+        tuple(v.reshape(-1, width) for v in results[2 * k : 2 * k + 2]) for k in range(len(orders))
+    ]
 
 
 def split_by(v, bit):
@@ -254,15 +268,77 @@
     return kept, swap(sent, axis, bit)
 
 
-def joined(pair):
-    return add(*pair).astype(BF)
-
-
-def side_by_side(v_a, v_b):
-    shape = (4, 1, v_a.shape[0] // 4, v_a.shape[1])
-    return jnp.concatenate([v_a.reshape(shape), v_b.reshape(shape)], axis=1).reshape(
-        2 * v_a.shape[0], v_a.shape[1]
-    )
+COLUMNS = 1152
+
+
+def stage_call(body, bits, operands, rows_out, name):
+    width = operands[0].shape[1]
+    return pl.pallas_call(
+        body,
+        grid_spec=pltpu.PrefetchScalarGridSpec(
+            num_scalar_prefetch=1,
+            grid=(width // COLUMNS,),
+            in_specs=[pl.BlockSpec((v.shape[0], COLUMNS), lambda i, b: (0, i)) for v in operands],
+            out_specs=[pl.BlockSpec((n, COLUMNS), lambda i, b: (0, i)) for n in rows_out],
+        ),
+        out_shape=[jax.ShapeDtypeStruct((n, width), BF) for n in rows_out],
+        compiler_params=pltpu.CompilerParams(vmem_limit_bytes=VMEM_LIMIT),
+        cost_estimate=cost(2),
+        name=name,
+    )(bits, *operands)
+
+
+def add_and_cut(bits, a, b):
+    n = a[0].shape[0] // 2
+
+    def body(bits_ref, a_own, a_got, b_own, b_got, a_sent, a_kept, b_sent, b_kept):
+        for own, got, sent, kept, bit in (
+            (a_own, a_got, a_sent, a_kept, bits_ref[0]),
+            (b_own, b_got, b_sent, b_kept, bits_ref[1]),
+        ):
+            there = pl.ds(pl.multiple_of((1 - bit) * n, 16), n)
+            here = pl.ds(pl.multiple_of(bit * n, 16), n)
+            sent[...] = add(own[there, :], got[there, :]).astype(BF)
+            kept[...] = add(own[here, :], got[here, :]).astype(BF)
+
+    a_sent, a_kept, b_sent, b_kept = stage_call(body, bits, [*a, *b], [n] * 4, "add_and_cut")
+    return (a_sent, a_kept), (b_sent, b_kept)
+
+
+def add_and_cut_z(bits, a, b):
+    h = a[0].shape[0] // 4
+
+    def body(bits_ref, a_own, a_got, b_own, b_got, sent, kept):
+        for even in range(2):
+
+            @pl.when(bits_ref[2] == even)
+            def _():
+                for ref, low in ((sent, 1 - even), (kept, even)):
+                    for k in range(2):
+                        rows = slice((low * 2 + k) * h, (low * 2 + k + 1) * h)
+                        ref[k * 2 * h : k * 2 * h + h, :] = add(
+                            a_own[rows, :], a_got[rows, :]
+                        ).astype(BF)
+                        ref[k * 2 * h + h : (k + 1) * 2 * h, :] = add(
+                            b_own[rows, :], b_got[rows, :]
+                        ).astype(BF)
+
+    return tuple(stage_call(body, bits, [*a, *b], [4 * h] * 2, "add_and_cut_z"))
+
+
+def add_and_cut_last(bits, got):
+    n = got[0].shape[0] // 2
+
+    def body(bits_ref, own, other, sent, kept):
+        for high in range(2):
+
+            @pl.when(bits_ref[3] == high)
+            def _():
+                there, here = slice((1 - high) * n, (2 - high) * n), slice(high * n, (high + 1) * n)
+                sent[...] = add(own[there, :], other[there, :]).astype(BF)
+                kept[...] = add(own[here, :], other[here, :]).astype(BF)
+
+    return tuple(stage_call(body, bits, [*got], [n] * 2, "add_and_cut_last"))
 
 
 def head_window(h, size):
@@ -282,7 +358,7 @@
     scale = size**-0.5
     blocks = tokens // BLOCK
 
-    def body(info_ref, q_ref, k_ref, v_ref, o_ref, lse_ref):
+    def body(info_ref, q_ref, k_ref, v_ref, o_ref, full_ref, lse_ref):
         def one_block(i, carry):
             row = pl.multiple_of(i * BLOCK, BLOCK)
             start = pl.multiple_of(info_ref[i], BLOCK)
@@ -300,12 +376,12 @@
                     peak = jnp.max(s, axis=1, keepdims=True)
                     p = jnp.exp(s - peak)
                     total = jnp.sum(p, axis=1, keepdims=True)
-                    o = (dot_nn(p.astype(BF), v) * (1.0 / total)).astype(BF)
+                    o = dot_nn(p.astype(BF), v) * (1.0 / total)
                     if off == 0:
-                        o_ref[pl.ds(row, BLOCK), lo:hi] = o
+                        full_ref[pl.ds(row, BLOCK), lo:hi] = o
                     else:
-                        o_ref[pl.ds(row, BLOCK), lo:hi] = jnp.where(
-                            mask, o, o_ref[pl.ds(row, BLOCK), lo:hi]
+                        full_ref[pl.ds(row, BLOCK), lo:hi] = jnp.where(
+                            mask, o, full_ref[pl.ds(row, BLOCK), lo:hi]
                         )
                     lse_all = jnp.where(
                         lane_mask(lse_all.shape, h, 1), peak + jnp.log(total), lse_all
@@ -323,6 +399,7 @@
             return carry
 
         lax.fori_loop(0, blocks, one_block, 0)
+        o_ref[...] = full_ref[...].astype(BF)
 
     return pl.pallas_call(
         body,
@@ -336,11 +413,13 @@
             ],
             out_specs=[
                 pl.BlockSpec((tokens, width), lambda i, s: (0, 0)),
+                pl.BlockSpec((tokens, width), lambda i, s: (0, 0)),
                 pl.BlockSpec((tokens, 128), lambda i, s: (0, 0)),
             ],
         ),
         out_shape=[
             jax.ShapeDtypeStruct((tokens, width), BF),
+            jax.ShapeDtypeStruct((tokens, width), F32),
             jax.ShapeDtypeStruct((tokens, 128), F32),
         ],
         compiler_params=pltpu.CompilerParams(vmem_limit_bytes=VMEM_LIMIT),
@@ -670,11 +749,11 @@
         ),
         out_shape=[
             jax.ShapeDtypeStruct((2 * tokens, width), BF),
-            jax.ShapeDtypeStruct((3 * tokens, width), BF),
+            jax.ShapeDtypeStruct((2 * tokens, width), BF),
             jax.ShapeDtypeStruct((tokens, 4 * width), BF),
         ],
         compiler_params=pltpu.CompilerParams(vmem_limit_bytes=VMEM_LIMIT),
-        cost_estimate=cost(1),
+        cost_estimate=cost(14),
         name="feed_forward_up",
     )(order, mlp_in, hidden_w, hidden_b)
 
@@ -727,18 +806,17 @@
                 whole(mods.shape),
             ],
             out_specs=[
-                pl.BlockSpec((tokens, width), lambda t, o: (2, 0)),
+                row,
                 row,
                 whole((8, width)),
             ],
             scratch_shapes=[pltpu.VMEM((tokens, width), F32)],
         ),
         out_shape=[
-            jax.ShapeDtypeStruct((3 * tokens, width), BF),
+            jax.ShapeDtypeStruct((tokens, width), BF),
             jax.ShapeDtypeStruct((tokens, width), BF),
             jax.ShapeDtypeStruct((8, width), F32),
         ],
-        input_output_aliases={2: 0},
         compiler_params=pltpu.CompilerParams(vmem_limit_bytes=VMEM_LIMIT),
         cost_estimate=cost(12),
         name="feed_forward_down",
@@ -746,7 +824,7 @@
 
 
 def feed_forward_back(
-    act_and_lower, slope, hidden_w, output_w, proj, after, branch, attn_low, lse, cotangent, mods, heads
+    grad_lower, slope, hidden_w, output_w, proj, after, branch, attended, lse, cotangent, mods, heads
 ):
     tokens, width = after.shape
     blocks = tokens // BLOCK
@@ -808,7 +886,7 @@
                 total = total + column_sum(low_branch)
                 grad = dot_nt(low_branch, wp[...]).astype(BF)
                 gat[rows, :width] = grad
-                product = grad.astype(F32) * low[rows, :].astype(F32)
+                product = grad.astype(F32) * low[rows, :]
                 high = product.astype(BF)
                 rest = (product - high.astype(F32)).astype(BF)
                 value = lse_ref[rows, :] + dot_nn(high, pick) + dot_nn(rest, pick)
@@ -825,7 +903,7 @@
         body,
         grid=(4,),
         in_specs=[
-            pl.BlockSpec((tokens, width), lambda t: (2, 0)),
+            row,
             pl.BlockSpec((tokens, width), lambda t: (0, t)),
             pl.BlockSpec((width, width), lambda t: (0, t)),
             pl.BlockSpec((width, width), lambda t: (t, 0)),
@@ -856,14 +934,14 @@
         cost_estimate=cost(24),
         name="feed_forward_back",
     )(
-        act_and_lower,
+        grad_lower,
         slope,
         hidden_w,
         output_w,
         proj,
         after,
         branch,
-        attn_low,
+        attended,
         lse,
         cotangent,
         mods,
@@ -1029,6 +1107,8 @@
         sent = lax.dynamic_index_in_dim(kept, 1 - y, 0, keepdims=False).astype(BF)
         kept = lax.dynamic_index_in_dim(kept, y, 0, keepdims=False)
         row_mod = kept + swap(sent, "dp", 2).astype(F32)
+        row_mod, ada_pair = barrier((row_mod, pair_up(ada_weight[None], "dp", core, 1)))
+        ada_got = swap(ada_pair, "dp", 2)
         for bit in (1, 2, 4):
             low = row_mod.astype(BF)
             row_mod = low.astype(F32) + swap(low, "blk", bit).astype(F32)
@@ -1090,8 +1170,8 @@
     )
 
     if fast:
-        attn_in_all, first_halves, second_line, third_shard = barrier(
-            (attn_in_all, first_halves, second_line, second[4 * rows :])
+        attn_in_all, first_halves, second_line, third_shard, ada_got = barrier(
+            (attn_in_all, first_halves, second_line, second[4 * rows :], ada_got)
         )
         first_parts = both_cores(*first_halves)
         second_halves = gather_cross(second_line, x, y)
@@ -1126,7 +1206,7 @@
         queries, second_halves, third_line = barrier((queries, second_halves, third_line))
         second_parts = both_cores(*second_halves)
         third_halves = gather_cross(third_line, x, y)
-    attn_low, lse = attend_forward(forward_info, queries, keys, values, HEADS)
+    attn_low, attended, lse = attend_forward(forward_info, queries, keys, values, HEADS)
 
     def eight(v):
         return jnp.broadcast_to(v[None, :], (8, v.shape[0]))
@@ -1145,7 +1225,7 @@
             [(0, 0), (0, 1), (0, 2), (0, 3)],
             "unpack_hidden",
         )
-        attn_in_send, mlp_low_send, ada_rows = barrier((attn_in_send, mlp_low_send, ada_weight))
+        attn_in_send, mlp_low_send = barrier((attn_in_send, mlp_low_send))
         attn_in_oth, mlp_low_oth = swap(attn_in_send, "dp", 1), swap(mlp_low_send, "dp", 1)
         mlp_in, attn_in_oth, mlp_low_oth = lax.optimization_barrier(
             (mlp_in, attn_in_oth, mlp_low_oth)
@@ -1154,10 +1234,10 @@
     act_keep, act_send, slope = feed_forward_up(order, mlp_in, full_hidden, eight(full_hidden_bias))
     if fast:
         act_keep, third_halves = barrier((act_keep, third_halves))
-        full_output = unpack_rows(core_only, both_cores(*third_halves), 4 * rows, "unpack_output")
-        full_output, ada_rows = barrier((full_output, ada_rows))
-        ada_rows = pair_up(ada_rows[None], "dp", core, 1)
-    act_and_lower, block_out, lower_sums = feed_forward_down(
+        third_parts = both_cores(*third_halves)
+        act_oth = swap(act_send, "dp", 1)
+        full_output = unpack_rows(core_only, third_parts, 4 * rows, "unpack_output")
+    grad_lower, block_out, lower_sums = feed_forward_down(
         order,
         act_keep,
         act_send,
@@ -1171,17 +1251,51 @@
     shape = (tokens_dev, width)
     orders = ["yxz", "xyz"]
     if fast:
-        act_and_lower, ada_pair = barrier((act_and_lower, ada_rows))
-        act_and_lower_oth = swap(act_and_lower, "dp", 1)
+        bits = jnp.stack([x, y, z % 2, z // 2]).astype(jnp.int32)
+
+        def step_1(halves):
+            return send(halves[0], "dp", 2), send(halves[1], "blk", 1)
+
+        def step_2(halves):
+            return send(halves[0], "blk", 1), send(halves[1], "dp", 2)
+
+        def step_3(halves):
+            return send(halves, "blk", 2)
+
+        def step_4(halves):
+            return send(halves, "blk", 4)
+
+        def half_2(got):
+            return add_and_cut(bits, *got)
+
+        def half_3(got):
+            return add_and_cut_z(bits, *got)
+
+        def half_4(got):
+            return add_and_cut_last(bits, got)
+
+        act_keep, act_oth, grad_lower_oth = barrier((act_keep, act_oth, swap(grad_lower, "dp", 1)))
+        third = chip_grads(
+            bits,
+            [(act_keep, act_oth)],
+            [(grad_lower, grad_lower_oth, 0, 0)],
+            [(0, 0, 4 * rows, [(0, 2 * rows, 0, 0), (2 * rows, 2 * rows, 1, 0)])],
+            orders,
+            False,
+            shape,
+            "grad_output_weight",
+        )
+        grad_lower, third = barrier((grad_lower, third))
+        third = step_1(third)
     grad_upper, grad_after, grad_attn, upper_sums, branch_sums = feed_forward_back(
-        act_and_lower,
+        grad_lower,
         slope,
         full_hidden,
         full_output,
         full_proj,
         after_attn,
         branch,
-        attn_low,
+        attended,
         lse,
         cotangent[0],
         own_mods,
@@ -1217,55 +1331,26 @@
         grad_near, grad_far = halo(grad_attn, fast)
     else:
 
-        def half_1(group):
-            return split_by(group[0], y), split_by(group[1], x)
-
-        def step_1(halves):
-            return send(halves[0], "dp", 2), send(halves[1], "blk", 1)
-
-        def half_2(got):
-            return split_by(joined(got[0]), x), split_by(joined(got[1]), y)
-
-        def step_2(halves):
-            return send(halves[0], "blk", 1), send(halves[1], "dp", 2)
-
-        def half_3(got):
-            return split_by(side_by_side(joined(got[0]), joined(got[1])), z % 2)
-
-        def step_3(halves):
-            return send(halves, "blk", 2)
-
-        def half_4(got):
-            return split_by(joined(got), z // 2)
-
-        def step_4(halves):
-            return send(halves, "blk", 4)
-
         early = early_message()
-        act_keep, grad_upper, grad_attn, early, act_and_lower_oth, ada_pair = barrier(
-            (act_keep, grad_upper, grad_attn, early, act_and_lower_oth, ada_pair)
-        )
-        ada_got = swap(ada_pair, "dp", 2)
+        grad_attn, grad_upper, third, early = barrier((grad_attn, grad_upper, third, early))
         grad_upper_oth = swap(grad_upper, "dp", 1)
+        grad_near = swap(grad_attn, "blk", 1)
         early_got = swap_exact(early, 1, 2)
-        grad_near = swap(grad_attn, "blk", 1)
-        third = chip_grads(
-            [(act_keep, act_and_lower_oth)],
-            [(act_and_lower, act_and_lower_oth, 2, 0)],
-            [(0, 0, 4 * rows, [(0, 2 * rows, 0, 0), (2 * rows, 2 * rows, 1, 0)])],
-            orders,
-            False,
-            shape,
-            "grad_output_weight",
-        )
-
-        mlp_keep, third, grad_upper_oth, early, early_got = barrier(
-            (mlp_keep, half_1(third), grad_upper_oth, early, early_got)
-        )
-        third = step_1(third)
+        third = half_2(third)
+    grad_q, grad_k_own, grad_v_own = attend_backward_own(
+        forward_info, queries, keys, values, grad_attn, HEADS
+    )
+    if fast:
+        mlp_keep, grad_q, grad_near, grad_upper_oth, early, early_got, third = barrier(
+            (mlp_keep, grad_q, grad_near, grad_upper_oth, early, early_got, third)
+        )
+        grad_far = lax.ppermute(grad_near, "blk", halo_hops())
+        grad_q_oth = swap(grad_q, "dp", 1)
+        third = step_2(third)
         early = early + early_got
         early_got = swap_exact(early, 2, 2)
         second = chip_grads(
+            bits,
             [(mlp_keep, mlp_low_oth)],
             [(grad_upper, grad_upper_oth, 0, g) for g in range(4)],
             [(0, g, rows, [(0, rows, g // 2, g % 2 * rows)]) for g in range(4)],
@@ -1274,28 +1359,9 @@
             shape,
             "grad_hidden_weight",
         )
-
-        grad_attn, second, grad_near, early, early_got = barrier(
-            (grad_attn, half_1(second), grad_near, early, early_got)
-        )
-        grad_far = lax.ppermute(grad_near, "blk", halo_hops())
-        early = early + early_got
-        early_got = swap_exact(early, 4, 2)
-    grad_q, grad_k_own, grad_v_own = attend_backward_own(
-        forward_info, queries, keys, values, grad_attn, HEADS
-    )
-    if fast:
-        grad_q, third, grad_far, early, early_got, ada_got = barrier(
-            (grad_q, third, grad_far, early, early_got, ada_got)
-        )
-        grad_q_oth = swap(grad_q, "dp", 1)
-        second = step_1(second)
-        third = step_2(half_2(third))
-
-        attn_in_keep, grad_q_oth = barrier((attn_in_keep, grad_q_oth))
-        early_row = early + early_got
-        early_pair = pair_up(early_row[None], "dp", core, 1)
+        attn_in_keep, grad_q_oth, second = barrier((attn_in_keep, grad_q_oth, second))
         first = chip_grads(
+            bits,
             [(attn_in_keep, attn_in_oth), (low_keep, mlp_low_oth[width // 2 :])],
             [(grad_q, grad_q_oth, 0, 0), (grad_upper, grad_upper_oth, 0, 4)],
             [(0, 0, rows, [(0, rows, 0, 0)]), (1, 1, rows, [(0, rows, 1, 0)])],
@@ -1305,8 +1371,13 @@
             "grad_query_weight",
         )
 
-        grad_near, first, early_pair = barrier((grad_near, half_1(first), early_pair))
-        early_all = pair_up(early_pair, "dp", y, 2)
+        grad_far, first, second, third, early, early_got = barrier(
+            (grad_far, first, second, third, early, early_got)
+        )
+        second = step_1(second)
+        third = step_3(half_3(third))
+        early = early + early_got
+        early_got = swap_exact(early, 4, 2)
     grad_kv = attend_backward_other(
         backward_info,
         queries,
@@ -1319,24 +1390,28 @@
         HEADS,
     )
     if fast:
-        grad_kv, hidden, second, third, first, early_all = barrier(
-            (grad_kv, hidden, second, third, first, early_all)
-        )
-        grad_kv_oth = swap(grad_kv, "dp", 1)
+        grad_kv, hidden, first, second, third, early, early_got = barrier(
+            (grad_kv, hidden, first, second, third, early, early_got)
+        )
         first = step_1(first)
-        third = step_3(half_3(third))
+        second = step_2(half_2(second))
+        third = step_4(half_4(third))
+        early_row = early + early_got
     grad_tokens, input_sums = input_gradient(
         (grad_q, grad_kv), full_qkv, hidden, grad_after, own_mods
     )
     if fast:
         late = late_message(input_sums)
-        attn_in_keep, grad_kv_oth, third, first, late = barrier(
-            (attn_in_keep, grad_kv_oth, third, first, late)
-        )
-        second = step_2(half_2(second))
-        third = step_4(half_4(third))
+        attn_in_keep, grad_kv, first, second, third, late = barrier(
+            (attn_in_keep, grad_kv, first, second, third, late)
+        )
+        grad_kv_oth = swap(grad_kv, "dp", 1)
         late_got = swap_exact(late, 1, 1)
+        second = step_3(half_3(second))
+        first = step_2(half_2(first))
+        third_sum = add(*third)
         last = chip_grads(
+            bits,
             [(attn_in_keep, attn_in_oth)],
             [(grad_kv, grad_kv_oth, 0, 0), (grad_kv, grad_kv_oth, 0, 1)],
             [(0, 0, rows, [(0, rows, 0, 0)]), (0, 1, rows, [(0, rows, 1, 0)])],
@@ -1346,23 +1421,26 @@
             "grad_key_weight",
         )
 
-        last, second, late, late_got = barrier((half_1(last), second, late, late_got))
+        last, first, second, late, late_got, early_row = barrier(
+            (last, first, second, late, late_got, early_row)
+        )
         last = step_1(last)
-        second = step_3(half_3(second))
         late = late + late_got
         late_got = swap_exact(late, 2, 1)
-
-        last, second, third, late, late_got = barrier((last, second, third, late, late_got))
-        third_sum = add(*third)
-        first = step_2(half_2(first))
         second = step_4(half_4(second))
+        first = step_3(half_3(first))
+
+        last, first, second, late, late_got, early_row = barrier(
+            (last, first, second, late, late_got, early_row)
+        )
         late = late + late_got
         late_got = swap_exact(late, 4, 1)
-
-        last, first, second, late, late_got = barrier((last, first, second, late, late_got))
+        last = step_2(half_2(last))
+        first = step_4(half_4(first))
+        early_pair = pair_up(early_row[None], "dp", core, 1)
         second_sum = add(*second)
-        last = step_2(half_2(last))
-        first = step_3(half_3(first))
+
+        last, first, late, late_got, early_pair = barrier((last, first, late, late_got, early_pair))
         late_row = late + late_got
         ada_rows = jnp.concatenate(
             [jnp.where(y == 0, ada_pair, ada_got), jnp.where(y == 0, ada_got, ada_pair)], axis=0
@@ -1371,19 +1449,26 @@
         row_high = lax.reduce_precision(own_row, 8, 7)
         row_rest = (own_row - row_high).astype(BF)
         part = dot_nt(ada_rows, row_high.astype(BF)) + dot_nt(ada_rows, row_rest)
-        part = pair_up(part[None], "blk", z // 2, 4)
+        parts = [part] + [swap(part, "blk", bit) for bit in (2, 4, 6)]
+        last = step_3(half_3(last))
         late_pair = pair_up(late_row[None], "dp", core, 1)
-
-        last, first, part, late_pair = barrier((last, first, part, late_pair))
-        last = step_3(half_3(last))
-        first = step_4(half_4(first))
-        part = pair_up(part[None], "blk", z % 2, 2)
+        first_sum = add(*first)
+
+        last, parts, late_pair, early_pair = barrier((last, parts, late_pair, early_pair))
+        low = [jnp.where(z % 2 == 0, a, b) for a, b in ((parts[0], parts[1]), (parts[2], parts[3]))]
+        high = [jnp.where(z % 2 == 0, b, a) for a, b in ((parts[0], parts[1]), (parts[2], parts[3]))]
+        line = jnp.stack(
+            [
+                jnp.where(z // 2 == 0, low[0], low[1]),
+                jnp.where(z // 2 == 0, high[0], high[1]),
+                jnp.where(z // 2 == 0, low[1], low[0]),
+                jnp.where(z // 2 == 0, high[1], high[0]),
+            ]
+        )
+        part = pair_up(line[None], "blk", x, 1)
+        last = step_4(half_4(last))
         late_all = pair_up(late_pair, "dp", y, 2)
-
-        last, first, part, late_all = barrier((last, first, part, late_all))
-        first_sum = add(*first)
-        last = step_4(half_4(last))
-        part = pair_up(part[None], "blk", x, 1)
+        early_all = pair_up(early_pair, "dp", y, 2)
         last_sum = add(*last)
 
     if not fast:
@@ -1411,7 +1496,7 @@
     mod_rest = (mod_all - mod_high.astype(F32)).astype(BF)
     grad_ada_weight = dot_nn(silu_own, mod_high) + dot_nn(silu_own, mod_rest)
     if fast:
-        part = part.reshape(2, 2, 2, 4, rows, segs).transpose(5, 3, 2, 1, 0, 4)
+        part = part.reshape(2, 4, 4, rows, segs).transpose(4, 2, 1, 0, 3)
         own_silu = part.reshape(segs, width)
     else:
         silu_grad = dot_nt(ada_weight, mod_high) + dot_nt(ada_weight, mod_rest)
@@ -1447,8 +1532,6 @@
         grad_qkv_weight = scattered(attn_in_t, jnp.concatenate([grad_q, grad_kv], axis=1))
         grad_proj_weight = scattered(in_order(low_keep, low_send), grad_upper[:, 4 * width :])
         grad_hidden_weight = scattered(in_order(mlp_keep, mlp_send), grad_upper[:, : 4 * width])
-        act_send = act_and_lower[: 2 * tokens_dev]
-        grad_lower = act_and_lower[2 * tokens_dev :]
         act = jnp.stack(
             [act_keep.reshape(2, tokens_dev, width), act_send.reshape(2, tokens_dev, width)], axis=1
         ).reshape(4, tokens_dev, width)

time: 626 us -> 608 us (0.971)
  local copies, waits for them, and re-layouts: 59.6 us -> 24.6 us
  Pallas kernels: 213 us -> 240 us
  waiting for transfers between devices: 141 us -> 164 us
  other arithmetic: 63.4 us -> 46.9 us
  starting transfers between devices: 106 us -> 94.1 us
    pallas_call x5 -> x17, Pallas kernels: 64 us -> 112 us  [the longest x4 44.7 us: chip_grads(): pl.pallas_call(body, grid_spec=pltpu.PrefetchScalarGridSpec(num_scalar_pr...]
    ppermute x79 -> x81, waiting for transfers between devices: 107 us -> 149 us  [swap(): return lax.ppermute(v, axis, [(i, i ^ bit) for i in range(count)])]
    squeeze x24 -> x0, local copies, waits for them, and re-layouts: 26.9 us -> none  [the longest x8 15.5 us: split_by(): lax.dynamic_index_in_dim(both, bit, 0, keepdims=False)]
    convert_element_type x20 -> x0, other arithmetic: 20 us -> none  [joined(): return add(*pair).astype(BF)]
    ppermute x1, waiting for transfers between devices: 18.6 us -> 0.01 us  [per_device(): grad_far = lax.ppermute(grad_near, 'blk', halo_hops())]
    pallas_call x1, Pallas kernels: 22 us -> 6.64 us  [attend_backward_other(): pl.pallas_call(body, grid_spec=pltpu.PrefetchScalarGridSpec(num_scalar_pr...]
    ppermute x79 -> x81, starting transfers between devices: 91.4 us -> 85.8 us  [swap(): return lax.ppermute(v, axis, [(i, i ^ bit) for i in range(count)])]
    select_n x26 -> x24, other arithmetic: 15.7 us -> 17.3 us  [pair_up(): jnp.where(bit_value == 0, v, got)]
  transfers between devices with their start and end apart: 82 -> 84, of which waited for: 25 -> 31; matrix products, arithmetic and copies ran while one was open for 22% -> 12% of each run, Pallas kernels for 33% -> 37%
where the time goes in v2:
time: 608 us; the launch traced here: 600 us
  Pallas kernels  240 us (39%)
  waiting for transfers between devices  164 us (27%)
  starting transfers between devices  94.1 us (15%)
  other arithmetic  46.9 us (8%)
  matrix products  27 us (4%)
  local copies, waits for them, and re-layouts  24.6 us (4%)
    ppermute x81, waiting for transfers between devices, swap(): return lax.ppermute(v, axis, [(i, i ^ bit) for i in range(count)])  149 us
    ppermute x81, starting transfers between devices, swap(): return lax.ppermute(v, axis, [(i, i ^ bit) for i in range(count)])  85.8 us
    pallas_call x4, Pallas kernels, chip_grads(): pl.pallas_call(body, grid_spec=pltpu.PrefetchScalarGridSpec(num_scalar_pr...  44.7 us
    pallas_call x12, Pallas kernels, stage_call(): pl.pallas_call(body, grid_spec=pltpu.PrefetchScalarGridSpec(num_scalar_pr...  42 us
    pallas_call x1, Pallas kernels, feed_forward_back(): pl.pallas_call(body, grid=(4,), in_specs=[row, pl.BlockSpec((tokens, widt...  25.3 us
    dot_general x5, matrix products, dot_nn(): lax.dot_general(a, b, (((1,), (0,)), ((), ())), preferred_element_type=F32)  21.8 us
    pallas_call x2, Pallas kernels, unpack_weight(): pl.pallas_call(body, grid_spec=pltpu.PrefetchScalarGridSpec(num_scalar_pr...  20 us
    pallas_call x1, Pallas kernels, attend_backward_own(): pl.pallas_call(body, grid_spec=pltpu.PrefetchScalarGridSpec(num_scalar_pr...  19.8 us
  transfers between devices with their start and end apart: 84, of which 31 were waited for; matrix products, arithmetic and copies ran while one was open for 12% of the time, Pallas kernels for 37%

profile of v2, /device:TPU:0, one launch (start us, length us, event | category | flops | bytes accessed | tf_op | source)
XLA Modules:
  0.0 599.8 jit_solution(1153650627298290386)
XLA Ops:
  3.6 4.0 collective-permute-start.2
  17.9 3.5 collective-permute-start.8
  31.0 2.3 collective-permute-start.3
  36.5 12.4 %collective-permute-done.3 = bf16[288,1152]{1,0:T(8,128)(2,1)S(1)} collective-permute-done((bf16[288,1152]{1,0:T(8,128)(2,1)S(1)}, bf16[288,1152]{1,0:T(8,128)(2,1)S(1)}, u32[]{:S(2)}, u32[]{:S(2)}) %collective-permute-start.3) | collective-permute-done | bytes 663584 | tf_op jit(solution)/shard_map/ppermute | solution.py:39
  49.2 2.3 collective-permute-start.6
  57.1 9.8 %collective-permute-done.6 = bf16[144,1152]{1,0:T(8,128)(2,1)S(1)} collective-permute-done((bf16[144,1152]{1,0:T(8,128)(2,1)S(1)}, bf16[144,1152]{1,0:T(8,128)(2,1)S(1)}, u32[]{:S(2)}, u32[]{:S(2)}) %collective-permute-start.6) | collective-permute-done | bytes 331808 | tf_op jit(solution)/shard_map/ppermute | solution.py:39
  68.5 5.4 collective-permute-done.14
  74.6 5.4 collective-permute-done.15
  85.7 5.0 collective-permute-done.16
  90.6 2.4 collective-permute-start.7
  94.9 7.0 %collective-permute-done.19 = bf16[288,1152]{1,0:T(8,128)(2,1)} collective-permute-done((bf16[288,1152]{1,0:T(8,128)(2,1)S(1)}, bf16[288,1152]{1,0:T(8,128)(2,1)}, u32[]{:S(2)}, u32[]{:S(2)}) %collective-permute-start.19) | collective-permute-done | bytes 663584 | tf_op jit(solution)/shard_map/ppermute | solution.py:39
  103.3 14.3 %collective-permute-done.7.far = bf16[384,1152]{1,0:T(8,128)(2,1)} collective-permute-done((bf16[384,1152]{1,0:T(8,128)(2,1)}, bf16[384,1152]{1,0:T(8,128)(2,1)}, u32[]{:S(2)}, u32[]{:S(2)}) %collective-permute-start.7) | collective-permute-done | bytes 884768 | tf_op jit(solution)/shard_map/ppermute | solution.py:996
  117.6 10.9 %attention_input.1 = (bf16[1152,1152]{1,0:T(8,128)(2,1)}, f32[384,1152]{1,0:T(8,128)}, bf16[576,384]{1,0:T(8,128)(2,1)}, bf16[576,384]{1,0:T(8,128)(2,1)}) custom-call(s32[2]{0:T(128)} %pad_add_fusion.1.core_ref, bf16[384,1152]{1,0:T(8,128)(2,1)} %collective-permute-done.1.near, bf16[384,1152]{1,0:T(8,128)(2,1)} %bitcast.7.own, ...), custom_call_target="tpu_custom_call" | custom-call | flops 11000000512 | bytes 1024 | tf_op jit(solution)/shard_map/attention_input/pallas_call | solution.py:641
  133.9 3.3 collective-permute-start.25
  138.7 12.0 %collective-permute-done.25 = bf16[144,1152]{1,0:T(8,128)(2,1)S(1)} collective-permute-done((bf16[144,1152]{1,0:T(8,128)(2,1)S(1)}, bf16[144,1152]{1,0:T(8,128)(2,1)S(1)}, u32[]{:S(2)}, u32[]{:S(2)}) %collective-permute-start.25) | collective-permute-done | bytes 331808 | tf_op jit(solution)/shard_map/ppermute | solution.py:39
  150.9 3.8 collective-permute-done.24
  156.4 2.5 collective-permute-start.28
  160.7 9.9 %unpack_first.1 = (bf16[1152,3456]{1,0:T(8,128)(2,1)}, bf16[1152,1152]{1,0:T(8,128)(2,1)}) custom-call(s32[1]{0:T(128)} %bitcast.2.core_ref, bf16[1152,1152]{1,0:T(8,128)(2,1)} %copy-done.5, bf16[2,2,288,1152]{3,2,1,0:T(8,128)(2,1)} %bitcast.125, bf16[1152,1152]{1,0:T(8,128)(2,1)} %copy-done.36, bf16[2,2,288,1152]{3,2,1,0:T(8,128)(2,1)} %bitcast.138), custom_call_target="tpu_custom_call" | custom-call | flops 11000000512 | bytes 1024 | tf_op jit(solution)/shard_map/unpack_first/pallas_call | solution.py:118
  170.6 8.1 %fusion.q_ref.q_near.q_far = bf16[1152,1152]{1,0:T(8,128)(2,1)} fusion(bf16[1152,1152]{1,0:T(8,128)(2,1)} %get-tuple-element.258, f32[1152]{0:T(1024)S(1)} %copy-done.32, bf16[1152,3456]{1,0:T(8,128)(2,1)} %get-tuple-element.267.w_ref), kind=kOutput, calls=%fused_computation.4 | convolution fusion | flops 3060301824 | bytes 7967232 | tf_op jit(solution)/shard_map/dot_general | solution.py:26
  178.8 5.2 fusion.1.v_ref
  184.0 5.1 convolution_convert_fusion.k_ref
  199.4 13.1 %attend_forward.1 = (bf16[384,1152]{1,0:T(8,128)(2,1)}, f32[384,1152]{1,0:T(8,128)}, f32[384,128]{1,0:T(8,128)}) custom-call(s32[6]{0:T(128)} %pad_add_fusion.2.info_ref, bf16[1152,1152]{1,0:T(8,128)(2,1)} %fusion.q_ref.q_near.q_far, bf16[1152,1152]{1,0:T(8,128)(2,1)} %convolution_convert_fusion.k_ref, bf16[1152,1152]{1,0:T(8,128)(2,1)} %fusion.1.v_ref), custom_call_target="tpu_custom_call" | custom-call | flops 16499999744 | bytes 1024 | tf_op jit(solution)/shard_map/attend_forward/pallas_call | solution.py:404
  214.2 3.9 collective-permute-start.36
  220.0 8.3 %after_attention.1 = (f32[384,1152]{1,0:T(8,128)}, f32[384,1152]{1,0:T(8,128)}, bf16[384,1152]{1,0:T(8,128)(2,1)}, bf16[576,384]{1,0:T(8,128)(2,1)}, bf16[576,38...) custom-call(s32[2]{0:T(128)} %pad_add_fusion.1.core_ref, bf16[384,1152]{1,0:T(8,128)(2,1)} %get-tuple-element.276.low, ...), custom_call_target="tpu_custom_call" | custom-call | flops 8800000000 | bytes 1024 | tf_op jit(solution)/shard_map/after_attention/pallas_call | solution.py:690
  228.9 10.1 %unpack_hidden.1.wh = bf16[1152,4608]{1,0:T(8,128)(2,1)} custom-call(s32[1]{0:T(128)} %bitcast.2.core_ref, bf16[1152,1152]{1,0:T(8,128)(2,1)} %pad_maximum_fusion.2.a_own, bf16[2,2,288,1152]{3,2,1,0:T(8,128)(2,1)} %bitcast.27.b_own, bf16[1152,1152]{1,0:T(8,128)(2,1)} %collective-permute-done.29.a_oth, bf16[2,2,288,1152]{3,2,1,0:T(8,128)(2,1)} %bitcast.28.b_oth), custom_call_target="tpu_custom_call" | custom-call | flops 11000000512 | bytes 1024 | tf_op jit(solution)/shard_map/unpack_hidden/pallas_call | solution.py:118
  239.7 12.8 %feed_forward_up.1 = (bf16[768,1152]{1,0:T(8,128)(2,1)}, bf16[768,1152]{1,0:T(8,128)(2,1)}, bf16[384,4608]{1,0:T(8,128)(2,1)}) custom-call(s32[4]{0:T(128)} %pad_add_fusion.order_ref, bf16[384,1152]{1,0:T(8,128)(2,1)} %get-tuple-element.284.x, bf16[1152,4608]{1,0:T(8,128)(2,1)} %unpack_hidden.1.wh, f32[8,4608]{1,0:T(8,128)} %broadcast_in_dim.148.bh), custom_call_target="tpu_custom_call" | custom-call | flops 15399999488 | bytes 1024 | tf_op jit(solution)/shard_map/feed_forward_up/pallas_call | solution.py:734
  254.3 2.9 broadcast_select_fusion.7
  259.5 2.8 broadcast_select_fusion.13
  262.5 3.8 collective-permute-done.37.a_oth
  267.8 9.7 %unpack_output.1.wo = bf16[4608,1152]{1,0:T(8,128)(2,1)} custom-call(s32[1]{0:T(128)} %bitcast.2.core_ref, bf16[1152,1152]{1,0:T(8,128)(2,1)} %copy-done.7, bf16[2,2,288,1152]{3,2,1,0:T(8,128)(2,1)} %bitcast.126, bf16[1152,1152]{1,0:T(8,128)(2,1)} %copy-done.39, bf16[2,2,288,1152]{3,2,1,0:T(8,128)(2,1)} %bitcast.139), custom_call_target="tpu_custom_call" | custom-call | flops 11000000512 | bytes 1024 | tf_op jit(solution)/shard_map/unpack_output/pallas_call | solution.py:154
  278.1 13.0 %feed_forward_down.1 = (bf16[384,1152]{1,0:T(8,128)(2,1)}, bf16[384,1152]{1,0:T(8,128)(2,1)}, f32[8,1152]{1,0:T(8,128)}) custom-call(s32[4]{0:T(128)} %pad_add_fusion.order_ref, bf16[768,1152]{1,0:T(8,128)(2,1)} %get-tuple-element.300.keep_ref.refs_0_, bf16[768,1152]{1,0:T(8,128)(2,1)} %get-tuple-element.293.send_ref, bf16[4608,1152]{1,0:T(8,128)(2,1)} %unpack_output.1.wo, ...), custom_call_target="tpu_custom_call" | custom-call | flops 13200000000 | bytes 1024 | tf_op jit(solution)/shard_map/feed_forward_down/pallas_call | solution.py:794
  295.1 12.2 %grad_output_weight.1 = (bf16[576,1152]{1,0:T(8,128)(2,1)}, bf16[576,1152]{1,0:T(8,128)(2,1)}, bf16[2,288,1152]{2,1,0:T(8,128)(2,1)}, bf16[2,288,1152]{2,1,0:T(8,128)(2,1)}) custom-call(s32[4]{0:T(128)} %pad_add_fusion.3.bits_ref, bf16[768,1152]{1,0:T(8,128)(2,1)} %get-tuple-element.300.keep_ref.refs_0_, bf16[768,1152]{1,0:T(8,128)(2,1)} %collective-permute-done.39.refs_1_, ...), custom_call_target="tpu_custom_call" | custom-call | flops 11000000512 | bytes 1024 | tf_op jit(solution)/shard_map/grad_output_weight/pallas_call | solution.py:229
  309.0 25.3 %feed_forward_back.1 = (bf16[384,5760]{1,0:T(8,128)(2,1)}, f32[384,1152]{1,0:T(8,128)}, bf16[384,1280]{1,0:T(8,128)(2,1)}, f32[8,4608]{1,0:T(8,128)}, f32[8,3456]{1,0:T(8,128)}) custom-call(bf16[384,1152]{1,0:T(8,128)(2,1)} %get-tuple-element.307.refs_2_.gl, bf16[384,4608]{1,0:T(8,128)(2,1)} %get-tuple-element.308.sl, bf16[1152,4608]{1,0:T(8,128)(2,1)} %unpack_hidden.1.wh, ...), custom_call_target="tpu_custom_call" | custom-call | flops 26400000000 | bytes 1024 | tf_op jit(solution)/shard_map/feed_forward_back/pallas_call | solution.py:902
  341.7 19.8 %attend_backward_own.1 = (bf16[384,1152]{1,0:T(8,128)(2,1)}, f32[384,1152]{1,0:T(8,128)}, f32[384,1152]{1,0:T(8,128)}) custom-call(s32[6]{0:T(128)} %pad_add_fusion.2.info_ref, bf16[1152,1152]{1,0:T(8,128)(2,1)} %fusion.q_ref.q_near.q_far, bf16[1152,1152]{1,0:T(8,128)(2,1)} %convolution_convert_fusion.k_ref, bf16[1152,1152]{1,0:T(8,128)(2,1)} %fusion.1.v_ref, ...), custom_call_target="tpu_custom_call" | custom-call | flops 26400000000 | bytes 1024 | tf_op jit(solution)/shard_map/attend_backward_own/pallas_call | solution.py:494
  361.6 4.9 add_and_cut.4
  367.2 7.2 %collective-permute-start.50 = (bf16[16,4608]{1,0:T(8,128)(2,1)S(1)}, bf16[16,4608]{1,0:T(8,128)(2,1)S(1)}, u32[]{:S(2)}, u32[]{:S(2)}) collective-permute-start(bf16[16,4608]{1,0:T(8,128)(2,1)S(1)} %pad_maximum_fusion.35), channel_id=1, source_target_pairs={{0,2},{1,3},{2,0},{3,1},{4,6},{5,7},{6,4},{7,5},{8,10},{9,11},{10,... | collective-permute-start | bytes 442376 | tf_op jit(solution)/shard_map/ppermute | solution.py:39
  374.4 2.4 collective-permute-start.46
  377.1 15.0 %grad_hidden_weight.1 = (bf16[576,1152]{1,0:T(8,128)(2,1)}, bf16[576,1152]{1,0:T(8,128)(2,1)}, bf16[2,288,1152]{2,1,0:T(8,128)(2,1)}, bf16[2,288,1152]{2,1,0:T(8,128)(2,1)}) custom-call(s32[4]{0:T(128)} %pad_add_fusion.3.bits_ref, bf16[576,384]{1,0:T(8,128)(2,1)} %get-tuple-element.336.refs_0_, bf16[1152,384]{1,0:T(8,128)(2,1)} %copy-done.21, ...), custom_call_target="tpu_custom_call" | custom-call | flops 11000000512 | bytes 1024 | tf_op jit(solution)/shard_map/grad_hidden_weight/pallas_call | solution.py:229
  392.3 8.9 %grad_query_weight.1 = (bf16[288,1152]{1,0:T(8,128)(2,1)}, bf16[288,1152]{1,0:T(8,128)(2,1)}, bf16[2,144,1152]{2,1,0:T(8,128)(2,1)}, bf16[2,144,1152]{2,1,0:T(8,128)(2,1)}) custom-call(s32[4]{0:T(128)} %pad_add_fusion.3.bits_ref, bf16[576,384]{1,0:T(8,128)(2,1)} %get-tuple-element.401.refs_0_, bf16[576,384]{1,0:T(8,128)(2,1)} %get-tuple-element.344.refs_1_, ...), custom_call_target="tpu_custom_call" | custom-call | flops 11000000512 | bytes 1024 | tf_op jit(solution)/shard_map/grad_query_weight/pallas_call | solution.py:229
  402.3 3.2 collective-permute-start.54
  405.5 3.8 add_and_cut_z.4
  411.1 6.6 %attend_backward_other.1.gkv.refs_2_.refs_3_ = bf16[384,2304]{1,0:T(8,128)(2,1)} custom-call(s32[10]{0:T(128)} %pad_add_fusion.4.info_ref, bf16[1152,1152]{1,0:T(8,128)(2,1)} %fusion.q_ref.q_near.q_far, bf16[1152,1152]{1,0:T(8,128)(2,1)} %fusion.q_ref.q_near.q_far, bf16[1152,1152]{1,0:T(8,128)(2,1)} %convolution_convert_fusion.k_ref, ...), custom_call_target="tpu_custom_call" | custom-call | flops 24199999488 | bytes 1024 | tf_op jit(solution)/shard_map/attend_backward_other/pallas_call | solution.py:551
  417.9 8.7 %collective-permute-done.53.other = bf16[288,1152]{1,0:T(8,128)(2,1)} collective-permute-done((bf16[288,1152]{1,0:T(8,128)(2,1)}, bf16[288,1152]{1,0:T(8,128)(2,1)}, u32[]{:S(2)}, u32[]{:S(2)}) %collective-permute-start.53) | collective-permute-done | bytes 663584 | tf_op jit(solution)/shard_map/ppermute | solution.py:39
  426.6 14.1 %collective-permute-done.51.a_got = bf16[576,1152]{1,0:T(8,128)(2,1)} collective-permute-done((bf16[576,1152]{1,0:T(8,128)(2,1)S(1)}, bf16[576,1152]{1,0:T(8,128)(2,1)}, u32[]{:S(2)}, u32[]{:S(2)}) %collective-permute-start.51) | collective-permute-done | bytes 1327136 | tf_op jit(solution)/shard_map/ppermute | solution.py:39
  440.8 5.0 add_and_cut.5
  449.9 14.0 %input_gradient.1 = (f32[384,1152]{1,0:T(8,128)}, f32[8,2304]{1,0:T(8,128)}) custom-call(bf16[384,1152]{1,0:T(8,128)(2,1)} %get-tuple-element.333.refs_4_.gq, bf16[384,2304]{1,0:T(8,128)(2,1)} %attend_backward_other.1.gkv.refs_2_.refs_3_, bf16[1152,3456]{1,0:T(8,128)(2,1)} %get-tuple-element.267.w_ref, f32[384,1152]{1,0:T(8,128)} %get-tuple-element.381.hid, ...), custom_call_target="tpu_custom_call" | custom-call | flops 15399999488 | bytes 1024 | tf_op jit(solution)/shard_map/input_gradient/pallas_call | solution.py:973
  463.9 3.3 add_and_cut_last.4
  469.6 13.4 %collective-permute-done.59 = bf16[144,1152]{1,0:T(8,128)(2,1)S(1)} collective-permute-done((bf16[144,1152]{1,0:T(8,128)(2,1)}, bf16[144,1152]{1,0:T(8,128)(2,1)S(1)}, u32[]{:S(2)}, u32[]{:S(2)}) %collective-permute-start.59) | collective-permute-done | bytes 331808 | tf_op jit(solution)/shard_map/ppermute | solution.py:39
  484.9 3.7 add_and_cut_z.5
  488.6 3.6 add_and_cut.6
  494.9 8.7 %grad_key_weight.1 = (bf16[288,1152]{1,0:T(8,128)(2,1)}, bf16[288,1152]{1,0:T(8,128)(2,1)}, bf16[2,144,1152]{2,1,0:T(8,128)(2,1)}, bf16[2,144,1152]{2,1,0:T(8,128)(2,1)}) custom-call(s32[4]{0:T(128)} %pad_add_fusion.3.bits_ref, bf16[576,384]{1,0:T(8,128)(2,1)} %get-tuple-element.401.refs_0_, bf16[576,384]{1,0:T(8,128)(2,1)} %copy-done.52, ...), custom_call_target="tpu_custom_call" | custom-call | flops 11000000512 | bytes 1024 | tf_op jit(solution)/shard_map/grad_key_weight/pallas_call | solution.py:229
  503.6 2.6 collective-permute-done.63.other
  507.0 2.9 add_and_cut_last.5
  511.2 3.0 add_and_cut_z.6
  516.8 11.0 %collective-permute-done.68 = bf16[144,1152]{1,0:T(8,128)(2,1)S(1)} collective-permute-done((bf16[144,1152]{1,0:T(8,128)(2,1)}, bf16[144,1152]{1,0:T(8,128)(2,1)S(1)}, u32[]{:S(2)}, u32[]{:S(2)}) %collective-permute-start.68) | collective-permute-done | bytes 331808 | tf_op jit(solution)/shard_map/ppermute | solution.py:39
  534.2 2.5 add_and_cut_last.6
  537.6 3.5 add_and_cut.7
  544.6 2.5 collective-permute-done.72
  547.1 3.4 collective-permute-done.70.a_got
  557.1 3.2 add_and_cut_z.7
  561.3 9.3 %collective-permute-done.75.other = bf16[144,1152]{1,0:T(8,128)(2,1)S(1)} collective-permute-done((bf16[144,1152]{1,0:T(8,128)(2,1)}, bf16[144,1152]{1,0:T(8,128)(2,1)S(1)}, u32[]{:S(2)}, u32[]{:S(2)}) %collective-permute-start.75) | collective-permute-done | bytes 331808 | tf_op jit(solution)/shard_map/ppermute | solution.py:39
  574.1 2.5 add_and_cut_last.7
  579.4 6.6 %collective-permute-done.83 = bf16[72,1152]{1,0:T(8,128)(2,1)S(1)} collective-permute-done((bf16[72,1152]{1,0:T(8,128)(2,1)}, bf16[72,1152]{1,0:T(8,128)(2,1)S(1)}, u32[]{:S(2)}, u32[]{:S(2)}) %collective-permute-start.83) | collective-permute-done | bytes 165920 | tf_op jit(solution)/shard_map/ppermute | solution.py:39
  586.9 3.7 collective-permute-done.81
  (500 shorter events, 140.9 us)
Async XLA Ops:
  3.6 26.2 %collective-permute-start.2 = (bf16[144,1152]{1,0:T(8,128)(2,1)}, bf16[144,1152]{1,0:T(8,128)(2,1)}, u32[]{:S(2)}, u32[]{:S(2)}) collective-permute-start(bf16[144,1152]{1,0:T(8,128)(2,1)} %pad_maximum_fusion.25), channel_id=1, source_target_pairs={{0,4},{1,5},{2,6},{3,7},{4,0},{5,1},{6,2},{7,3},{8,12},{9,13},{10,... | collective-permute-start | bytes 995336 | tf_op jit(solution)/shard_map/ppermute | solution.py:39
  9.1 13.7 %collective-permute-start.9 = (bf16[12,1152]{1,0:T(8,128)(2,1)S(1)}, bf16[12,1152]{1,0:T(8,128)(2,1)S(1)}, u32[]{:S(2)}, u32[]{:S(2)}) collective-permute-start(bf16[12,1152]{1,0:T(8,128)(2,1)S(1)} %get-tuple-element.666), channel_id=1, source_target_pairs={{0,8},{8,0},{16,24},{24,16},{1,9},{9,1},{17,25},{25,17},{2,10},{10... | collective-permute-start | bytes 82952 | tf_op jit(solution)/shard_map/ppermute | solution.py:39
  9.1 24.3 %collective-permute-start.13 = (bf16[1,36,6912]{2,1,0:T(8,128)(2,1)}, bf16[1,36,6912]{2,1,0:T(8,128)(2,1)}, u32[]{:S(2)}, u32[]{:S(2)}) collective-permute-start(bf16[1,36,6912]{2,1,0:T(8,128)(2,1)} %bitcast.136), channel_id=1, source_target_pairs={{0,8},{8,0},{16,24},{24,16},{1,9},{9,1},{17,25},{25,17},{2,10},{10... | collective-permute-start | bytes 1493000 | tf_op jit(solution)/shard_map/ppermute | solution.py:39
  22.2 63.0 %collective-permute-start.1 = (bf16[384,1152]{1,0:T(8,128)(2,1)}, bf16[384,1152]{1,0:T(8,128)(2,1)}, u32[]{:S(2)}, u32[]{:S(2)}) collective-permute-start(bf16[384,1152]{1,0:T(8,128)(2,1)} %bitcast.7.own), channel_id=1, source_target_pairs={{0,1},{1,0},{2,3},{3,2},{4,5},{5,4},{6,7},{7,6},{8,9},{9,8},{10,11... | collective-permute-start | bytes 2654216 | tf_op jit(solution)/shard_map/ppermute | solution.py:39
  31.0 17.9 %collective-permute-start.3 = (bf16[288,1152]{1,0:T(8,128)(2,1)S(1)}, bf16[288,1152]{1,0:T(8,128)(2,1)S(1)}, u32[]{:S(2)}, u32[]{:S(2)}) collective-permute-start(bf16[288,1152]{1,0:T(8,128)(2,1)S(1)} %pad_maximum_fusion.19), channel_id=1, source_target_pairs={{0,2},{1,3},{2,0},{3,1},{4,6},{5,7},{6,4},{7,5},{8,10},{9,11},{10,... | collective-permute-start | bytes 1990664 | tf_op jit(solution)/shard_map/ppermute | solution.py:39
  34.9 18.4 %collective-permute-start.12 = (bf16[16,6912]{1,0:T(8,128)(2,1)S(1)}, bf16[16,6912]{1,0:T(8,128)(2,1)S(1)}, u32[]{:S(2)}, u32[]{:S(2)}) collective-permute-start(bf16[16,6912]{1,0:T(8,128)(2,1)S(1)} %fusion.15), channel_id=1, source_target_pairs={{0,16},{8,24},{16,0},{24,8},{1,17},{9,25},{17,1},{25,9},{2,18},{10... | collective-permute-start | bytes 663560 | tf_op jit(solution)/shard_map/ppermute | solution.py:39
  49.2 17.6 %collective-permute-start.6 = (bf16[144,1152]{1,0:T(8,128)(2,1)S(1)}, bf16[144,1152]{1,0:T(8,128)(2,1)S(1)}, u32[]{:S(2)}, u32[]{:S(2)}) collective-permute-start(bf16[144,1152]{1,0:T(8,128)(2,1)S(1)} %pad_maximum_fusion.26), channel_id=1, source_target_pairs={{0,4},{1,5},{2,6},{3,7},{4,0},{5,1},{6,2},{7,3},{8,12},{9,13},{10,... | collective-permute-start | bytes 995336 | tf_op jit(solution)/shard_map/ppermute | solution.py:39
  51.7 29.3 %collective-permute-start.5 = (bf16[288,1152]{1,0:T(8,128)(2,1)S(1)}, bf16[288,1152]{1,0:T(8,128)(2,1)S(1)}, u32[]{:S(2)}, u32[]{:S(2)}) collective-permute-start(bf16[288,1152]{1,0:T(8,128)(2,1)S(1)} %bitcast.128), channel_id=1, source_target_pairs={{0,16},{8,24},{16,0},{24,8},{1,17},{9,25},{17,1},{25,9},{2,18},{10... | collective-permute-start | bytes 1990664 | tf_op jit(solution)/shard_map/ppermute | solution.py:39
  53.3 27.9 %collective-permute-start.4 = (bf16[288,1152]{1,0:T(8,128)(2,1)S(1)}, bf16[288,1152]{1,0:T(8,128)(2,1)S(1)}, u32[]{:S(2)}, u32[]{:S(2)}) collective-permute-start(bf16[288,1152]{1,0:T(8,128)(2,1)S(1)} %bitcast.127), channel_id=1, source_target_pairs={{0,1},{1,0},{2,3},{3,2},{4,5},{5,4},{6,7},{7,6},{8,9},{9,8},{10,11... | collective-permute-start | bytes 1990664 | tf_op jit(solution)/shard_map/ppermute | solution.py:39
  53.3 20.6 %collective-permute-start.14 = (bf16[16,6912]{1,0:T(8,128)(2,1)S(1)}, bf16[16,6912]{1,0:T(8,128)(2,1)S(1)}, u32[]{:S(2)}, u32[]{:S(2)}) collective-permute-start(bf16[16,6912]{1,0:T(8,128)(2,1)S(1)} %bitcast_add_fusion), channel_id=1, source_target_pairs={{0,1},{1,0},{2,3},{3,2},{4,5},{5,4},{6,7},{7,6},{8,9},{9,8},{10,11... | collective-permute-start | bytes 663560 | tf_op jit(solution)/shard_map/ppermute | solution.py:39
  66.9 66.0 %collective-permute-start.20 = (bf16[2,36,6912]{2,0,1:T(2,128)(2,1)}, bf16[2,36,6912]{2,0,1:T(2,128)(2,1)}, u32[]{:S(2)}, u32[]{:S(2)}) collective-permute-start(bf16[2,36,6912]{2,0,1:T(2,128)(2,1)} %copy.52), channel_id=1, source_target_pairs={{0,16},{8,24},{16,0},{24,8},{1,17},{9,25},{17,1},{25,9},{2,18},{10... | collective-permute-start | bytes 2985992 | tf_op jit(solution)/shard_map/ppermute | solution.py:39
  80.0 10.6 %collective-permute-start.16 = (bf16[16,6912]{1,0:T(8,128)(2,1)S(1)}, bf16[16,6912]{1,0:T(8,128)(2,1)S(1)}, u32[]{:S(2)}, u32[]{:S(2)}) collective-permute-start(bf16[16,6912]{1,0:T(8,128)(2,1)S(1)} %add_convert_fusion), channel_id=1, source_target_pairs={{0,4},{1,5},{2,6},{3,7},{4,0},{5,1},{6,2},{7,3},{8,12},{9,13},{10,... | collective-permute-start | bytes 663560 | tf_op jit(solution)/shard_map/ppermute | solution.py:39
  83.1 18.9 %collective-permute-start.19 = (bf16[288,1152]{1,0:T(8,128)(2,1)S(1)}, bf16[288,1152]{1,0:T(8,128)(2,1)}, u32[]{:S(2)}, u32[]{:S(2)}) collective-permute-start(bf16[288,1152]{1,0:T(8,128)(2,1)S(1)} %pad_maximum_fusion.20), channel_id=1, source_target_pairs={{0,2},{1,3},{2,0},{3,1},{4,6},{5,7},{6,4},{7,5},{8,10},{9,11},{10,... | collective-permute-start | bytes 1990664 | tf_op jit(solution)/shard_map/ppermute | solution.py:39
  84.6 43.9 %collective-permute-start.18 = (bf16[576,1152]{1,0:T(8,128)(2,1)}, bf16[576,1152]{1,0:T(8,128)(2,1)}, u32[]{:S(2)}, u32[]{:S(2)}) collective-permute-start(bf16[576,1152]{1,0:T(8,128)(2,1)} %get-tuple-element.256), channel_id=1, source_target_pairs={{0,1},{1,0},{2,3},{3,2},{4,5},{5,4},{6,7},{7,6},{8,9},{9,8},{10,11... | collective-permute-start | bytes 3981320 | tf_op jit(solution)/shard_map/ppermute | solution.py:39
  85.2 45.3 %collective-permute-start.17 = (bf16[576,1152]{1,0:T(8,128)(2,1)}, bf16[576,1152]{1,0:T(8,128)(2,1)}, u32[]{:S(2)}, u32[]{:S(2)}) collective-permute-start(bf16[576,1152]{1,0:T(8,128)(2,1)} %get-tuple-element.255), channel_id=1, source_target_pairs={{0,16},{8,24},{16,0},{24,8},{1,17},{9,25},{17,1},{25,9},{2,18},{10... | collective-permute-start | bytes 3981320 | tf_op jit(solution)/shard_map/ppermute | solution.py:39
  90.6 27.0 %collective-permute-start.7 = (bf16[384,1152]{1,0:T(8,128)(2,1)}, bf16[384,1152]{1,0:T(8,128)(2,1)}, u32[]{:S(2)}, u32[]{:S(2)}) collective-permute-start(bf16[384,1152]{1,0:T(8,128)(2,1)} %collective-permute-done.1.near), channel_id=1, source_target_pairs={{0,2},{2,4},{4,6},{3,1},{5,3},{7,5},{8,10},{10,12},{12,14},{11,9},... | collective-permute-start | bytes 2654216 | tf_op jit(solution)/shard_map/ppermute | solution.py:996
  133.9 16.8 %collective-permute-start.25 = (bf16[144,1152]{1,0:T(8,128)(2,1)S(1)}, bf16[144,1152]{1,0:T(8,128)(2,1)S(1)}, u32[]{:S(2)}, u32[]{:S(2)}) collective-permute-start(bf16[144,1152]{1,0:T(8,128)(2,1)S(1)} %copy-done.18), channel_id=1, source_target_pairs={{0,4},{1,5},{2,6},{3,7},{4,0},{5,1},{6,2},{7,3},{8,12},{9,13},{10,... | collective-permute-start | bytes 995336 | tf_op jit(solution)/shard_map/ppermute | solution.py:39
  137.2 19.2 %collective-permute-start.21 = (bf16[1152,1152]{1,0:T(8,128)(2,1)S(1)}, bf16[1152,1152]{1,0:T(8,128)(2,1)S(1)}, u32[]{:S(2)}, u32[]{:S(2)}) collective-permute-start(bf16[1152,1152]{1,0:T(8,128)(2,1)S(1)} %pad_maximum_fusion.a_own), channel_id=1, source_target_pairs={{0,8},{8,0},{16,24},{24,16},{1,9},{9,1},{17,25},{25,17},{2,10},{10... | collective-permute-start | bytes 7962632 | tf_op jit(solution)/shard_map/ppermute | solution.py:39
  137.2 19.2 %collective-permute-start.22 = (bf16[1152,1152]{1,0:T(8,128)(2,1)S(1)}, bf16[1152,1152]{1,0:T(8,128)(2,1)S(1)}, u32[]{:S(2)}, u32[]{:S(2)}) collective-permute-start(bf16[1152,1152]{1,0:T(8,128)(2,1)S(1)} %pad_maximum_fusion.1), channel_id=1, source_target_pairs={{0,8},{8,0},{16,24},{24,16},{1,9},{9,1},{17,25},{25,17},{2,10},{10... | collective-permute-start | bytes 7962632 | tf_op jit(solution)/shard_map/ppermute | solution.py:39
  137.8 16.9 %collective-permute-start.24 = (bf16[288,1152]{1,0:T(8,128)(2,1)S(1)}, bf16[288,1152]{1,0:T(8,128)(2,1)S(1)}, u32[]{:S(2)}, u32[]{:S(2)}) collective-permute-start(bf16[288,1152]{1,0:T(8,128)(2,1)S(1)} %bitcast.132), channel_id=1, source_target_pairs={{0,16},{8,24},{16,0},{24,8},{1,17},{9,25},{17,1},{25,9},{2,18},{10... | collective-permute-start | bytes 1990664 | tf_op jit(solution)/shard_map/ppermute | solution.py:39
  138.4 16.6 %collective-permute-start.23 = (bf16[288,1152]{1,0:T(8,128)(2,1)S(1)}, bf16[288,1152]{1,0:T(8,128)(2,1)S(1)}, u32[]{:S(2)}, u32[]{:S(2)}) collective-permute-start(bf16[288,1152]{1,0:T(8,128)(2,1)S(1)} %bitcast.130), channel_id=1, source_target_pairs={{0,1},{1,0},{2,3},{3,2},{4,5},{5,4},{6,7},{7,6},{8,9},{9,8},{10,11... | collective-permute-start | bytes 1990664 | tf_op jit(solution)/shard_map/ppermute | solution.py:39
  156.4 32.7 %collective-permute-start.28 = (bf16[288,1152]{1,0:T(8,128)(2,1)S(1)}, bf16[288,1152]{1,0:T(8,128)(2,1)S(1)}, u32[]{:S(2)}, u32[]{:S(2)}) collective-permute-start(bf16[288,1152]{1,0:T(8,128)(2,1)S(1)} %pad_maximum_fusion.21), channel_id=1, source_target_pairs={{0,2},{1,3},{2,0},{3,1},{4,6},{5,7},{6,4},{7,5},{8,10},{9,11},{10,... | collective-permute-start | bytes 1990664 | tf_op jit(solution)/shard_map/ppermute | solution.py:39
  158.9 30.4 %collective-permute-start.27 = (bf16[576,1152]{1,0:T(8,128)(2,1)S(1)}, bf16[576,1152]{1,0:T(8,128)(2,1)}, u32[]{:S(2)}, u32[]{:S(2)}) collective-permute-start(bf16[576,1152]{1,0:T(8,128)(2,1)S(1)} %pad_maximum_fusion.13), channel_id=1, source_target_pairs={{0,1},{1,0},{2,3},{3,2},{4,5},{5,4},{6,7},{7,6},{8,9},{9,8},{10,11... | collective-permute-start | bytes 3981320 | tf_op jit(solution)/shard_map/ppermute | solution.py:39
  159.2 33.5 %collective-permute-start.26 = (bf16[576,1152]{1,0:T(8,128)(2,1)}, bf16[576,1152]{1,0:T(8,128)(2,1)}, u32[]{:S(2)}, u32[]{:S(2)}) collective-permute-start(bf16[576,1152]{1,0:T(8,128)(2,1)} %pad_maximum_fusion.12), channel_id=1, source_target_pairs={{0,16},{8,24},{16,0},{24,8},{1,17},{9,25},{17,1},{25,9},{2,18},{10... | collective-permute-start | bytes 3981320 | tf_op jit(solution)/shard_map/ppermute | solution.py:39
  196.5 16.1 %collective-permute-start.32 = (bf16[288,1152]{1,0:T(8,128)(2,1)S(1)}, bf16[288,1152]{1,0:T(8,128)(2,1)S(1)}, u32[]{:S(2)}, u32[]{:S(2)}) collective-permute-start(bf16[288,1152]{1,0:T(8,128)(2,1)S(1)} %bitcast.131), channel_id=1, source_target_pairs={{0,16},{8,24},{16,0},{24,8},{1,17},{9,25},{17,1},{25,9},{2,18},{10... | collective-permute-start | bytes 1990664 | tf_op jit(solution)/shard_map/ppermute | solution.py:39
  197.2 15.6 %collective-permute-start.31 = (bf16[288,1152]{1,0:T(8,128)(2,1)S(1)}, bf16[288,1152]{1,0:T(8,128)(2,1)S(1)}, u32[]{:S(2)}, u32[]{:S(2)}) collective-permute-start(bf16[288,1152]{1,0:T(8,128)(2,1)S(1)} %bitcast.129), channel_id=1, source_target_pairs={{0,1},{1,0},{2,3},{3,2},{4,5},{5,4},{6,7},{7,6},{8,9},{9,8},{10,11... | collective-permute-start | bytes 1990664 | tf_op jit(solution)/shard_map/ppermute | solution.py:39
  198.9 15.3 %collective-permute-start.29 = (bf16[1152,1152]{1,0:T(8,128)(2,1)}, bf16[1152,1152]{1,0:T(8,128)(2,1)}, u32[]{:S(2)}, u32[]{:S(2)}) collective-permute-start(bf16[1152,1152]{1,0:T(8,128)(2,1)} %pad_maximum_fusion.2.a_own), channel_id=1, source_target_pairs={{0,8},{8,0},{16,24},{24,16},{1,9},{9,1},{17,25},{25,17},{2,10},{10... | collective-permute-start | bytes 7962632 | tf_op jit(solution)/shard_map/ppermute | solution.py:39
  198.9 15.3 %collective-permute-start.30 = (bf16[1152,1152]{1,0:T(8,128)(2,1)}, bf16[1152,1152]{1,0:T(8,128)(2,1)}, u32[]{:S(2)}, u32[]{:S(2)}) collective-permute-start(bf16[1152,1152]{1,0:T(8,128)(2,1)} %pad_maximum_fusion.3), channel_id=1, source_target_pairs={{0,8},{8,0},{16,24},{24,16},{1,9},{9,1},{17,25},{25,17},{2,10},{10... | collective-permute-start | bytes 7962632 | tf_op jit(solution)/shard_map/ppermute | solution.py:39
  214.2 38.3 %collective-permute-start.36 = (bf16[576,1152]{1,0:T(8,128)(2,1)S(1)}, bf16[576,1152]{1,0:T(8,128)(2,1)}, u32[]{:S(2)}, u32[]{:S(2)}) collective-permute-start(bf16[576,1152]{1,0:T(8,128)(2,1)S(1)} %pad_maximum_fusion.16), channel_id=1, source_target_pairs={{0,1},{1,0},{2,3},{3,2},{4,5},{5,4},{6,7},{7,6},{8,9},{9,8},{10,11... | collective-permute-start | bytes 3981320 | tf_op jit(solution)/shard_map/ppermute | solution.py:39
  218.1 36.2 %collective-permute-start.35 = (bf16[576,1152]{1,0:T(8,128)(2,1)}, bf16[576,1152]{1,0:T(8,128)(2,1)}, u32[]{:S(2)}, u32[]{:S(2)}) collective-permute-start(bf16[576,1152]{1,0:T(8,128)(2,1)} %pad_maximum_fusion.15), channel_id=1, source_target_pairs={{0,16},{8,24},{16,0},{24,8},{1,17},{9,25},{17,1},{25,9},{2,18},{10... | collective-permute-start | bytes 3981320 | tf_op jit(solution)/shard_map/ppermute | solution.py:39
  228.4 10.6 %collective-permute-start.34 = (bf16[1152,384]{1,0:T(8,128)(2,1)}, bf16[1152,384]{1,0:T(8,128)(2,1)S(1)}, u32[]{:S(2)}, u32[]{:S(2)}) collective-permute-start(bf16[1152,384]{1,0:T(8,128)(2,1)} %get-tuple-element.283), channel_id=1, source_target_pairs={{0,8},{8,0},{16,24},{24,16},{1,9},{9,1},{17,25},{25,17},{2,10},{10... | collective-permute-start | bytes 2654216 | tf_op jit(solution)/shard_map/ppermute | solution.py:39
  228.4 10.6 %collective-permute-start.33 = (bf16[576,384]{1,0:T(8,128)(2,1)}, bf16[576,384]{1,0:T(8,128)(2,1)S(1)}, u32[]{:S(2)}, u32[]{:S(2)}) collective-permute-start(bf16[576,384]{1,0:T(8,128)(2,1)} %get-tuple-element.282), channel_id=1, source_target_pairs={{0,8},{8,0},{16,24},{24,16},{1,9},{9,1},{17,25},{25,17},{2,10},{10... | collective-permute-start | bytes 1327112 | tf_op jit(solution)/shard_map/ppermute | solution.py:39
  262.4 32.7 %collective-permute-start.39 = (bf16[768,1152]{1,0:T(8,128)(2,1)}, bf16[768,1152]{1,0:T(8,128)(2,1)}, u32[]{:S(2)}, u32[]{:S(2)}) collective-permute-start(bf16[768,1152]{1,0:T(8,128)(2,1)} %get-tuple-element.293.send_ref), channel_id=1, source_target_pairs={{0,8},{8,0},{16,24},{24,16},{1,9},{9,1},{17,25},{25,17},{2,10},{10... | collective-permute-start | bytes 5308424 | tf_op jit(solution)/shard_map/ppermute | solution.py:39
  307.3 31.6 %collective-permute-start.41 = (bf16[576,1152]{1,0:T(8,128)(2,1)}, bf16[576,1152]{1,0:T(8,128)(2,1)S(1)}, u32[]{:S(2)}, u32[]{:S(2)}) collective-permute-start(bf16[576,1152]{1,0:T(8,128)(2,1)} %get-tuple-element.315), channel_id=1, source_target_pairs={{0,16},{8,24},{16,0},{24,8},{1,17},{9,25},{17,1},{25,9},{2,18},{10... | collective-permute-start | bytes 3981320 | tf_op jit(solution)/shard_map/ppermute | solution.py:39
  308.0 31.4 %collective-permute-start.42 = (bf16[576,1152]{1,0:T(8,128)(2,1)}, bf16[576,1152]{1,0:T(8,128)(2,1)}, u32[]{:S(2)}, u32[]{:S(2)}) collective-permute-start(bf16[576,1152]{1,0:T(8,128)(2,1)} %bitcast.141), channel_id=1, source_target_pairs={{0,1},{1,0},{2,3},{3,2},{4,5},{5,4},{6,7},{7,6},{8,9},{9,8},{10,11... | collective-permute-start | bytes 3981320 | tf_op jit(solution)/shard_map/ppermute | solution.py:39
  339.5 27.5 %collective-permute-start.44 = (bf16[384,5760]{1,0:T(8,128)(2,1)}, bf16[384,5760]{1,0:T(8,128)(2,1)}, u32[]{:S(2)}, u32[]{:S(2)}) collective-permute-start(bf16[384,5760]{1,0:T(8,128)(2,1)} %get-tuple-element.323.refs_2_.refs_3_.refs_4_.refs_5_), channel_id=1, source_target_pairs={{0,8},{8,0},{16,24},{24,16},{1,9},{9,1},{17,25},{25,17},{2,10},{10... | collective-permute-start | bytes 13271048 | tf_op jit(solution)/shard_map/ppermute | solution.py:39
  339.6 26.8 %collective-permute-start.45 = (bf16[16,4608]{1,0:T(8,128)(2,1)S(1)}, bf16[16,4608]{1,0:T(8,128)(2,1)S(1)}, u32[]{:S(2)}, u32[]{:S(2)}) collective-permute-start(bf16[16,4608]{1,0:T(8,128)(2,1)S(1)} %pad_maximum_fusion.34), channel_id=1, source_target_pairs={{0,1},{1,0},{2,3},{3,2},{4,5},{5,4},{6,7},{7,6},{8,9},{9,8},{10,11... | collective-permute-start | bytes 442376 | tf_op jit(solution)/shard_map/ppermute | solution.py:39
  340.5 26.5 %collective-permute-start.43 = (bf16[384,1280]{1,0:T(8,128)(2,1)}, bf16[384,1280]{1,0:T(8,128)(2,1)S(1)}, u32[]{:S(2)}, u32[]{:S(2)}) collective-permute-start(bf16[384,1280]{1,0:T(8,128)(2,1)} %get-tuple-element.321.g_ref), channel_id=1, source_target_pairs={{0,1},{1,0},{2,3},{3,2},{4,5},{5,4},{6,7},{7,6},{8,9},{9,8},{10,11... | collective-permute-start | bytes 2949128 | tf_op jit(solution)/shard_map/ppermute | solution.py:39
  367.2 24.9 %collective-permute-start.50 = (bf16[16,4608]{1,0:T(8,128)(2,1)S(1)}, bf16[16,4608]{1,0:T(8,128)(2,1)S(1)}, u32[]{:S(2)}, u32[]{:S(2)}) collective-permute-start(bf16[16,4608]{1,0:T(8,128)(2,1)S(1)} %pad_maximum_fusion.35), channel_id=1, source_target_pairs={{0,2},{1,3},{2,0},{3,1},{4,6},{5,7},{6,4},{7,5},{8,10},{9,11},{10,... | collective-permute-start | bytes 442376 | tf_op jit(solution)/shard_map/ppermute | solution.py:39
  374.4 17.9 %collective-permute-start.47 = (bf16[384,1152]{1,0:T(8,128)(2,1)}, bf16[384,1152]{1,0:T(8,128)(2,1)}, u32[]{:S(2)}, u32[]{:S(2)}) collective-permute-start(bf16[384,1152]{1,0:T(8,128)(2,1)} %get-tuple-element.333.refs_4_.gq), channel_id=1, source_target_pairs={{0,8},{8,0},{16,24},{24,16},{1,9},{9,1},{17,25},{25,17},{2,10},{10... | collective-permute-start | bytes 2654216 | tf_op jit(solution)/shard_map/ppermute | solution.py:39
  374.4 26.8 %collective-permute-start.46 = (bf16[384,1280]{1,0:T(8,128)(2,1)S(1)}, bf16[384,1280]{1,0:T(8,128)(2,1)S(1)}, u32[]{:S(2)}, u32[]{:S(2)}) collective-permute-start(bf16[384,1280]{1,0:T(8,128)(2,1)S(1)} %collective-permute-done.43.gn), channel_id=1, source_target_pairs={{0,2},{2,4},{4,6},{3,1},{5,3},{7,5},{8,10},{10,12},{12,14},{11,9},... | collective-permute-start | bytes 2949128 | tf_op jit(solution)/shard_map/ppermute | solution.py:1347
  376.8 24.4 %collective-permute-start.48 = (bf16[288,1152]{1,0:T(8,128)(2,1)}, bf16[288,1152]{1,0:T(8,128)(2,1)}, u32[]{:S(2)}, u32[]{:S(2)}) collective-permute-start(bf16[288,1152]{1,0:T(8,128)(2,1)} %get-tuple-element.356), channel_id=1, source_target_pairs={{0,1},{1,0},{2,3},{3,2},{4,5},{5,4},{6,7},{7,6},{8,9},{9,8},{10,11... | collective-permute-start | bytes 1990664 | tf_op jit(solution)/shard_map/ppermute | solution.py:39
  376.9 24.3 %collective-permute-start.49 = (bf16[288,1152]{1,0:T(8,128)(2,1)}, bf16[288,1152]{1,0:T(8,128)(2,1)}, u32[]{:S(2)}, u32[]{:S(2)}) collective-permute-start(bf16[288,1152]{1,0:T(8,128)(2,1)} %get-tuple-element.358), channel_id=1, source_target_pairs={{0,16},{8,24},{16,0},{24,8},{1,17},{9,25},{17,1},{25,9},{2,18},{10... | collective-permute-start | bytes 1990664 | tf_op jit(solution)/shard_map/ppermute | solution.py:39
  402.3 15.5 %collective-permute-start.54 = (bf16[16,4608]{1,0:T(8,128)(2,1)S(1)}, bf16[16,4608]{1,0:T(8,128)(2,1)S(1)}, u32[]{:S(2)}, u32[]{:S(2)}) collective-permute-start(bf16[16,4608]{1,0:T(8,128)(2,1)S(1)} %pad_maximum_fusion.36), channel_id=1, source_target_pairs={{0,4},{1,5},{2,6},{3,7},{4,0},{5,1},{6,2},{7,3},{8,12},{9,13},{10,... | collective-permute-start | bytes 442376 | tf_op jit(solution)/shard_map/ppermute | solution.py:39
  409.2 17.4 %collective-permute-start.53 = (bf16[288,1152]{1,0:T(8,128)(2,1)}, bf16[288,1152]{1,0:T(8,128)(2,1)}, u32[]{:S(2)}, u32[]{:S(2)}) collective-permute-start(bf16[288,1152]{1,0:T(8,128)(2,1)} %get-tuple-element.377), channel_id=1, source_target_pairs={{0,2},{1,3},{2,0},{3,1},{4,6},{5,7},{6,4},{7,5},{8,10},{9,11},{10,... | collective-permute-start | bytes 1990664 | tf_op jit(solution)/shard_map/ppermute | solution.py:39
  410.4 30.2 %collective-permute-start.51 = (bf16[576,1152]{1,0:T(8,128)(2,1)S(1)}, bf16[576,1152]{1,0:T(8,128)(2,1)}, u32[]{:S(2)}, u32[]{:S(2)}) collective-permute-start(bf16[576,1152]{1,0:T(8,128)(2,1)S(1)} %copy-done.42), channel_id=1, source_target_pairs={{0,16},{8,24},{16,0},{24,8},{1,17},{9,25},{17,1},{25,9},{2,18},{10... | collective-permute-start | bytes 3981320 | tf_op jit(solution)/shard_map/ppermute | solution.py:39
  410.6 30.2 %collective-permute-start.52 = (bf16[576,1152]{1,0:T(8,128)(2,1)S(1)}, bf16[576,1152]{1,0:T(8,128)(2,1)}, u32[]{:S(2)}, u32[]{:S(2)}) collective-permute-start(bf16[576,1152]{1,0:T(8,128)(2,1)S(1)} %bitcast.140), channel_id=1, source_target_pairs={{0,1},{1,0},{2,3},{3,2},{4,5},{5,4},{6,7},{7,6},{8,9},{9,8},{10,11... | collective-permute-start | bytes 3981320 | tf_op jit(solution)/shard_map/ppermute | solution.py:39
  445.8 37.1 %collective-permute-start.57 = (bf16[288,1152]{1,0:T(8,128)(2,1)}, bf16[288,1152]{1,0:T(8,128)(2,1)}, u32[]{:S(2)}, u32[]{:S(2)}) collective-permute-start(bf16[288,1152]{1,0:T(8,128)(2,1)} %get-tuple-element.393), channel_id=1, source_target_pairs={{0,1},{1,0},{2,3},{3,2},{4,5},{5,4},{6,7},{7,6},{8,9},{9,8},{10,11... | collective-permute-start | bytes 1990664 | tf_op jit(solution)/shard_map/ppermute | solution.py:39
  446.3 36.6 %collective-permute-start.58 = (bf16[288,1152]{1,0:T(8,128)(2,1)}, bf16[288,1152]{1,0:T(8,128)(2,1)}, u32[]{:S(2)}, u32[]{:S(2)}) collective-permute-start(bf16[288,1152]{1,0:T(8,128)(2,1)} %get-tuple-element.395), channel_id=1, source_target_pairs={{0,16},{8,24},{16,0},{24,8},{1,17},{9,25},{17,1},{25,9},{2,18},{10... | collective-permute-start | bytes 1990664 | tf_op jit(solution)/shard_map/ppermute | solution.py:39
  447.8 35.1 %collective-permute-start.55 = (bf16[288,1152]{1,0:T(8,128)(2,1)}, bf16[288,1152]{1,0:T(8,128)(2,1)}, u32[]{:S(2)}, u32[]{:S(2)}) collective-permute-start(bf16[288,1152]{1,0:T(8,128)(2,1)} %get-tuple-element.385), channel_id=1, source_target_pairs={{0,16},{8,24},{16,0},{24,8},{1,17},{9,25},{17,1},{25,9},{2,18},{10... | collective-permute-start | bytes 1990664 | tf_op jit(solution)/shard_map/ppermute | solution.py:39
  448.4 34.6 %collective-permute-start.56 = (bf16[288,1152]{1,0:T(8,128)(2,1)S(1)}, bf16[288,1152]{1,0:T(8,128)(2,1)}, u32[]{:S(2)}, u32[]{:S(2)}) collective-permute-start(bf16[288,1152]{1,0:T(8,128)(2,1)S(1)} %bitcast.144), channel_id=1, source_target_pairs={{0,1},{1,0},{2,3},{3,2},{4,5},{5,4},{6,7},{7,6},{8,9},{9,8},{10,11... | collective-permute-start | bytes 1990664 | tf_op jit(solution)/shard_map/ppermute | solution.py:39
  467.3 15.7 %collective-permute-start.59 = (bf16[144,1152]{1,0:T(8,128)(2,1)}, bf16[144,1152]{1,0:T(8,128)(2,1)S(1)}, u32[]{:S(2)}, u32[]{:S(2)}) collective-permute-start(bf16[144,1152]{1,0:T(8,128)(2,1)} %get-tuple-element.399), channel_id=1, source_target_pairs={{0,4},{1,5},{2,6},{3,7},{4,0},{5,1},{6,2},{7,3},{8,12},{9,13},{10,... | collective-permute-start | bytes 995336 | tf_op jit(solution)/shard_map/ppermute | solution.py:39
  483.0 11.7 %collective-permute-start.64 = (bf16[14,2304]{1,0:T(8,128)(2,1)S(1)}, bf16[14,2304]{1,0:T(8,128)(2,1)S(1)}, u32[]{:S(2)}, u32[]{:S(2)}) collective-permute-start(bf16[14,2304]{1,0:T(8,128)(2,1)S(1)} %pad_maximum_fusion.46), channel_id=1, source_target_pairs={{0,1},{1,0},{2,3},{3,2},{4,5},{5,4},{6,7},{7,6},{8,9},{9,8},{10,11... | collective-permute-start | bytes 193544 | tf_op jit(solution)/shard_map/ppermute | solution.py:39
  488.6 17.5 %collective-permute-start.63 = (bf16[288,1152]{1,0:T(8,128)(2,1)}, bf16[288,1152]{1,0:T(8,128)(2,1)S(1)}, u32[]{:S(2)}, u32[]{:S(2)}) collective-permute-start(bf16[288,1152]{1,0:T(8,128)(2,1)} %get-tuple-element.420), channel_id=1, source_target_pairs={{0,2},{1,3},{2,0},{3,1},{4,6},{5,7},{6,4},{7,5},{8,10},{9,11},{10,... | collective-permute-start | bytes 1990664 | tf_op jit(solution)/shard_map/ppermute | solution.py:39
  492.2 11.3 %collective-permute-start.61 = (bf16[144,1152]{1,0:T(8,128)(2,1)}, bf16[144,1152]{1,0:T(8,128)(2,1)S(1)}, u32[]{:S(2)}, u32[]{:S(2)}) collective-permute-start(bf16[144,1152]{1,0:T(8,128)(2,1)} %get-tuple-element.412), channel_id=1, source_target_pairs={{0,1},{1,0},{2,3},{3,2},{4,5},{5,4},{6,7},{7,6},{8,9},{9,8},{10,11... | collective-permute-start | bytes 995336 | tf_op jit(solution)/shard_map/ppermute | solution.py:39
  492.5 11.0 %collective-permute-start.62 = (bf16[144,1152]{1,0:T(8,128)(2,1)}, bf16[144,1152]{1,0:T(8,128)(2,1)}, u32[]{:S(2)}, u32[]{:S(2)}) collective-permute-start(bf16[144,1152]{1,0:T(8,128)(2,1)} %get-tuple-element.414), channel_id=1, source_target_pairs={{0,16},{8,24},{16,0},{24,8},{1,17},{9,25},{17,1},{25,9},{2,18},{10... | collective-permute-start | bytes 995336 | tf_op jit(solution)/shard_map/ppermute | solution.py:39
  510.0 17.8 %collective-permute-start.68 = (bf16[144,1152]{1,0:T(8,128)(2,1)}, bf16[144,1152]{1,0:T(8,128)(2,1)S(1)}, u32[]{:S(2)}, u32[]{:S(2)}) collective-permute-start(bf16[144,1152]{1,0:T(8,128)(2,1)} %get-tuple-element.437), channel_id=1, source_target_pairs={{0,4},{1,5},{2,6},{3,7},{4,0},{5,1},{6,2},{7,3},{8,12},{9,13},{10,... | collective-permute-start | bytes 995336 | tf_op jit(solution)/shard_map/ppermute | solution.py:39
  514.2 15.6 %collective-permute-start.67 = (bf16[144,1152]{1,0:T(8,128)(2,1)}, bf16[144,1152]{1,0:T(8,128)(2,1)S(1)}, u32[]{:S(2)}, u32[]{:S(2)}) collective-permute-start(bf16[144,1152]{1,0:T(8,128)(2,1)} %get-tuple-element.433), channel_id=1, source_target_pairs={{0,2},{1,3},{2,0},{3,1},{4,6},{5,7},{6,4},{7,5},{8,10},{9,11},{10,... | collective-permute-start | bytes 995336 | tf_op jit(solution)/shard_map/ppermute | solution.py:39
  514.9 16.0 %collective-permute-start.65 = (bf16[288,1152]{1,0:T(8,128)(2,1)S(1)}, bf16[288,1152]{1,0:T(8,128)(2,1)S(1)}, u32[]{:S(2)}, u32[]{:S(2)}) collective-permute-start(bf16[288,1152]{1,0:T(8,128)(2,1)S(1)} %copy-done.48), channel_id=1, source_target_pairs={{0,16},{8,24},{16,0},{24,8},{1,17},{9,25},{17,1},{25,9},{2,18},{10... | collective-permute-start | bytes 1990664 | tf_op jit(solution)/shard_map/ppermute | solution.py:39
  515.5 15.7 %collective-permute-start.66 = (bf16[288,1152]{1,0:T(8,128)(2,1)S(1)}, bf16[288,1152]{1,0:T(8,128)(2,1)S(1)}, u32[]{:S(2)}, u32[]{:S(2)}) collective-permute-start(bf16[288,1152]{1,0:T(8,128)(2,1)S(1)} %bitcast.145), channel_id=1, source_target_pairs={{0,1},{1,0},{2,3},{3,2},{4,5},{5,4},{6,7},{7,6},{8,9},{9,8},{10,11... | collective-permute-start | bytes 1990664 | tf_op jit(solution)/shard_map/ppermute | solution.py:39
  531.4 13.1 %collective-permute-start.74 = (f32[1,14,4608]{2,1,0:T(8,128)S(1)}, f32[1,14,4608]{2,1,0:T(8,128)S(1)}, u32[]{:S(2)}, u32[]{:S(2)}) collective-permute-start(f32[1,14,4608]{2,1,0:T(8,128)S(1)} %bitcast.122), channel_id=1, source_target_pairs={{0,8},{8,0},{16,24},{24,16},{1,9},{9,1},{17,25},{25,17},{2,10},{10... | collective-permute-start | bytes 774152 | tf_op jit(solution)/shard_map/ppermute | solution.py:39
  532.1 12.2 %collective-permute-start.73 = (bf16[14,2304]{1,0:T(8,128)(2,1)S(1)}, bf16[14,2304]{1,0:T(8,128)(2,1)S(1)}, u32[]{:S(2)}, u32[]{:S(2)}) collective-permute-start(bf16[14,2304]{1,0:T(8,128)(2,1)S(1)} %pad_maximum_fusion.48), channel_id=1, source_target_pairs={{0,4},{1,5},{2,6},{3,7},{4,0},{5,1},{6,2},{7,3},{8,12},{9,13},{10,... | collective-permute-start | bytes 193544 | tf_op jit(solution)/shard_map/ppermute | solution.py:39
  571.0 21.8 %collective-permute-start.82 = (f32[2,14,4608]{2,0,1:T(2,128)S(1)}, f32[2,14,4608]{2,0,1:T(2,128)S(1)}, u32[]{:S(2)}, u32[]{:S(2)}) collective-permute-start(f32[2,14,4608]{2,0,1:T(2,128)S(1)} %copy.57), channel_id=1, source_target_pairs={{0,16},{8,24},{16,0},{24,8},{1,17},{9,25},{17,1},{25,9},{2,18},{10... | collective-permute-start | bytes 1548296 | tf_op jit(solution)/shard_map/ppermute | solution.py:39
  572.2 18.4 %collective-permute-start.81 = (f32[2,13,2304]{2,1,0:T(8,128)S(1)}, f32[2,13,2304]{2,1,0:T(8,128)S(1)}, u32[]{:S(2)}, u32[]{:S(2)}) collective-permute-start(f32[2,13,2304]{2,1,0:T(8,128)S(1)} %pad_maximum_fusion.31), channel_id=1, source_target_pairs={{0,16},{8,24},{16,0},{24,8},{1,17},{9,25},{17,1},{25,9},{2,18},{10... | collective-permute-start | bytes 718856 | tf_op jit(solution)/shard_map/ppermute | solution.py:39
  (86 other events, 742.4 us)

commit v3 on v2

--- a/solution.py
+++ b/solution.py
@@ -124,42 +124,6 @@
             out_specs=[pl.BlockSpec((8 * rows, w), lambda i, c: (i, 0)) for w in widths],
         ),
         out_shape=[jax.ShapeDtypeStruct((32 * rows, w), BF) for w in widths],
-        compiler_params=pltpu.CompilerParams(vmem_limit_bytes=VMEM_LIMIT),
-        cost_estimate=cost(10),
-        name=name,
-    )(core, parts[0], turned[0], parts[2], turned[1])
-
-
-def unpack_rows(core, parts, rows, name):
-    width = parts[0].shape[1]
-    half = rows // 2
-
-    def body(core_ref, a_own, b_own, a_oth, b_oth, out):
-        dp = pl.program_id(0)
-        for a_ref, b_ref, own in ((a_own, b_own, True), (a_oth, b_oth, False)):
-
-            @pl.when((dp % 2 == core_ref[0]) == own)
-            def _(a_ref=a_ref, b_ref=b_ref):
-                for z in range(4):
-                    for x in range(2):
-                        at = (z * 2 + x) * rows
-                        start = (x * 4 + z_place(z)) * half
-                        out[at : at + half, :] = a_ref[start : start + half, :]
-                        start = z_place(z) * half
-                        out[at + half : at + rows, :] = b_ref[x, 0][start : start + half, :]
-
-    by_y = pl.BlockSpec((8 * half, width), lambda i, c: (i // 2, 0))
-    by_x = pl.BlockSpec((2, 1, 4 * half, width), lambda i, c: (0, i // 2, 0, 0))
-    turned = [p.reshape(2, 2, 4 * half, width) for p in (parts[1], parts[3])]
-    return pl.pallas_call(
-        body,
-        grid_spec=pltpu.PrefetchScalarGridSpec(
-            num_scalar_prefetch=1,
-            grid=(4,),
-            in_specs=[by_y, by_x, by_y, by_x],
-            out_specs=pl.BlockSpec((8 * rows, width), lambda i, c: (i, 0)),
-        ),
-        out_shape=jax.ShapeDtypeStruct((32 * rows, width), BF),
         compiler_params=pltpu.CompilerParams(vmem_limit_bytes=VMEM_LIMIT),
         cost_estimate=cost(10),
         name=name,
@@ -268,27 +232,39 @@
     return kept, swap(sent, axis, bit)
 
 
-COLUMNS = 1152
-
-
-def stage_call(body, bits, operands, rows_out, name):
-    width = operands[0].shape[1]
-    return pl.pallas_call(
+def run_together(bits, *tasks):
+    width = tasks[0][1][0].shape[1]
+    operands = [v for task in tasks for v in task[1]]
+    rows_out = [n for task in tasks for n in task[2]]
+
+    def body(bits_ref, *refs):
+        ins, outs = refs[: len(operands)], refs[len(operands) :]
+        for task in tasks:
+            n_in, n_out = len(task[1]), len(task[2])
+            task[0](bits_ref, *ins[:n_in], *outs[:n_out])
+            ins, outs = ins[n_in:], outs[n_out:]
+
+    results = pl.pallas_call(
         body,
         grid_spec=pltpu.PrefetchScalarGridSpec(
             num_scalar_prefetch=1,
-            grid=(width // COLUMNS,),
-            in_specs=[pl.BlockSpec((v.shape[0], COLUMNS), lambda i, b: (0, i)) for v in operands],
-            out_specs=[pl.BlockSpec((n, COLUMNS), lambda i, b: (0, i)) for n in rows_out],
+            grid=(1,),
+            in_specs=[whole(v.shape) for v in operands],
+            out_specs=[whole((n, width)) for n in rows_out],
         ),
         out_shape=[jax.ShapeDtypeStruct((n, width), BF) for n in rows_out],
         compiler_params=pltpu.CompilerParams(vmem_limit_bytes=VMEM_LIMIT),
         cost_estimate=cost(2),
-        name=name,
+        name="add_and_cut",
     )(bits, *operands)
-
-
-def add_and_cut(bits, a, b):
+    found = []
+    for task in tasks:
+        found.append(task[3](results[: len(task[2])]))
+        results = results[len(task[2]) :]
+    return found
+
+
+def add_and_cut(a, b):
     n = a[0].shape[0] // 2
 
     def body(bits_ref, a_own, a_got, b_own, b_got, a_sent, a_kept, b_sent, b_kept):
@@ -301,11 +277,10 @@
             sent[...] = add(own[there, :], got[there, :]).astype(BF)
             kept[...] = add(own[here, :], got[here, :]).astype(BF)
 
-    a_sent, a_kept, b_sent, b_kept = stage_call(body, bits, [*a, *b], [n] * 4, "add_and_cut")
-    return (a_sent, a_kept), (b_sent, b_kept)
-
-
-def add_and_cut_z(bits, a, b):
+    return body, [*a, *b], [n] * 4, lambda r: ((r[0], r[1]), (r[2], r[3]))
+
+
+def add_and_cut_z(a, b):
     h = a[0].shape[0] // 4
 
     def body(bits_ref, a_own, a_got, b_own, b_got, sent, kept):
@@ -323,10 +298,10 @@
                             b_own[rows, :], b_got[rows, :]
                         ).astype(BF)
 
-    return tuple(stage_call(body, bits, [*a, *b], [4 * h] * 2, "add_and_cut_z"))
-
-
-def add_and_cut_last(bits, got):
+    return body, [*a, *b], [4 * h] * 2, tuple
+
+
+def add_and_cut_last(got):
     n = got[0].shape[0] // 2
 
     def body(bits_ref, own, other, sent, kept):
@@ -338,7 +313,7 @@
                 sent[...] = add(own[there, :], other[there, :]).astype(BF)
                 kept[...] = add(own[here, :], other[here, :]).astype(BF)
 
-    return tuple(stage_call(body, bits, [*got], [n] * 2, "add_and_cut_last"))
+    return body, [*got], [n] * 2, tuple
 
 
 def head_window(h, size):
@@ -432,11 +407,9 @@
     scale = size**-0.5
     width = heads * size
 
-    def term(row, lane):
-        at = [width + lane + 2 * heads * k for k in range(3)]
-        return sum(g_ref[pl.ds(row, BLOCK), i : i + 1].astype(F32) for i in at)
-
     def pairs(row, start, length, at, dq, dq_at):
+        terms = g_ref[pl.ds(row, BLOCK), width : width + 128].astype(F32).T
+        stats = terms[: 2 * heads] + terms[2 * heads : 4 * heads] + terms[4 * heads : 6 * heads]
         for h in range(heads):
             lo, hi, off = head_window(h, size)
             q = q_ref[pl.ds(row, BLOCK), lo:hi]
@@ -446,13 +419,12 @@
             g = jnp.where(mask, g, jnp.zeros_like(g))
             k = k_ref[pl.ds(start, length), lo:hi]
             v = v_ref[pl.ds(start, length), lo:hi]
-            lse, delta = term(row, h), term(row, heads + h)
-            p = jnp.exp(dot_nt(q, k) * scale - lse)
-            ds = (p * (dot_nt(g, v) - delta)).astype(BF)
-            dv[pl.ds(at, length), lo:hi] += dot_tn(p.astype(BF), g)
-            dk[pl.ds(at, length), lo:hi] += dot_tn(ds, q)
+            p = jnp.exp(dot_nt(k, q) * scale - stats[h : h + 1, :])
+            ds = (p * (dot_nt(v, g) - stats[heads + h : heads + h + 1, :])).astype(BF)
+            dv[pl.ds(at, length), lo:hi] += dot_nn(p.astype(BF), g)
+            dk[pl.ds(at, length), lo:hi] += dot_nn(ds, q)
             if dq is not None:
-                part = dot_nn(ds, k)
+                part = dot_tn(ds, k)
                 dq[pl.ds(dq_at, BLOCK), lo:hi] += jnp.where(mask, part, jnp.zeros_like(part))
 
     return pairs
@@ -758,12 +730,30 @@
     )(order, mlp_in, hidden_w, hidden_b)
 
 
-def feed_forward_down(order, keep, send, output_w, output_b, after, cotangent, mods):
+def feed_forward_down(order, keep, send, output_w, output_b, after, cotangent, mods, core=None):
     tokens, width = after.shape
     blocks = tokens // BLOCK
-
-    def body(order_ref, keep_ref, send_ref, wo, bo, after_ref, cot, mod, low, out, sums, acc):
+    parts = core is not None
+
+    def body(order_ref, keep_ref, send_ref, *refs):
         t = pl.program_id(0)
+        if parts:
+            a_own, b_own, a_oth, b_oth, bo, after_ref, cot, mod, low, out, sums, wo, acc = refs
+            half = a_own.shape[0] // 8
+            for a_ref, b_ref, own in ((a_own, b_own, True), (a_oth, b_oth, False)):
+
+                @pl.when((order_ref[t] % 2 == order_ref[4]) == own)
+                def _(a_ref=a_ref, b_ref=b_ref):
+                    for z in range(4):
+                        for x in range(2):
+                            at = (z * 2 + x) * 2 * half
+                            start = (x * 4 + z_place(z)) * half
+                            wo[at : at + half, :] = a_ref[start : start + half, :]
+                            start = z_place(z) * half
+                            wo[at + half : at + 2 * half, :] = b_ref[x, 0][start : start + half, :]
+
+        else:
+            wo, bo, after_ref, cot, mod, low, out, sums, acc = refs
 
         @pl.when(t == 0)
         def _():
@@ -791,6 +781,18 @@
             sums[blocks : blocks + 1, :] = column_sum(low[...])
 
     row = whole((tokens, width))
+    chunk = pl.BlockSpec((width, width), lambda t, o: (o[t], 0))
+    if parts:
+        size = output_w[0].shape[0] // 2
+        by_y = pl.BlockSpec((size, width), lambda t, o: (o[t] // 2, 0))
+        by_x = pl.BlockSpec((2, 1, size // 2, width), lambda t, o: (0, o[t] // 2, 0, 0))
+        weights = [
+            v if k % 2 == 0 else v.reshape(2, 2, size // 2, width) for k, v in enumerate(output_w)
+        ]
+        weight_specs = [by_y, by_x] * 2
+        order = jnp.concatenate([order, core])
+    else:
+        weights, weight_specs = [output_w], [chunk]
     return pl.pallas_call(
         body,
         grid_spec=pltpu.PrefetchScalarGridSpec(
@@ -799,7 +801,7 @@
             in_specs=[
                 pl.BlockSpec((tokens, width), lambda t, o: (jnp.maximum(t - 2, 0), 0)),
                 pl.BlockSpec((tokens, width), lambda t, o: (jnp.minimum(t, 1), 0)),
-                pl.BlockSpec((width, width), lambda t, o: (o[t], 0)),
+                *weight_specs,
                 whole((8, width)),
                 row,
                 row,
@@ -809,18 +811,20 @@
                 row,
                 row,
                 whole((8, width)),
-            ],
+            ]
+            + [chunk] * parts,
             scratch_shapes=[pltpu.VMEM((tokens, width), F32)],
         ),
         out_shape=[
             jax.ShapeDtypeStruct((tokens, width), BF),
             jax.ShapeDtypeStruct((tokens, width), BF),
             jax.ShapeDtypeStruct((8, width), F32),
-        ],
+        ]
+        + [jax.ShapeDtypeStruct((4 * width, width), BF)] * parts,
         compiler_params=pltpu.CompilerParams(vmem_limit_bytes=VMEM_LIMIT),
         cost_estimate=cost(12),
         name="feed_forward_down",
-    )(order, keep, send, output_w, output_b, after, cotangent, mods)
+    )(order, keep, send, *weights, output_b, after, cotangent, mods)
 
 
 def feed_forward_back(
@@ -1236,17 +1240,28 @@
         act_keep, third_halves = barrier((act_keep, third_halves))
         third_parts = both_cores(*third_halves)
         act_oth = swap(act_send, "dp", 1)
-        full_output = unpack_rows(core_only, third_parts, 4 * rows, "unpack_output")
-    grad_lower, block_out, lower_sums = feed_forward_down(
-        order,
-        act_keep,
-        act_send,
-        full_output,
-        eight(full_output_bias),
-        after_attn,
-        cotangent[0],
-        own_mods,
-    )
+        grad_lower, block_out, lower_sums, full_output = feed_forward_down(
+            order,
+            act_keep,
+            act_send,
+            third_parts,
+            eight(full_output_bias),
+            after_attn,
+            cotangent[0],
+            own_mods,
+            core_only,
+        )
+    else:
+        grad_lower, block_out, lower_sums = feed_forward_down(
+            order,
+            act_keep,
+            act_send,
+            full_output,
+            eight(full_output_bias),
+            after_attn,
+            cotangent[0],
+            own_mods,
+        )
 
     shape = (tokens_dev, width)
     orders = ["yxz", "xyz"]
@@ -1266,13 +1281,16 @@
             return send(halves, "blk", 4)
 
         def half_2(got):
-            return add_and_cut(bits, *got)
+            return add_and_cut(*got)
 
         def half_3(got):
-            return add_and_cut_z(bits, *got)
-
-        def half_4(got):
-            return add_and_cut_last(bits, got)
+            return add_and_cut_z(*got)
+
+        half_4 = add_and_cut_last
+
+        def cut(*tasks):
+            found = run_together(bits, *tasks)
+            return found[0] if len(tasks) == 1 else found
 
         act_keep, act_oth, grad_lower_oth = barrier((act_keep, act_oth, swap(grad_lower, "dp", 1)))
         third = chip_grads(
@@ -1336,7 +1354,7 @@
         grad_upper_oth = swap(grad_upper, "dp", 1)
         grad_near = swap(grad_attn, "blk", 1)
         early_got = swap_exact(early, 1, 2)
-        third = half_2(third)
+        third = cut(half_2(third))
     grad_q, grad_k_own, grad_v_own = attend_backward_own(
         forward_info, queries, keys, values, grad_attn, HEADS
     )
@@ -1375,7 +1393,7 @@
             (grad_far, first, second, third, early, early_got)
         )
         second = step_1(second)
-        third = step_3(half_3(third))
+        third = step_3(cut(half_3(third)))
         early = early + early_got
         early_got = swap_exact(early, 4, 2)
     grad_kv = attend_backward_other(
@@ -1393,22 +1411,25 @@
         grad_kv, hidden, first, second, third, early, early_got = barrier(
             (grad_kv, hidden, first, second, third, early, early_got)
         )
+        second, third = cut(half_2(second), half_4(third))
+        hidden, first, second, third = barrier((hidden, first, second, third))
         first = step_1(first)
-        second = step_2(half_2(second))
-        third = step_4(half_4(third))
+        second = step_2(second)
+        third = step_4(third)
         early_row = early + early_got
     grad_tokens, input_sums = input_gradient(
         (grad_q, grad_kv), full_qkv, hidden, grad_after, own_mods
     )
     if fast:
+        attn_in_keep, grad_kv, first, second, third, input_sums, early_row = barrier(
+            (attn_in_keep, grad_kv, first, second, third, input_sums, early_row)
+        )
         late = late_message(input_sums)
-        attn_in_keep, grad_kv, first, second, third, late = barrier(
-            (attn_in_keep, grad_kv, first, second, third, late)
-        )
         grad_kv_oth = swap(grad_kv, "dp", 1)
         late_got = swap_exact(late, 1, 1)
-        second = step_3(half_3(second))
-        first = step_2(half_2(first))
+        second, first = cut(half_3(second), half_2(first))
+        second = step_3(second)
+        first = step_2(first)
         third_sum = add(*third)
         last = chip_grads(
             bits,
@@ -1427,16 +1448,18 @@
         last = step_1(last)
         late = late + late_got
         late_got = swap_exact(late, 2, 1)
-        second = step_4(half_4(second))
-        first = step_3(half_3(first))
+        second, first = cut(half_4(second), half_3(first))
+        second = step_4(second)
+        first = step_3(first)
 
         last, first, second, late, late_got, early_row = barrier(
             (last, first, second, late, late_got, early_row)
         )
         late = late + late_got
         late_got = swap_exact(late, 4, 1)
-        last = step_2(half_2(last))
-        first = step_4(half_4(first))
+        last, first = cut(half_2(last), half_4(first))
+        last = step_2(last)
+        first = step_4(first)
         early_pair = pair_up(early_row[None], "dp", core, 1)
         second_sum = add(*second)
 
@@ -1450,7 +1473,7 @@
         row_rest = (own_row - row_high).astype(BF)
         part = dot_nt(ada_rows, row_high.astype(BF)) + dot_nt(ada_rows, row_rest)
         parts = [part] + [swap(part, "blk", bit) for bit in (2, 4, 6)]
-        last = step_3(half_3(last))
+        last = step_3(cut(half_3(last)))
         late_pair = pair_up(late_row[None], "dp", core, 1)
         first_sum = add(*first)
 
@@ -1466,7 +1489,7 @@
             ]
         )
         part = pair_up(line[None], "blk", x, 1)
-        last = step_4(half_4(last))
+        last = step_4(cut(half_4(last)))
         late_all = pair_up(late_pair, "dp", y, 2)
         early_all = pair_up(early_pair, "dp", y, 2)
         last_sum = add(*last)

time: 608 us -> 595 us (0.979)
  waiting for transfers between devices: 164 us -> 153 us
  starting transfers between devices: 94.1 us -> 87 us
    pallas_call x13 -> x8, Pallas kernels: 51.7 us -> 33.6 us  [run_together(): pl.pallas_call(body, grid_spec=pltpu.PrefetchScalarGridSpec(num_scalar_pr...]
    pallas_call x1, Pallas kernels: 6.64 us -> 18.1 us  [attend_backward_other(): pl.pallas_call(body, grid_spec=pltpu.PrefetchScalarGridSpec(num_scalar_pr...]
    ppermute x81, waiting for transfers between devices: 149 us -> 138 us  [swap(): return lax.ppermute(v, axis, [(i, i ^ bit) for i in range(count)])]
    ppermute x81, starting transfers between devices: 85.8 us -> 77.5 us  [swap(): return lax.ppermute(v, axis, [(i, i ^ bit) for i in range(count)])]
  transfers between devices with their start and end apart: 84 -> 84, of which waited for: 31 -> 26; matrix products, arithmetic and copies ran while one was open for 12% -> 13% of each run, Pallas kernels for 37% -> 38%
where the time goes in v3:
time: 595 us; the launch traced here: 587 us
  Pallas kernels  242 us (41%)
  waiting for transfers between devices  153 us (26%)
  starting transfers between devices  87 us (15%)
  other arithmetic  50.8 us (9%)
  matrix products  27.9 us (5%)
  local copies, waits for them, and re-layouts  23.7 us (4%)
    ppermute x81, waiting for transfers between devices, swap(): return lax.ppermute(v, axis, [(i, i ^ bit) for i in range(count)])  138 us
    ppermute x81, starting transfers between devices, swap(): return lax.ppermute(v, axis, [(i, i ^ bit) for i in range(count)])  77.5 us
    pallas_call x4, Pallas kernels, chip_grads(): pl.pallas_call(body, grid_spec=pltpu.PrefetchScalarGridSpec(num_scalar_pr...  44.9 us
    pallas_call x8, Pallas kernels, run_together(): pl.pallas_call(body, grid_spec=pltpu.PrefetchScalarGridSpec(num_scalar_pr...  33.6 us
    pallas_call x1, Pallas kernels, feed_forward_back(): pl.pallas_call(body, grid=(4,), in_specs=[row, pl.BlockSpec((tokens, widt...  25.3 us
    dot_general x5, matrix products, dot_nn(): lax.dot_general(a, b, (((1,), (0,)), ((), ())), preferred_element_type=F32)  21.8 us
    pallas_call x1, Pallas kernels, attend_backward_own(): pl.pallas_call(body, grid_spec=pltpu.PrefetchScalarGridSpec(num_scalar_pr...  20.7 us
    pallas_call x2, Pallas kernels, unpack_weight(): pl.pallas_call(body, grid_spec=pltpu.PrefetchScalarGridSpec(num_scalar_pr...  20.3 us
  transfers between devices with their start and end apart: 84, of which 26 were waited for; matrix products, arithmetic and copies ran while one was open for 13% of the time, Pallas kernels for 38%

profile of v3, /device:TPU:0, one launch (start us, length us, event | category | flops | bytes accessed | tf_op | source)
XLA Modules:
  0.0 587.3 jit_solution(8110972047467461)
XLA Ops:
  3.6 4.0 collective-permute-start.2
  17.9 3.5 collective-permute-start.8
  25.1 2.1 collective-permute-done.10
  31.1 2.3 collective-permute-start.3
  36.5 12.4 %collective-permute-done.3 = bf16[288,1152]{1,0:T(8,128)(2,1)S(1)} collective-permute-done((bf16[288,1152]{1,0:T(8,128)(2,1)S(1)}, bf16[288,1152]{1,0:T(8,128)(2,1)S(1)}, u32[]{:S(2)}, u32[]{:S(2)}) %collective-permute-start.3) | collective-permute-done | bytes 663584 | tf_op jit(solution)/shard_map/ppermute | solution.py:39
  49.3 2.3 collective-permute-start.6
  53.3 2.1 collective-permute-start.14
  57.1 9.8 %collective-permute-done.6 = bf16[144,1152]{1,0:T(8,128)(2,1)S(1)} collective-permute-done((bf16[144,1152]{1,0:T(8,128)(2,1)S(1)}, bf16[144,1152]{1,0:T(8,128)(2,1)S(1)}, u32[]{:S(2)}, u32[]{:S(2)}) %collective-permute-start.6) | collective-permute-done | bytes 331808 | tf_op jit(solution)/shard_map/ppermute | solution.py:39
  68.5 5.4 collective-permute-done.14
  74.6 5.4 collective-permute-done.15
  85.7 5.0 collective-permute-done.16
  90.7 2.7 collective-permute-start.7
  95.3 6.7 %collective-permute-done.19 = bf16[288,1152]{1,0:T(8,128)(2,1)} collective-permute-done((bf16[288,1152]{1,0:T(8,128)(2,1)S(1)}, bf16[288,1152]{1,0:T(8,128)(2,1)}, u32[]{:S(2)}, u32[]{:S(2)}) %collective-permute-start.19) | collective-permute-done | bytes 663584 | tf_op jit(solution)/shard_map/ppermute | solution.py:39
  103.3 14.3 %collective-permute-done.7.far = bf16[384,1152]{1,0:T(8,128)(2,1)} collective-permute-done((bf16[384,1152]{1,0:T(8,128)(2,1)}, bf16[384,1152]{1,0:T(8,128)(2,1)}, u32[]{:S(2)}, u32[]{:S(2)}) %collective-permute-start.7) | collective-permute-done | bytes 884768 | tf_op jit(solution)/shard_map/ppermute | solution.py:1000
  117.7 10.8 %attention_input.1 = (bf16[1152,1152]{1,0:T(8,128)(2,1)}, f32[384,1152]{1,0:T(8,128)}, bf16[576,384]{1,0:T(8,128)(2,1)}, bf16[576,384]{1,0:T(8,128)(2,1)}) custom-call(s32[2]{0:T(128)} %pad_add_fusion.1.core_ref, bf16[384,1152]{1,0:T(8,128)(2,1)} %collective-permute-done.1.near, bf16[384,1152]{1,0:T(8,128)(2,1)} %bitcast.7.own, ...), custom_call_target="tpu_custom_call" | custom-call | flops 11000000512 | bytes 1024 | tf_op jit(solution)/shard_map/attention_input/pallas_call | solution.py:613
  128.4 2.0 broadcast_select_fusion.5
  130.4 2.0 broadcast_select_fusion.11
  133.8 3.3 collective-permute-start.25
  138.7 12.0 %collective-permute-done.25 = bf16[144,1152]{1,0:T(8,128)(2,1)S(1)} collective-permute-done((bf16[144,1152]{1,0:T(8,128)(2,1)S(1)}, bf16[144,1152]{1,0:T(8,128)(2,1)S(1)}, u32[]{:S(2)}, u32[]{:S(2)}) %collective-permute-start.25) | collective-permute-done | bytes 331808 | tf_op jit(solution)/shard_map/ppermute | solution.py:39
  150.8 3.8 collective-permute-done.24
  156.3 2.5 collective-permute-start.28
  160.6 9.9 %unpack_first.1 = (bf16[1152,3456]{1,0:T(8,128)(2,1)}, bf16[1152,1152]{1,0:T(8,128)(2,1)}) custom-call(s32[1]{0:T(128)} %bitcast.2.core_ref, bf16[1152,1152]{1,0:T(8,128)(2,1)} %copy-done.5, bf16[2,2,288,1152]{3,2,1,0:T(8,128)(2,1)} %bitcast.125, bf16[1152,1152]{1,0:T(8,128)(2,1)} %copy-done.32, bf16[2,2,288,1152]{3,2,1,0:T(8,128)(2,1)} %bitcast.137), custom_call_target="tpu_custom_call" | custom-call | flops 11000000512 | bytes 1024 | tf_op jit(solution)/shard_map/unpack_first/pallas_call | solution.py:118
  170.6 8.2 %fusion.q_ref.q_near.q_far = bf16[1152,1152]{1,0:T(8,128)(2,1)} fusion(bf16[1152,1152]{1,0:T(8,128)(2,1)} %get-tuple-element.271, f32[1152]{0:T(1024)S(1)} %copy-done.28, bf16[1152,3456]{1,0:T(8,128)(2,1)} %get-tuple-element.280.w_ref), kind=kOutput, calls=%fused_computation.4 | convolution fusion | flops 3060301824 | bytes 7967232 | tf_op jit(solution)/shard_map/dot_general | solution.py:26
  178.8 5.2 fusion.1.v_ref
  184.0 5.1 convolution_convert_fusion.k_ref
  192.6 2.0 broadcast_select_fusion.9
  199.4 15.2 %attend_forward.1 = (bf16[384,1152]{1,0:T(8,128)(2,1)}, f32[384,1152]{1,0:T(8,128)}, f32[384,128]{1,0:T(8,128)}) custom-call(s32[6]{0:T(128)} %pad_add_fusion.2.info_ref, bf16[1152,1152]{1,0:T(8,128)(2,1)} %fusion.q_ref.q_near.q_far, bf16[1152,1152]{1,0:T(8,128)(2,1)} %convolution_convert_fusion.k_ref, bf16[1152,1152]{1,0:T(8,128)(2,1)} %fusion.1.v_ref), custom_call_target="tpu_custom_call" | custom-call | flops 16499999744 | bytes 1024 | tf_op jit(solution)/shard_map/attend_forward/pallas_call | solution.py:379
  218.6 8.3 %after_attention.1 = (f32[384,1152]{1,0:T(8,128)}, f32[384,1152]{1,0:T(8,128)}, bf16[384,1152]{1,0:T(8,128)(2,1)}, bf16[576,384]{1,0:T(8,128)(2,1)}, bf16[576,38...) custom-call(s32[2]{0:T(128)} %pad_add_fusion.1.core_ref, bf16[384,1152]{1,0:T(8,128)(2,1)} %get-tuple-element.289.low, ...), custom_call_target="tpu_custom_call" | custom-call | flops 8800000000 | bytes 1024 | tf_op jit(solution)/shard_map/after_attention/pallas_call | solution.py:662
  227.6 10.3 %unpack_hidden.1.wh = bf16[1152,4608]{1,0:T(8,128)(2,1)} custom-call(s32[1]{0:T(128)} %bitcast.2.core_ref, bf16[1152,1152]{1,0:T(8,128)(2,1)} %pad_maximum_fusion.2.a_own, bf16[2,2,288,1152]{3,2,1,0:T(8,128)(2,1)} %bitcast.27.b_own, bf16[1152,1152]{1,0:T(8,128)(2,1)} %collective-permute-done.29.a_oth, bf16[2,2,288,1152]{3,2,1,0:T(8,128)(2,1)} %bitcast.28.b_oth), custom_call_target="tpu_custom_call" | custom-call | flops 11000000512 | bytes 1024 | tf_op jit(solution)/shard_map/unpack_hidden/pallas_call | solution.py:118
  238.6 12.8 %feed_forward_up.1 = (bf16[768,1152]{1,0:T(8,128)(2,1)}, bf16[768,1152]{1,0:T(8,128)(2,1)}, bf16[384,4608]{1,0:T(8,128)(2,1)}) custom-call(s32[4]{0:T(128)} %pad_add_fusion.order_ref, bf16[384,1152]{1,0:T(8,128)(2,1)} %get-tuple-element.297.x, bf16[1152,4608]{1,0:T(8,128)(2,1)} %unpack_hidden.1.wh, f32[8,4608]{1,0:T(8,128)} %broadcast_in_dim.148.bh), custom_call_target="tpu_custom_call" | custom-call | flops 15399999488 | bytes 1024 | tf_op jit(solution)/shard_map/feed_forward_up/pallas_call | solution.py:706
  254.8 2.0 broadcast_select_fusion.7
  260.8 2.8 broadcast_select_fusion.13
  264.1 3.5 collective-permute-done.37.refs_2_
  268.2 17.6 %feed_forward_down.1 = (bf16[384,1152]{1,0:T(8,128)(2,1)}, bf16[384,1152]{1,0:T(8,128)(2,1)}, f32[8,1152]{1,0:T(8,128)}, bf16[4608,1152]{1,0:T(8,128)(2,1)}) custom-call(s32[5]{0:T(128)} %concatenate.226.order_ref, bf16[768,1152]{1,0:T(8,128)(2,1)} %get-tuple-element.313.keep_ref.refs_0_, bf16[768,1152]{1,0:T(8,128)(2,1)} %get-tuple-element.306.send_ref, ...), custom_call_target="tpu_custom_call" | custom-call | flops 13200000000 | bytes 1024 | tf_op jit(solution)/shard_map/feed_forward_down/pallas_call | solution.py:796
  290.2 12.1 %grad_output_weight.1 = (bf16[576,1152]{1,0:T(8,128)(2,1)}, bf16[576,1152]{1,0:T(8,128)(2,1)}, bf16[2,288,1152]{2,1,0:T(8,128)(2,1)}, bf16[2,288,1152]{2,1,0:T(8,128)(2,1)}) custom-call(s32[4]{0:T(128)} %pad_add_fusion.3.bits_ref, bf16[768,1152]{1,0:T(8,128)(2,1)} %get-tuple-element.313.keep_ref.refs_0_, bf16[768,1152]{1,0:T(8,128)(2,1)} %collective-permute-done.39.refs_1_, ...), custom_call_target="tpu_custom_call" | custom-call | flops 11000000512 | bytes 1024 | tf_op jit(solution)/shard_map/grad_output_weight/pallas_call | solution.py:193
  304.6 25.3 %feed_forward_back.1 = (bf16[384,5760]{1,0:T(8,128)(2,1)}, f32[384,1152]{1,0:T(8,128)}, bf16[384,1280]{1,0:T(8,128)(2,1)}, f32[8,4608]{1,0:T(8,128)}, f32[8,3456]{1,0:T(8,128)}) custom-call(bf16[384,1152]{1,0:T(8,128)(2,1)} %get-tuple-element.320.refs_2_.gl, bf16[384,4608]{1,0:T(8,128)(2,1)} %get-tuple-element.321.sl, bf16[1152,4608]{1,0:T(8,128)(2,1)} %unpack_hidden.1.wh, ...), custom_call_target="tpu_custom_call" | custom-call | flops 26400000000 | bytes 1024 | tf_op jit(solution)/shard_map/feed_forward_back/pallas_call | solution.py:906
  337.4 20.7 %attend_backward_own.1 = (bf16[384,1152]{1,0:T(8,128)(2,1)}, f32[384,1152]{1,0:T(8,128)}, f32[384,1152]{1,0:T(8,128)}) custom-call(s32[6]{0:T(128)} %pad_add_fusion.2.info_ref, bf16[1152,1152]{1,0:T(8,128)(2,1)} %fusion.q_ref.q_near.q_far, bf16[1152,1152]{1,0:T(8,128)(2,1)} %convolution_convert_fusion.k_ref, bf16[1152,1152]{1,0:T(8,128)(2,1)} %fusion.1.v_ref, ...), custom_call_target="tpu_custom_call" | custom-call | flops 26400000000 | bytes 1024 | tf_op jit(solution)/shard_map/attend_backward_own/pallas_call | solution.py:466
  358.1 4.8 add_and_cut.8
  365.0 3.3 collective-permute-start.46
  368.4 15.2 %grad_hidden_weight.1 = (bf16[576,1152]{1,0:T(8,128)(2,1)}, bf16[576,1152]{1,0:T(8,128)(2,1)}, bf16[2,288,1152]{2,1,0:T(8,128)(2,1)}, bf16[2,288,1152]{2,1,0:T(8,128)(2,1)}) custom-call(s32[4]{0:T(128)} %pad_add_fusion.3.bits_ref, bf16[576,384]{1,0:T(8,128)(2,1)} %get-tuple-element.350.refs_0_, bf16[1152,384]{1,0:T(8,128)(2,1)} %copy-done.18, ...), custom_call_target="tpu_custom_call" | custom-call | flops 11000000512 | bytes 1024 | tf_op jit(solution)/shard_map/grad_hidden_weight/pallas_call | solution.py:193
  383.8 9.0 %grad_query_weight.1 = (bf16[288,1152]{1,0:T(8,128)(2,1)}, bf16[288,1152]{1,0:T(8,128)(2,1)}, bf16[2,144,1152]{2,1,0:T(8,128)(2,1)}, bf16[2,144,1152]{2,1,0:T(8,128)(2,1)}) custom-call(s32[4]{0:T(128)} %pad_add_fusion.3.bits_ref, bf16[576,384]{1,0:T(8,128)(2,1)} %get-tuple-element.428.refs_0_, bf16[576,384]{1,0:T(8,128)(2,1)} %get-tuple-element.358.refs_1_, ...), custom_call_target="tpu_custom_call" | custom-call | flops 11000000512 | bytes 1024 | tf_op jit(solution)/shard_map/grad_query_weight/pallas_call | solution.py:193
  393.8 2.5 collective-permute-start.54
  396.3 3.8 add_and_cut.9
  400.0 2.1 collective-permute-start.53
  402.5 18.1 %attend_backward_other.1.gkv.refs_2_.refs_3_ = bf16[384,2304]{1,0:T(8,128)(2,1)} custom-call(s32[10]{0:T(128)} %pad_add_fusion.4.info_ref, bf16[1152,1152]{1,0:T(8,128)(2,1)} %fusion.q_ref.q_near.q_far, bf16[1152,1152]{1,0:T(8,128)(2,1)} %fusion.q_ref.q_near.q_far, bf16[1152,1152]{1,0:T(8,128)(2,1)} %convolution_convert_fusion.k_ref, ...), custom_call_target="tpu_custom_call" | custom-call | flops 24199999488 | bytes 1024 | tf_op jit(solution)/shard_map/attend_backward_other/pallas_call | solution.py:523
  420.7 11.6 %collective-permute-done.51.refs_1_ = bf16[576,1152]{1,0:T(8,128)(2,1)} collective-permute-done((bf16[576,1152]{1,0:T(8,128)(2,1)S(1)}, bf16[576,1152]{1,0:T(8,128)(2,1)}, u32[]{:S(2)}, u32[]{:S(2)}) %collective-permute-start.51) | collective-permute-done | bytes 1327136 | tf_op jit(solution)/shard_map/ppermute | solution.py:39
  432.4 6.3 %add_and_cut.10 = (bf16[288,1152]{1,0:T(8,128)(2,1)}, bf16[288,1152]{1,0:T(8,128)(2,1)}, bf16[288,1152]{1,0:T(8,128)(2,1)}, bf16[288,1152]{1,0:T(8,128)(2,1)}, b...) custom-call(s32[4]{0:T(128)} %pad_add_fusion.3.bits_ref, bf16[576,1152]{1,0:T(8,128)(2,1)} %get-tuple-element.400.refs_0_, ...), custom_call_target="tpu_custom_call" | custom-call | flops 2200000000 | bytes 1024 | tf_op jit(solution)/shard_map/add_and_cut/pallas_call | solution.py:247
  444.1 14.0 %input_gradient.1 = (f32[384,1152]{1,0:T(8,128)}, f32[8,2304]{1,0:T(8,128)}) custom-call(bf16[384,1152]{1,0:T(8,128)(2,1)} %get-tuple-element.347.refs_4_.gq, bf16[384,2304]{1,0:T(8,128)(2,1)} %attend_backward_other.1.gkv.refs_2_.refs_3_, bf16[1152,3456]{1,0:T(8,128)(2,1)} %get-tuple-element.280.w_ref, f32[384,1152]{1,0:T(8,128)} %get-tuple-element.412.hid, ...), custom_call_target="tpu_custom_call" | custom-call | flops 15399999488 | bytes 1024 | tf_op jit(solution)/shard_map/input_gradient/pallas_call | solution.py:977
  458.4 10.8 %collective-permute-done.57.refs_1_ = bf16[288,1152]{1,0:T(8,128)(2,1)} collective-permute-done((bf16[288,1152]{1,0:T(8,128)(2,1)}, bf16[288,1152]{1,0:T(8,128)(2,1)}, u32[]{:S(2)}, u32[]{:S(2)}) %collective-permute-start.57) | collective-permute-done | bytes 663584 | tf_op jit(solution)/shard_map/ppermute | solution.py:39
  473.1 5.0 add_and_cut.11
  482.4 8.6 %grad_key_weight.1 = (bf16[288,1152]{1,0:T(8,128)(2,1)}, bf16[288,1152]{1,0:T(8,128)(2,1)}, bf16[2,144,1152]{2,1,0:T(8,128)(2,1)}, bf16[2,144,1152]{2,1,0:T(8,128)(2,1)}) custom-call(s32[4]{0:T(128)} %pad_add_fusion.3.bits_ref, bf16[576,384]{1,0:T(8,128)(2,1)} %get-tuple-element.428.refs_0_, bf16[576,384]{1,0:T(8,128)(2,1)} %copy-done.46, ...), custom_call_target="tpu_custom_call" | custom-call | flops 11000000512 | bytes 1024 | tf_op jit(solution)/shard_map/grad_key_weight/pallas_call | solution.py:193
  491.0 4.3 collective-permute-done.63.refs_1_
  496.2 3.8 add_and_cut.12
  504.3 10.5 %collective-permute-done.67.refs_5_ = bf16[144,1152]{1,0:T(8,128)(2,1)S(1)} collective-permute-done((bf16[144,1152]{1,0:T(8,128)(2,1)}, bf16[144,1152]{1,0:T(8,128)(2,1)S(1)}, u32[]{:S(2)}, u32[]{:S(2)}) %collective-permute-start.67) | collective-permute-done | bytes 331808 | tf_op jit(solution)/shard_map/ppermute | solution.py:39
  514.9 3.2 collective-permute-done.68
  521.6 4.3 add_and_cut.13
  530.7 8.3 %collective-permute-done.72 = bf16[72,1152]{1,0:T(8,128)(2,1)S(1)} collective-permute-done((bf16[72,1152]{1,0:T(8,128)(2,1)}, bf16[72,1152]{1,0:T(8,128)(2,1)S(1)}, u32[]{:S(2)}, u32[]{:S(2)}) %collective-permute-start.72) | collective-permute-done | bytes 165920 | tf_op jit(solution)/shard_map/ppermute | solution.py:39
  542.4 2.5 collective-permute-start.78
  544.9 3.1 add_and_cut.14
  548.9 9.4 %collective-permute-done.75.refs_1_ = bf16[144,1152]{1,0:T(8,128)(2,1)S(1)} collective-permute-done((bf16[144,1152]{1,0:T(8,128)(2,1)}, bf16[144,1152]{1,0:T(8,128)(2,1)S(1)}, u32[]{:S(2)}, u32[]{:S(2)}) %collective-permute-start.75) | collective-permute-done | bytes 331808 | tf_op jit(solution)/shard_map/ppermute | solution.py:39
  561.6 2.5 add_and_cut.15
  566.9 6.7 %collective-permute-done.83 = bf16[72,1152]{1,0:T(8,128)(2,1)S(1)} collective-permute-done((bf16[72,1152]{1,0:T(8,128)(2,1)}, bf16[72,1152]{1,0:T(8,128)(2,1)S(1)}, u32[]{:S(2)}, u32[]{:S(2)}) %collective-permute-start.83) | collective-permute-done | bytes 165920 | tf_op jit(solution)/shard_map/ppermute | solution.py:39
  574.6 3.7 collective-permute-done.81
  584.3 2.1 convolution_add_fusion.2
  (484 shorter events, 128.8 us)
Async XLA Ops:
  3.6 26.2 %collective-permute-start.2 = (bf16[144,1152]{1,0:T(8,128)(2,1)}, bf16[144,1152]{1,0:T(8,128)(2,1)}, u32[]{:S(2)}, u32[]{:S(2)}) collective-permute-start(bf16[144,1152]{1,0:T(8,128)(2,1)} %pad_maximum_fusion.25), channel_id=1, source_target_pairs={{0,4},{1,5},{2,6},{3,7},{4,0},{5,1},{6,2},{7,3},{8,12},{9,13},{10,... | collective-permute-start | bytes 995336 | tf_op jit(solution)/shard_map/ppermute | solution.py:39
  9.1 13.7 %collective-permute-start.9 = (bf16[12,1152]{1,0:T(8,128)(2,1)S(1)}, bf16[12,1152]{1,0:T(8,128)(2,1)S(1)}, u32[]{:S(2)}, u32[]{:S(2)}) collective-permute-start(bf16[12,1152]{1,0:T(8,128)(2,1)S(1)} %get-tuple-element.692), channel_id=1, source_target_pairs={{0,8},{8,0},{16,24},{24,16},{1,9},{9,1},{17,25},{25,17},{2,10},{10... | collective-permute-start | bytes 82952 | tf_op jit(solution)/shard_map/ppermute | solution.py:39
  9.1 24.3 %collective-permute-start.13 = (bf16[1,36,6912]{2,1,0:T(8,128)(2,1)}, bf16[1,36,6912]{2,1,0:T(8,128)(2,1)}, u32[]{:S(2)}, u32[]{:S(2)}) collective-permute-start(bf16[1,36,6912]{2,1,0:T(8,128)(2,1)} %bitcast.135), channel_id=1, source_target_pairs={{0,8},{8,0},{16,24},{24,16},{1,9},{9,1},{17,25},{25,17},{2,10},{10... | collective-permute-start | bytes 1493000 | tf_op jit(solution)/shard_map/ppermute | solution.py:39
  22.2 63.0 %collective-permute-start.1 = (bf16[384,1152]{1,0:T(8,128)(2,1)}, bf16[384,1152]{1,0:T(8,128)(2,1)}, u32[]{:S(2)}, u32[]{:S(2)}) collective-permute-start(bf16[384,1152]{1,0:T(8,128)(2,1)} %bitcast.7.own), channel_id=1, source_target_pairs={{0,1},{1,0},{2,3},{3,2},{4,5},{5,4},{6,7},{7,6},{8,9},{9,8},{10,11... | collective-permute-start | bytes 2654216 | tf_op jit(solution)/shard_map/ppermute | solution.py:39
  31.1 17.9 %collective-permute-start.3 = (bf16[288,1152]{1,0:T(8,128)(2,1)S(1)}, bf16[288,1152]{1,0:T(8,128)(2,1)S(1)}, u32[]{:S(2)}, u32[]{:S(2)}) collective-permute-start(bf16[288,1152]{1,0:T(8,128)(2,1)S(1)} %pad_maximum_fusion.19), channel_id=1, source_target_pairs={{0,2},{1,3},{2,0},{3,1},{4,6},{5,7},{6,4},{7,5},{8,10},{9,11},{10,... | collective-permute-start | bytes 1990664 | tf_op jit(solution)/shard_map/ppermute | solution.py:39
  34.9 18.4 %collective-permute-start.12 = (bf16[16,6912]{1,0:T(8,128)(2,1)S(1)}, bf16[16,6912]{1,0:T(8,128)(2,1)S(1)}, u32[]{:S(2)}, u32[]{:S(2)}) collective-permute-start(bf16[16,6912]{1,0:T(8,128)(2,1)S(1)} %fusion.15), channel_id=1, source_target_pairs={{0,16},{8,24},{16,0},{24,8},{1,17},{9,25},{17,1},{25,9},{2,18},{10... | collective-permute-start | bytes 663560 | tf_op jit(solution)/shard_map/ppermute | solution.py:39
  49.3 17.6 %collective-permute-start.6 = (bf16[144,1152]{1,0:T(8,128)(2,1)S(1)}, bf16[144,1152]{1,0:T(8,128)(2,1)S(1)}, u32[]{:S(2)}, u32[]{:S(2)}) collective-permute-start(bf16[144,1152]{1,0:T(8,128)(2,1)S(1)} %pad_maximum_fusion.26), channel_id=1, source_target_pairs={{0,4},{1,5},{2,6},{3,7},{4,0},{5,1},{6,2},{7,3},{8,12},{9,13},{10,... | collective-permute-start | bytes 995336 | tf_op jit(solution)/shard_map/ppermute | solution.py:39
  51.7 29.3 %collective-permute-start.5 = (bf16[288,1152]{1,0:T(8,128)(2,1)S(1)}, bf16[288,1152]{1,0:T(8,128)(2,1)S(1)}, u32[]{:S(2)}, u32[]{:S(2)}) collective-permute-start(bf16[288,1152]{1,0:T(8,128)(2,1)S(1)} %bitcast.127), channel_id=1, source_target_pairs={{0,16},{8,24},{16,0},{24,8},{1,17},{9,25},{17,1},{25,9},{2,18},{10... | collective-permute-start | bytes 1990664 | tf_op jit(solution)/shard_map/ppermute | solution.py:39
  53.3 27.9 %collective-permute-start.4 = (bf16[288,1152]{1,0:T(8,128)(2,1)S(1)}, bf16[288,1152]{1,0:T(8,128)(2,1)S(1)}, u32[]{:S(2)}, u32[]{:S(2)}) collective-permute-start(bf16[288,1152]{1,0:T(8,128)(2,1)S(1)} %bitcast.126), channel_id=1, source_target_pairs={{0,1},{1,0},{2,3},{3,2},{4,5},{5,4},{6,7},{7,6},{8,9},{9,8},{10,11... | collective-permute-start | bytes 1990664 | tf_op jit(solution)/shard_map/ppermute | solution.py:39
  53.3 20.6 %collective-permute-start.14 = (bf16[16,6912]{1,0:T(8,128)(2,1)S(1)}, bf16[16,6912]{1,0:T(8,128)(2,1)S(1)}, u32[]{:S(2)}, u32[]{:S(2)}) collective-permute-start(bf16[16,6912]{1,0:T(8,128)(2,1)S(1)} %bitcast_add_fusion), channel_id=1, source_target_pairs={{0,1},{1,0},{2,3},{3,2},{4,5},{5,4},{6,7},{7,6},{8,9},{9,8},{10,11... | collective-permute-start | bytes 663560 | tf_op jit(solution)/shard_map/ppermute | solution.py:39
  66.9 65.9 %collective-permute-start.20 = (bf16[2,36,6912]{2,0,1:T(2,128)(2,1)}, bf16[2,36,6912]{2,0,1:T(2,128)(2,1)}, u32[]{:S(2)}, u32[]{:S(2)}) collective-permute-start(bf16[2,36,6912]{2,0,1:T(2,128)(2,1)} %copy.52), channel_id=1, source_target_pairs={{0,16},{8,24},{16,0},{24,8},{1,17},{9,25},{17,1},{25,9},{2,18},{10... | collective-permute-start | bytes 2985992 | tf_op jit(solution)/shard_map/ppermute | solution.py:39
  80.0 10.6 %collective-permute-start.16 = (bf16[16,6912]{1,0:T(8,128)(2,1)S(1)}, bf16[16,6912]{1,0:T(8,128)(2,1)S(1)}, u32[]{:S(2)}, u32[]{:S(2)}) collective-permute-start(bf16[16,6912]{1,0:T(8,128)(2,1)S(1)} %add_convert_fusion), channel_id=1, source_target_pairs={{0,4},{1,5},{2,6},{3,7},{4,0},{5,1},{6,2},{7,3},{8,12},{9,13},{10,... | collective-permute-start | bytes 663560 | tf_op jit(solution)/shard_map/ppermute | solution.py:39
  83.1 18.9 %collective-permute-start.19 = (bf16[288,1152]{1,0:T(8,128)(2,1)S(1)}, bf16[288,1152]{1,0:T(8,128)(2,1)}, u32[]{:S(2)}, u32[]{:S(2)}) collective-permute-start(bf16[288,1152]{1,0:T(8,128)(2,1)S(1)} %pad_maximum_fusion.20), channel_id=1, source_target_pairs={{0,2},{1,3},{2,0},{3,1},{4,6},{5,7},{6,4},{7,5},{8,10},{9,11},{10,... | collective-permute-start | bytes 1990664 | tf_op jit(solution)/shard_map/ppermute | solution.py:39
  84.6 43.8 %collective-permute-start.18 = (bf16[576,1152]{1,0:T(8,128)(2,1)}, bf16[576,1152]{1,0:T(8,128)(2,1)}, u32[]{:S(2)}, u32[]{:S(2)}) collective-permute-start(bf16[576,1152]{1,0:T(8,128)(2,1)} %get-tuple-element.269), channel_id=1, source_target_pairs={{0,1},{1,0},{2,3},{3,2},{4,5},{5,4},{6,7},{7,6},{8,9},{9,8},{10,11... | collective-permute-start | bytes 3981320 | tf_op jit(solution)/shard_map/ppermute | solution.py:39
  85.2 45.2 %collective-permute-start.17 = (bf16[576,1152]{1,0:T(8,128)(2,1)}, bf16[576,1152]{1,0:T(8,128)(2,1)}, u32[]{:S(2)}, u32[]{:S(2)}) collective-permute-start(bf16[576,1152]{1,0:T(8,128)(2,1)} %get-tuple-element.268), channel_id=1, source_target_pairs={{0,16},{8,24},{16,0},{24,8},{1,17},{9,25},{17,1},{25,9},{2,18},{10... | collective-permute-start | bytes 3981320 | tf_op jit(solution)/shard_map/ppermute | solution.py:39
  90.7 27.0 %collective-permute-start.7 = (bf16[384,1152]{1,0:T(8,128)(2,1)}, bf16[384,1152]{1,0:T(8,128)(2,1)}, u32[]{:S(2)}, u32[]{:S(2)}) collective-permute-start(bf16[384,1152]{1,0:T(8,128)(2,1)} %collective-permute-done.1.near), channel_id=1, source_target_pairs={{0,2},{2,4},{4,6},{3,1},{5,3},{7,5},{8,10},{10,12},{12,14},{11,9},... | collective-permute-start | bytes 2654216 | tf_op jit(solution)/shard_map/ppermute | solution.py:1000
  133.8 16.8 %collective-permute-start.25 = (bf16[144,1152]{1,0:T(8,128)(2,1)S(1)}, bf16[144,1152]{1,0:T(8,128)(2,1)S(1)}, u32[]{:S(2)}, u32[]{:S(2)}) collective-permute-start(bf16[144,1152]{1,0:T(8,128)(2,1)S(1)} %copy-done.16), channel_id=1, source_target_pairs={{0,4},{1,5},{2,6},{3,7},{4,0},{5,1},{6,2},{7,3},{8,12},{9,13},{10,... | collective-permute-start | bytes 995336 | tf_op jit(solution)/shard_map/ppermute | solution.py:39
  137.2 19.2 %collective-permute-start.21 = (bf16[1152,1152]{1,0:T(8,128)(2,1)S(1)}, bf16[1152,1152]{1,0:T(8,128)(2,1)S(1)}, u32[]{:S(2)}, u32[]{:S(2)}) collective-permute-start(bf16[1152,1152]{1,0:T(8,128)(2,1)S(1)} %pad_maximum_fusion.a_own), channel_id=1, source_target_pairs={{0,8},{8,0},{16,24},{24,16},{1,9},{9,1},{17,25},{25,17},{2,10},{10... | collective-permute-start | bytes 7962632 | tf_op jit(solution)/shard_map/ppermute | solution.py:39
  137.2 19.2 %collective-permute-start.22 = (bf16[1152,1152]{1,0:T(8,128)(2,1)S(1)}, bf16[1152,1152]{1,0:T(8,128)(2,1)S(1)}, u32[]{:S(2)}, u32[]{:S(2)}) collective-permute-start(bf16[1152,1152]{1,0:T(8,128)(2,1)S(1)} %pad_maximum_fusion.1), channel_id=1, source_target_pairs={{0,8},{8,0},{16,24},{24,16},{1,9},{9,1},{17,25},{25,17},{2,10},{10... | collective-permute-start | bytes 7962632 | tf_op jit(solution)/shard_map/ppermute | solution.py:39
  137.8 16.9 %collective-permute-start.24 = (bf16[288,1152]{1,0:T(8,128)(2,1)S(1)}, bf16[288,1152]{1,0:T(8,128)(2,1)S(1)}, u32[]{:S(2)}, u32[]{:S(2)}) collective-permute-start(bf16[288,1152]{1,0:T(8,128)(2,1)S(1)} %bitcast.131), channel_id=1, source_target_pairs={{0,16},{8,24},{16,0},{24,8},{1,17},{9,25},{17,1},{25,9},{2,18},{10... | collective-permute-start | bytes 1990664 | tf_op jit(solution)/shard_map/ppermute | solution.py:39
  138.4 16.6 %collective-permute-start.23 = (bf16[288,1152]{1,0:T(8,128)(2,1)S(1)}, bf16[288,1152]{1,0:T(8,128)(2,1)S(1)}, u32[]{:S(2)}, u32[]{:S(2)}) collective-permute-start(bf16[288,1152]{1,0:T(8,128)(2,1)S(1)} %bitcast.129), channel_id=1, source_target_pairs={{0,1},{1,0},{2,3},{3,2},{4,5},{5,4},{6,7},{7,6},{8,9},{9,8},{10,11... | collective-permute-start | bytes 1990664 | tf_op jit(solution)/shard_map/ppermute | solution.py:39
  156.3 32.8 %collective-permute-start.28 = (bf16[288,1152]{1,0:T(8,128)(2,1)S(1)}, bf16[288,1152]{1,0:T(8,128)(2,1)S(1)}, u32[]{:S(2)}, u32[]{:S(2)}) collective-permute-start(bf16[288,1152]{1,0:T(8,128)(2,1)S(1)} %pad_maximum_fusion.21), channel_id=1, source_target_pairs={{0,2},{1,3},{2,0},{3,1},{4,6},{5,7},{6,4},{7,5},{8,10},{9,11},{10,... | collective-permute-start | bytes 1990664 | tf_op jit(solution)/shard_map/ppermute | solution.py:39
  158.9 30.5 %collective-permute-start.27 = (bf16[576,1152]{1,0:T(8,128)(2,1)S(1)}, bf16[576,1152]{1,0:T(8,128)(2,1)}, u32[]{:S(2)}, u32[]{:S(2)}) collective-permute-start(bf16[576,1152]{1,0:T(8,128)(2,1)S(1)} %pad_maximum_fusion.13), channel_id=1, source_target_pairs={{0,1},{1,0},{2,3},{3,2},{4,5},{5,4},{6,7},{7,6},{8,9},{9,8},{10,11... | collective-permute-start | bytes 3981320 | tf_op jit(solution)/shard_map/ppermute | solution.py:39
  159.1 33.5 %collective-permute-start.26 = (bf16[576,1152]{1,0:T(8,128)(2,1)}, bf16[576,1152]{1,0:T(8,128)(2,1)}, u32[]{:S(2)}, u32[]{:S(2)}) collective-permute-start(bf16[576,1152]{1,0:T(8,128)(2,1)} %pad_maximum_fusion.12), channel_id=1, source_target_pairs={{0,16},{8,24},{16,0},{24,8},{1,17},{9,25},{17,1},{25,9},{2,18},{10... | collective-permute-start | bytes 3981320 | tf_op jit(solution)/shard_map/ppermute | solution.py:39
  196.5 18.1 %collective-permute-start.32 = (bf16[288,1152]{1,0:T(8,128)(2,1)S(1)}, bf16[288,1152]{1,0:T(8,128)(2,1)S(1)}, u32[]{:S(2)}, u32[]{:S(2)}) collective-permute-start(bf16[288,1152]{1,0:T(8,128)(2,1)S(1)} %bitcast.130), channel_id=1, source_target_pairs={{0,16},{8,24},{16,0},{24,8},{1,17},{9,25},{17,1},{25,9},{2,18},{10... | collective-permute-start | bytes 1990664 | tf_op jit(solution)/shard_map/ppermute | solution.py:39
  197.2 17.7 %collective-permute-start.31 = (bf16[288,1152]{1,0:T(8,128)(2,1)S(1)}, bf16[288,1152]{1,0:T(8,128)(2,1)S(1)}, u32[]{:S(2)}, u32[]{:S(2)}) collective-permute-start(bf16[288,1152]{1,0:T(8,128)(2,1)S(1)} %bitcast.128), channel_id=1, source_target_pairs={{0,1},{1,0},{2,3},{3,2},{4,5},{5,4},{6,7},{7,6},{8,9},{9,8},{10,11... | collective-permute-start | bytes 1990664 | tf_op jit(solution)/shard_map/ppermute | solution.py:39
  198.9 17.4 %collective-permute-start.29 = (bf16[1152,1152]{1,0:T(8,128)(2,1)}, bf16[1152,1152]{1,0:T(8,128)(2,1)}, u32[]{:S(2)}, u32[]{:S(2)}) collective-permute-start(bf16[1152,1152]{1,0:T(8,128)(2,1)} %pad_maximum_fusion.2.a_own), channel_id=1, source_target_pairs={{0,8},{8,0},{16,24},{24,16},{1,9},{9,1},{17,25},{25,17},{2,10},{10... | collective-permute-start | bytes 7962632 | tf_op jit(solution)/shard_map/ppermute | solution.py:39
  198.9 17.4 %collective-permute-start.30 = (bf16[1152,1152]{1,0:T(8,128)(2,1)}, bf16[1152,1152]{1,0:T(8,128)(2,1)}, u32[]{:S(2)}, u32[]{:S(2)}) collective-permute-start(bf16[1152,1152]{1,0:T(8,128)(2,1)} %pad_maximum_fusion.3), channel_id=1, source_target_pairs={{0,8},{8,0},{16,24},{24,16},{1,9},{9,1},{17,25},{25,17},{2,10},{10... | collective-permute-start | bytes 7962632 | tf_op jit(solution)/shard_map/ppermute | solution.py:39
  216.3 35.2 %collective-permute-start.36 = (bf16[576,1152]{1,0:T(8,128)(2,1)S(1)}, bf16[576,1152]{1,0:T(8,128)(2,1)}, u32[]{:S(2)}, u32[]{:S(2)}) collective-permute-start(bf16[576,1152]{1,0:T(8,128)(2,1)S(1)} %pad_maximum_fusion.16), channel_id=1, source_target_pairs={{0,1},{1,0},{2,3},{3,2},{4,5},{5,4},{6,7},{7,6},{8,9},{9,8},{10,11... | collective-permute-start | bytes 3981320 | tf_op jit(solution)/shard_map/ppermute | solution.py:39
  217.8 37.0 %collective-permute-start.35 = (bf16[576,1152]{1,0:T(8,128)(2,1)}, bf16[576,1152]{1,0:T(8,128)(2,1)}, u32[]{:S(2)}, u32[]{:S(2)}) collective-permute-start(bf16[576,1152]{1,0:T(8,128)(2,1)} %pad_maximum_fusion.15), channel_id=1, source_target_pairs={{0,16},{8,24},{16,0},{24,8},{1,17},{9,25},{17,1},{25,9},{2,18},{10... | collective-permute-start | bytes 3981320 | tf_op jit(solution)/shard_map/ppermute | solution.py:39
  226.9 11.0 %collective-permute-start.34 = (bf16[1152,384]{1,0:T(8,128)(2,1)}, bf16[1152,384]{1,0:T(8,128)(2,1)S(1)}, u32[]{:S(2)}, u32[]{:S(2)}) collective-permute-start(bf16[1152,384]{1,0:T(8,128)(2,1)} %get-tuple-element.296), channel_id=1, source_target_pairs={{0,8},{8,0},{16,24},{24,16},{1,9},{9,1},{17,25},{25,17},{2,10},{10... | collective-permute-start | bytes 2654216 | tf_op jit(solution)/shard_map/ppermute | solution.py:39
  263.6 26.5 %collective-permute-start.39 = (bf16[768,1152]{1,0:T(8,128)(2,1)}, bf16[768,1152]{1,0:T(8,128)(2,1)}, u32[]{:S(2)}, u32[]{:S(2)}) collective-permute-start(bf16[768,1152]{1,0:T(8,128)(2,1)} %get-tuple-element.306.send_ref), channel_id=1, source_target_pairs={{0,8},{8,0},{16,24},{24,16},{1,9},{9,1},{17,25},{25,17},{2,10},{10... | collective-permute-start | bytes 5308424 | tf_op jit(solution)/shard_map/ppermute | solution.py:39
  302.3 31.4 %collective-permute-start.41 = (bf16[576,1152]{1,0:T(8,128)(2,1)}, bf16[576,1152]{1,0:T(8,128)(2,1)S(1)}, u32[]{:S(2)}, u32[]{:S(2)}) collective-permute-start(bf16[576,1152]{1,0:T(8,128)(2,1)} %get-tuple-element.329), channel_id=1, source_target_pairs={{0,16},{8,24},{16,0},{24,8},{1,17},{9,25},{17,1},{25,9},{2,18},{10... | collective-permute-start | bytes 3981320 | tf_op jit(solution)/shard_map/ppermute | solution.py:39
  303.7 31.4 %collective-permute-start.42 = (bf16[576,1152]{1,0:T(8,128)(2,1)}, bf16[576,1152]{1,0:T(8,128)(2,1)}, u32[]{:S(2)}, u32[]{:S(2)}) collective-permute-start(bf16[576,1152]{1,0:T(8,128)(2,1)} %bitcast.139), channel_id=1, source_target_pairs={{0,1},{1,0},{2,3},{3,2},{4,5},{5,4},{6,7},{7,6},{8,9},{9,8},{10,11... | collective-permute-start | bytes 3981320 | tf_op jit(solution)/shard_map/ppermute | solution.py:39
  335.2 27.9 %collective-permute-start.44 = (bf16[384,5760]{1,0:T(8,128)(2,1)}, bf16[384,5760]{1,0:T(8,128)(2,1)}, u32[]{:S(2)}, u32[]{:S(2)}) collective-permute-start(bf16[384,5760]{1,0:T(8,128)(2,1)} %get-tuple-element.337.refs_2_.refs_3_.refs_4_.refs_5_), channel_id=1, source_target_pairs={{0,8},{8,0},{16,24},{24,16},{1,9},{9,1},{17,25},{25,17},{2,10},{10... | collective-permute-start | bytes 13271048 | tf_op jit(solution)/shard_map/ppermute | solution.py:39
  335.3 27.6 %collective-permute-start.45 = (bf16[16,4608]{1,0:T(8,128)(2,1)S(1)}, bf16[16,4608]{1,0:T(8,128)(2,1)S(1)}, u32[]{:S(2)}, u32[]{:S(2)}) collective-permute-start(bf16[16,4608]{1,0:T(8,128)(2,1)S(1)} %pad_maximum_fusion.34), channel_id=1, source_target_pairs={{0,1},{1,0},{2,3},{3,2},{4,5},{5,4},{6,7},{7,6},{8,9},{9,8},{10,11... | collective-permute-start | bytes 442376 | tf_op jit(solution)/shard_map/ppermute | solution.py:39
  336.1 27.0 %collective-permute-start.43 = (bf16[384,1280]{1,0:T(8,128)(2,1)}, bf16[384,1280]{1,0:T(8,128)(2,1)S(1)}, u32[]{:S(2)}, u32[]{:S(2)}) collective-permute-start(bf16[384,1280]{1,0:T(8,128)(2,1)} %get-tuple-element.335.g_ref), channel_id=1, source_target_pairs={{0,1},{1,0},{2,3},{3,2},{4,5},{5,4},{6,7},{7,6},{8,9},{9,8},{10,11... | collective-permute-start | bytes 2949128 | tf_op jit(solution)/shard_map/ppermute | solution.py:39
  363.3 20.3 %collective-permute-start.50 = (bf16[16,4608]{1,0:T(8,128)(2,1)S(1)}, bf16[16,4608]{1,0:T(8,128)(2,1)S(1)}, u32[]{:S(2)}, u32[]{:S(2)}) collective-permute-start(bf16[16,4608]{1,0:T(8,128)(2,1)S(1)} %pad_maximum_fusion.35), channel_id=1, source_target_pairs={{0,2},{1,3},{2,0},{3,1},{4,6},{5,7},{6,4},{7,5},{8,10},{9,11},{10,... | collective-permute-start | bytes 442376 | tf_op jit(solution)/shard_map/ppermute | solution.py:39
  365.0 18.8 %collective-permute-start.47 = (bf16[384,1152]{1,0:T(8,128)(2,1)}, bf16[384,1152]{1,0:T(8,128)(2,1)}, u32[]{:S(2)}, u32[]{:S(2)}) collective-permute-start(bf16[384,1152]{1,0:T(8,128)(2,1)} %get-tuple-element.347.refs_4_.gq), channel_id=1, source_target_pairs={{0,8},{8,0},{16,24},{24,16},{1,9},{9,1},{17,25},{25,17},{2,10},{10... | collective-permute-start | bytes 2654216 | tf_op jit(solution)/shard_map/ppermute | solution.py:39
  365.0 27.8 %collective-permute-start.46 = (bf16[384,1280]{1,0:T(8,128)(2,1)S(1)}, bf16[384,1280]{1,0:T(8,128)(2,1)S(1)}, u32[]{:S(2)}, u32[]{:S(2)}) collective-permute-start(bf16[384,1280]{1,0:T(8,128)(2,1)S(1)} %collective-permute-done.43.gn), channel_id=1, source_target_pairs={{0,2},{2,4},{4,6},{3,1},{5,3},{7,5},{8,10},{10,12},{12,14},{11,9},... | collective-permute-start | bytes 2949128 | tf_op jit(solution)/shard_map/ppermute | solution.py:1365
  368.3 24.5 %collective-permute-start.48 = (bf16[288,1152]{1,0:T(8,128)(2,1)}, bf16[288,1152]{1,0:T(8,128)(2,1)}, u32[]{:S(2)}, u32[]{:S(2)}) collective-permute-start(bf16[288,1152]{1,0:T(8,128)(2,1)} %get-tuple-element.370), channel_id=1, source_target_pairs={{0,1},{1,0},{2,3},{3,2},{4,5},{5,4},{6,7},{7,6},{8,9},{9,8},{10,11... | collective-permute-start | bytes 1990664 | tf_op jit(solution)/shard_map/ppermute | solution.py:39
  368.4 24.4 %collective-permute-start.49 = (bf16[288,1152]{1,0:T(8,128)(2,1)}, bf16[288,1152]{1,0:T(8,128)(2,1)}, u32[]{:S(2)}, u32[]{:S(2)}) collective-permute-start(bf16[288,1152]{1,0:T(8,128)(2,1)} %get-tuple-element.372), channel_id=1, source_target_pairs={{0,16},{8,24},{16,0},{24,8},{1,17},{9,25},{17,1},{25,9},{2,18},{10... | collective-permute-start | bytes 1990664 | tf_op jit(solution)/shard_map/ppermute | solution.py:39
  393.8 26.8 %collective-permute-start.54 = (bf16[16,4608]{1,0:T(8,128)(2,1)S(1)}, bf16[16,4608]{1,0:T(8,128)(2,1)S(1)}, u32[]{:S(2)}, u32[]{:S(2)}) collective-permute-start(bf16[16,4608]{1,0:T(8,128)(2,1)S(1)} %pad_maximum_fusion.36), channel_id=1, source_target_pairs={{0,4},{1,5},{2,6},{3,7},{4,0},{5,1},{6,2},{7,3},{8,12},{9,13},{10,... | collective-permute-start | bytes 442376 | tf_op jit(solution)/shard_map/ppermute | solution.py:39
  400.0 20.7 %collective-permute-start.53 = (bf16[288,1152]{1,0:T(8,128)(2,1)}, bf16[288,1152]{1,0:T(8,128)(2,1)}, u32[]{:S(2)}, u32[]{:S(2)}) collective-permute-start(bf16[288,1152]{1,0:T(8,128)(2,1)} %get-tuple-element.391), channel_id=1, source_target_pairs={{0,2},{1,3},{2,0},{3,1},{4,6},{5,7},{6,4},{7,5},{8,10},{9,11},{10,... | collective-permute-start | bytes 1990664 | tf_op jit(solution)/shard_map/ppermute | solution.py:39
  402.1 30.2 %collective-permute-start.51 = (bf16[576,1152]{1,0:T(8,128)(2,1)S(1)}, bf16[576,1152]{1,0:T(8,128)(2,1)}, u32[]{:S(2)}, u32[]{:S(2)}) collective-permute-start(bf16[576,1152]{1,0:T(8,128)(2,1)S(1)} %copy-done.36), channel_id=1, source_target_pairs={{0,16},{8,24},{16,0},{24,8},{1,17},{9,25},{17,1},{25,9},{2,18},{10... | collective-permute-start | bytes 3981320 | tf_op jit(solution)/shard_map/ppermute | solution.py:39
  402.1 30.3 %collective-permute-start.52 = (bf16[576,1152]{1,0:T(8,128)(2,1)S(1)}, bf16[576,1152]{1,0:T(8,128)(2,1)}, u32[]{:S(2)}, u32[]{:S(2)}) collective-permute-start(bf16[576,1152]{1,0:T(8,128)(2,1)S(1)} %bitcast.138), channel_id=1, source_target_pairs={{0,1},{1,0},{2,3},{3,2},{4,5},{5,4},{6,7},{7,6},{8,9},{9,8},{10,11... | collective-permute-start | bytes 3981320 | tf_op jit(solution)/shard_map/ppermute | solution.py:39
  438.8 19.4 %collective-permute-start.55 = (bf16[288,1152]{1,0:T(8,128)(2,1)}, bf16[288,1152]{1,0:T(8,128)(2,1)}, u32[]{:S(2)}, u32[]{:S(2)}) collective-permute-start(bf16[288,1152]{1,0:T(8,128)(2,1)} %get-tuple-element.416), channel_id=1, source_target_pairs={{0,16},{8,24},{16,0},{24,8},{1,17},{9,25},{17,1},{25,9},{2,18},{10... | collective-permute-start | bytes 1990664 | tf_op jit(solution)/shard_map/ppermute | solution.py:39
  440.5 17.9 %collective-permute-start.56 = (bf16[288,1152]{1,0:T(8,128)(2,1)S(1)}, bf16[288,1152]{1,0:T(8,128)(2,1)}, u32[]{:S(2)}, u32[]{:S(2)}) collective-permute-start(bf16[288,1152]{1,0:T(8,128)(2,1)S(1)} %bitcast.142), channel_id=1, source_target_pairs={{0,1},{1,0},{2,3},{3,2},{4,5},{5,4},{6,7},{7,6},{8,9},{9,8},{10,11... | collective-permute-start | bytes 1990664 | tf_op jit(solution)/shard_map/ppermute | solution.py:39
  440.8 28.4 %collective-permute-start.57 = (bf16[288,1152]{1,0:T(8,128)(2,1)}, bf16[288,1152]{1,0:T(8,128)(2,1)}, u32[]{:S(2)}, u32[]{:S(2)}) collective-permute-start(bf16[288,1152]{1,0:T(8,128)(2,1)} %get-tuple-element.420), channel_id=1, source_target_pairs={{0,1},{1,0},{2,3},{3,2},{4,5},{5,4},{6,7},{7,6},{8,9},{9,8},{10,11... | collective-permute-start | bytes 1990664 | tf_op jit(solution)/shard_map/ppermute | solution.py:39
  442.5 26.7 %collective-permute-start.58 = (bf16[288,1152]{1,0:T(8,128)(2,1)}, bf16[288,1152]{1,0:T(8,128)(2,1)}, u32[]{:S(2)}, u32[]{:S(2)}) collective-permute-start(bf16[288,1152]{1,0:T(8,128)(2,1)} %get-tuple-element.422), channel_id=1, source_target_pairs={{0,16},{8,24},{16,0},{24,8},{1,17},{9,25},{17,1},{25,9},{2,18},{10... | collective-permute-start | bytes 1990664 | tf_op jit(solution)/shard_map/ppermute | solution.py:39
  442.8 15.4 %collective-permute-start.59 = (bf16[144,1152]{1,0:T(8,128)(2,1)}, bf16[144,1152]{1,0:T(8,128)(2,1)S(1)}, u32[]{:S(2)}, u32[]{:S(2)}) collective-permute-start(bf16[144,1152]{1,0:T(8,128)(2,1)} %get-tuple-element.424), channel_id=1, source_target_pairs={{0,4},{1,5},{2,6},{3,7},{4,0},{5,1},{6,2},{7,3},{8,12},{9,13},{10,... | collective-permute-start | bytes 995336 | tf_op jit(solution)/shard_map/ppermute | solution.py:39
  478.1 17.2 %collective-permute-start.63 = (bf16[288,1152]{1,0:T(8,128)(2,1)}, bf16[288,1152]{1,0:T(8,128)(2,1)S(1)}, u32[]{:S(2)}, u32[]{:S(2)}) collective-permute-start(bf16[288,1152]{1,0:T(8,128)(2,1)} %get-tuple-element.447), channel_id=1, source_target_pairs={{0,2},{1,3},{2,0},{3,1},{4,6},{5,7},{6,4},{7,5},{8,10},{9,11},{10,... | collective-permute-start | bytes 1990664 | tf_op jit(solution)/shard_map/ppermute | solution.py:39
  478.7 12.3 %collective-permute-start.61 = (bf16[144,1152]{1,0:T(8,128)(2,1)}, bf16[144,1152]{1,0:T(8,128)(2,1)S(1)}, u32[]{:S(2)}, u32[]{:S(2)}) collective-permute-start(bf16[144,1152]{1,0:T(8,128)(2,1)} %get-tuple-element.443), channel_id=1, source_target_pairs={{0,1},{1,0},{2,3},{3,2},{4,5},{5,4},{6,7},{7,6},{8,9},{9,8},{10,11... | collective-permute-start | bytes 995336 | tf_op jit(solution)/shard_map/ppermute | solution.py:39
  480.0 11.0 %collective-permute-start.62 = (bf16[144,1152]{1,0:T(8,128)(2,1)}, bf16[144,1152]{1,0:T(8,128)(2,1)}, u32[]{:S(2)}, u32[]{:S(2)}) collective-permute-start(bf16[144,1152]{1,0:T(8,128)(2,1)} %get-tuple-element.445), channel_id=1, source_target_pairs={{0,16},{8,24},{16,0},{24,8},{1,17},{9,25},{17,1},{25,9},{2,18},{10... | collective-permute-start | bytes 995336 | tf_op jit(solution)/shard_map/ppermute | solution.py:39
  500.0 14.9 %collective-permute-start.67 = (bf16[144,1152]{1,0:T(8,128)(2,1)}, bf16[144,1152]{1,0:T(8,128)(2,1)S(1)}, u32[]{:S(2)}, u32[]{:S(2)}) collective-permute-start(bf16[144,1152]{1,0:T(8,128)(2,1)} %get-tuple-element.461), channel_id=1, source_target_pairs={{0,2},{1,3},{2,0},{3,1},{4,6},{5,7},{6,4},{7,5},{8,10},{9,11},{10,... | collective-permute-start | bytes 995336 | tf_op jit(solution)/shard_map/ppermute | solution.py:39
  501.3 16.8 %collective-permute-start.68 = (bf16[144,1152]{1,0:T(8,128)(2,1)}, bf16[144,1152]{1,0:T(8,128)(2,1)S(1)}, u32[]{:S(2)}, u32[]{:S(2)}) collective-permute-start(bf16[144,1152]{1,0:T(8,128)(2,1)} %get-tuple-element.463), channel_id=1, source_target_pairs={{0,4},{1,5},{2,6},{3,7},{4,0},{5,1},{6,2},{7,3},{8,12},{9,13},{10,... | collective-permute-start | bytes 995336 | tf_op jit(solution)/shard_map/ppermute | solution.py:39
  502.1 16.1 %collective-permute-start.65 = (bf16[288,1152]{1,0:T(8,128)(2,1)S(1)}, bf16[288,1152]{1,0:T(8,128)(2,1)S(1)}, u32[]{:S(2)}, u32[]{:S(2)}) collective-permute-start(bf16[288,1152]{1,0:T(8,128)(2,1)S(1)} %copy-done.42), channel_id=1, source_target_pairs={{0,16},{8,24},{16,0},{24,8},{1,17},{9,25},{17,1},{25,9},{2,18},{10... | collective-permute-start | bytes 1990664 | tf_op jit(solution)/shard_map/ppermute | solution.py:39
  502.8 15.4 %collective-permute-start.66 = (bf16[288,1152]{1,0:T(8,128)(2,1)S(1)}, bf16[288,1152]{1,0:T(8,128)(2,1)S(1)}, u32[]{:S(2)}, u32[]{:S(2)}) collective-permute-start(bf16[288,1152]{1,0:T(8,128)(2,1)S(1)} %bitcast.143), channel_id=1, source_target_pairs={{0,1},{1,0},{2,3},{3,2},{4,5},{5,4},{6,7},{7,6},{8,9},{9,8},{10,11... | collective-permute-start | bytes 1990664 | tf_op jit(solution)/shard_map/ppermute | solution.py:39
  519.5 11.1 %collective-permute-start.74 = (f32[1,14,4608]{2,1,0:T(8,128)S(1)}, f32[1,14,4608]{2,1,0:T(8,128)S(1)}, u32[]{:S(2)}, u32[]{:S(2)}) collective-permute-start(f32[1,14,4608]{2,1,0:T(8,128)S(1)} %bitcast.122), channel_id=1, source_target_pairs={{0,8},{8,0},{16,24},{24,16},{1,9},{9,1},{17,25},{25,17},{2,10},{10... | collective-permute-start | bytes 774152 | tf_op jit(solution)/shard_map/ppermute | solution.py:39
  519.7 10.8 %collective-permute-start.73 = (bf16[14,2304]{1,0:T(8,128)(2,1)S(1)}, bf16[14,2304]{1,0:T(8,128)(2,1)S(1)}, u32[]{:S(2)}, u32[]{:S(2)}) collective-permute-start(bf16[14,2304]{1,0:T(8,128)(2,1)S(1)} %pad_maximum_fusion.48), channel_id=1, source_target_pairs={{0,4},{1,5},{2,6},{3,7},{4,0},{5,1},{6,2},{7,3},{8,12},{9,13},{10,... | collective-permute-start | bytes 193544 | tf_op jit(solution)/shard_map/ppermute | solution.py:39
  525.9 13.2 %collective-permute-start.70 = (bf16[144,1152]{1,0:T(8,128)(2,1)}, bf16[144,1152]{1,0:T(8,128)(2,1)S(1)}, u32[]{:S(2)}, u32[]{:S(2)}) collective-permute-start(bf16[144,1152]{1,0:T(8,128)(2,1)} %get-tuple-element.474), channel_id=1, source_target_pairs={{0,1},{1,0},{2,3},{3,2},{4,5},{5,4},{6,7},{7,6},{8,9},{9,8},{10,11... | collective-permute-start | bytes 995336 | tf_op jit(solution)/shard_map/ppermute | solution.py:39
  527.4 11.7 %collective-permute-start.71 = (bf16[144,1152]{1,0:T(8,128)(2,1)}, bf16[144,1152]{1,0:T(8,128)(2,1)S(1)}, u32[]{:S(2)}, u32[]{:S(2)}) collective-permute-start(bf16[144,1152]{1,0:T(8,128)(2,1)} %get-tuple-element.476), channel_id=1, source_target_pairs={{0,16},{8,24},{16,0},{24,8},{1,17},{9,25},{17,1},{25,9},{2,18},{10... | collective-permute-start | bytes 995336 | tf_op jit(solution)/shard_map/ppermute | solution.py:39
  558.7 21.8 %collective-permute-start.82 = (f32[2,14,4608]{2,0,1:T(2,128)S(1)}, f32[2,14,4608]{2,0,1:T(2,128)S(1)}, u32[]{:S(2)}, u32[]{:S(2)}) collective-permute-start(f32[2,14,4608]{2,0,1:T(2,128)S(1)} %copy.57), channel_id=1, source_target_pairs={{0,16},{8,24},{16,0},{24,8},{1,17},{9,25},{17,1},{25,9},{2,18},{10... | collective-permute-start | bytes 1548296 | tf_op jit(solution)/shard_map/ppermute | solution.py:39
  559.6 18.7 %collective-permute-start.81 = (f32[2,13,2304]{2,1,0:T(8,128)S(1)}, f32[2,13,2304]{2,1,0:T(8,128)S(1)}, u32[]{:S(2)}, u32[]{:S(2)}) collective-permute-start(f32[2,13,2304]{2,1,0:T(8,128)S(1)} %pad_maximum_fusion.31), channel_id=1, source_target_pairs={{0,16},{8,24},{16,0},{24,8},{1,17},{9,25},{17,1},{25,9},{2,18},{10... | collective-permute-start | bytes 718856 | tf_op jit(solution)/shard_map/ppermute | solution.py:39
  (80 other events, 719.4 us)
